TPU v7x, 512 devices: a whole 4x4x16 slice. The times are simulated.
512 devices in a mesh: aux: 128 (over x, z, core), occ: 4 (over y).
Axes of the slice: x: 4, y: 4, z: 16, core: 2. Of those that a mesh axis runs over, the one named last changes fastest.
Arguments:
- half_ints: bfloat16 [8192, 3, 2560], P('aux', None, 'occ'), may hold values from -1.75 to 1.75
- coef_virt: bfloat16 [2048, 2560], P('aux', 'occ'), may hold values from -0.125 to 0.125
- screen: int32 [256, 20], P('aux', 'occ'), may hold values from 0 to 1, as said below
- occ_energy: float32 [512], replicated, may hold values from -2 to -0.3
- virt_energy: float32 [2048], replicated, may hold values from 0.2 to 4
- batch_orbitals: int32 [3], replicated, may hold values from 0 to 511, as said below
Outputs:
- amplitudes: float32 [128, 3, 256, 3, 128], P('aux', None, 'occ')
- gamma: bfloat16 [8192, 3, 2048], P(('aux', 'occ'))
Inputs may be any that keep to these rules, and one draw needn't show every extreme that they name: `screen`: 1 where a block of 32 auxiliary and 128 atomic functions is kept, 0 where it is screened out. `batch_orbitals`: 3 distinct occupied orbitals, among them the first and the last.
All inputs are finite; a program needn't handle non-finite values.
Results may differ from a plain program's by a relative error of at most 0.006.
Values may be sent and summed in bfloat16 or wider, within the bound.
No kernel may reach another device: no remote copies, remote signals or barrier semaphores. Data moves between devices by JAX's collectives and lax.ppermute only.
A program may use at most 64 MiB of HBM per device.

v0:
```python
import jax
import jax.numpy as jnp
from jax import lax
from jax.sharding import PartitionSpec as P

A_BLOCKS = 8


def denominators(slot_energy, row_energy, col_energy):
    return (
        slot_energy[:, None, None, None]
        + slot_energy[None, None, :, None]
        - row_energy[None, :, None, None]
        - col_energy[None, None, None, :]
    )


def local(half_ints, coef_virt, screen, occ_energy, virt_energy, batch_orbitals):
    p_rows, occ_count, ao_part = half_ints.shape
    virt_total = virt_energy.shape[0]
    aux_count = lax.axis_size("aux")
    occ_ways = lax.axis_size("occ")
    row_blocks = A_BLOCKS
    col_blocks = aux_count // row_blocks
    row_width = virt_total // row_blocks
    col_width = virt_total // col_blocks
    row_share = row_width // occ_ways
    slab_rows = p_rows // occ_ways
    tile_index = lax.axis_index("aux")
    quarter = lax.axis_index("occ")
    row_block = tile_index // col_blocks
    col_block = tile_index % col_blocks
    labels = jnp.arange(occ_energy.shape[0], dtype=jnp.int32)
    onehot = (batch_orbitals[:, None] == labels[None, :]).astype(jnp.float32)
    slot_energy = jnp.sum(onehot * occ_energy[None, :], axis=1)
    expanded = jnp.repeat(jnp.repeat(screen, 32, axis=0), 128, axis=1).astype(jnp.bfloat16)
    masked_half = half_ints * expanded[:, None, :]
    transformed = jnp.einsum(
        "pim,am->pia",
        masked_half,
        lax.all_gather(coef_virt, "aux", axis=0, tiled=True),
        preferred_element_type=jnp.float32,
    )
    three_rows = lax.psum_scatter(transformed, "occ", scatter_dimension=0, tiled=True).astype(
        jnp.bfloat16
    )
    row_part = three_rows.reshape(slab_rows, occ_count, row_blocks, row_width).transpose(2, 0, 1, 3)
    col_part = three_rows.reshape(slab_rows, occ_count, col_blocks, col_width).transpose(2, 0, 1, 3)
    row_wide = jnp.broadcast_to(
        row_part[:, None], (row_blocks, col_blocks, slab_rows, occ_count, row_width)
    )
    col_wide = jnp.broadcast_to(
        col_part[None], (row_blocks, col_blocks, slab_rows, occ_count, col_width)
    )
    outgoing = jnp.concatenate([row_wide, col_wide], axis=4)
    outgoing = outgoing.reshape(aux_count, slab_rows, occ_count, row_width + col_width)
    panels = lax.all_to_all(outgoing, "aux", split_axis=0, concat_axis=0, tiled=True)
    row_panel = panels[..., :row_width]
    col_panel = panels[..., row_width:]
    gram_part = jnp.einsum(
        "tria,trjb->iajb", row_panel, col_panel, preferred_element_type=jnp.float32
    )
    col_energy = lax.dynamic_slice_in_dim(virt_energy, col_block * col_width, col_width, 0)
    gram_whole = lax.psum(gram_part, "occ")
    row_energy = lax.dynamic_slice_in_dim(virt_energy, row_block * row_width, row_width, 0)
    amps_tile = gram_whole / denominators(slot_energy, row_energy, col_energy)
    mixed_block = (2.0 * amps_tile - jnp.transpose(amps_tile, (2, 1, 0, 3))).astype(jnp.bfloat16)
    own_amps = lax.dynamic_slice_in_dim(amps_tile, quarter * row_share, row_share, 1)
    partial_value = jnp.einsum(
        "iajb,trjb->tria", mixed_block, col_panel, preferred_element_type=jnp.float32
    )
    partial_value = partial_value.astype(jnp.bfloat16)
    returned = lax.all_to_all(partial_value, "aux", split_axis=0, concat_axis=0, tiled=True)
    summed = returned.astype(jnp.float32).reshape(
        row_blocks, col_blocks, slab_rows, occ_count, row_width
    )
    summed = jnp.sum(summed, axis=1)
    gamma_rows = (
        summed.transpose(1, 2, 0, 3).reshape(slab_rows, occ_count, virt_total).astype(jnp.bfloat16)
    )
    return (own_amps[None], gamma_rows)


def solution(mesh):
    in_specs = (P("aux", None, "occ"), P("aux", "occ"), P("aux", "occ"), P(), P(), P())
    out_specs = (P("aux", None, "occ", None, None), P(("aux", "occ"), None, None))
    return jax.shard_map(local, mesh=mesh, in_specs=in_specs, out_specs=out_specs, check_vma=False)
```

profile of v0, /device:TPU:1, one launch (start us, length us, event | category | flops | bytes accessed | tf_op | source)
XLA Modules:
  0.0 660.7 jit_solution(16249924293573015440)
XLA Ops:
  7.2 0.7 all-gather.2.cloned.1.call-update
  7.9 0.7 convert_element_type.35
  8.6 0.1 broadcast_in_dim.11
  8.8 148.6 %all-gather.2.cloned.1.call-done = bf16[2048,640]{1,0:T(8,128)(2,1)} async-done(((bf16[16,640]{1,0:T(8,128)(2,1)}), bf16[2048,640]{1,0:T(8,128)(2,1)}) %all-gather.2.cloned.1.call-update) | async-done | bytes 2621456 | tf_op jit(solution)/shard_map/all_gather | solution.py:41
  157.4 4.1 fusion.2
  161.5 28.1 %reduce-scatter.2.cloned.1.call-done = f32[16,3,2048]{2,0,1:T(8,128)} async-done(((f32[64,3,2048]{2,0,1:T(8,128)}), f32[16,3,2048]{2,0,1:T(8,128)}) %reduce-scatter.2.cloned.1.call-update) | async-done | bytes 393232 | tf_op jit(solution)/shard_map/reduce_scatter | solution.py:44
  189.6 1.0 convert_element_type.38
  190.8 0.2 broadcast_in_dim.13
  191.0 0.2 broadcast_in_dim.12
  191.2 0.5 pad_maximum_fusion
  191.7 230.6 %all_to_all.10 = bf16[128,16,3,384]{3,1,2,0:T(8,128)(2,1)S(1)} all-to-all(bf16[128,16,3,384]{3,1,2,0:T(8,128)(2,1)S(1)} %bitcast.61), channel_id=1, replica_groups=mesh['aux'=128,'occ'=4] {'aux'}, dimensions={0} | all-to-all | bytes 9437184 | tf_op jit(solution)/shard_map/all_to_all | solution.py:57
  422.3 2.1 copy-done
  424.4 0.2 slice.8
  424.7 3.5 copy.63
  428.2 1.8 slice.9
  430.0 0.5 copy-done.1
  430.5 2.9 fusion.5
  433.5 0.8 dynamic_slice.10
  434.2 0.8 dynamic_slice.9
  435.0 0.2 select_reduce_fusion
  435.2 0.1 broadcast_add_fusion
  435.2 0.1 broadcast_subtract_fusion
  435.3 49.3 %all-reduce.2.cloned.1.call-done = f32[3,256,3,128]{3,1,2,0:T(8,128)} async-done(((f32[3,256,3,128]{3,1,2,0:T(8,128)}), f32[3,256,3,128]{3,1,2,0:T(8,128)}) %all-reduce.2.cloned.1.call-update) | async-done | bytes 1179664 | tf_op jit(solution)/shard_map/psum | solution.py:64
  484.6 1.6 subtract_divide_fusion
  486.3 1.0 copy-done.2
  487.3 1.9 bitcast_convert_fusion
  489.2 3.4 copy.53
  492.6 17.7 %all-to-all-start.1 = ((bf16[128,16,3,256]{3,1,2,0:T(8,128)(2,1)}), bf16[128,16,3,256]{3,1,2,0:T(8,128)(2,1)S(1)}, u32[]{:S(2)}, u32[]{:S(2)}) async-start(bf16[128,16,3,256]{3,1,2,0:T(8,128)(2,1)} %copy.53), calls=%async_computation.2 | async-start | bytes 6291456 | tf_op jit(solution)/shard_map/all_to_all | solution.py:73
  510.3 1.7 dynamic-slice_bitcast_fusion
  512.0 141.1 %all-to-all-done.1 = bf16[128,16,3,256]{3,1,2,0:T(8,128)(2,1)S(1)} async-done(((bf16[128,16,3,256]{3,1,2,0:T(8,128)(2,1)}), bf16[128,16,3,256]{3,1,2,0:T(8,128)(2,1)S(1)}, u32[]{:S(2)}, u32[]{:S(2)}) %all-to-all-start.1) | async-done | bytes 3145760 | tf_op jit(solution)/shard_map/all_to_all | solution.py:73
  653.1 0.4 bitcast_reduce_fusion
  653.5 0.7 copy.66
  (18 shorter events, 0.3 us)
Async XLA Ops:
  7.2 150.2 %all-gather.2.cloned.1.call-start = ((), (), s32[]{:S(2)}) async-start(), calls=%async_computation.3 | async-start | bytes 2641920 | tf_op jit(solution)/shard_map/all_gather | solution.py:41
  7.9 181.7 %reduce-scatter.2.cloned.1.call-start = ((), (), s32[]{:S(2)}) async-start(), calls=%async_computation.4 | async-start | bytes 1966080 | tf_op jit(solution)/shard_map/reduce_scatter | solution.py:44
  161.5 323.2 %all-reduce.2.cloned.1.call-start = ((), (), s32[]{:S(2)}) async-start(), calls=%async_computation.5 | async-start | bytes 2359296 | tf_op jit(solution)/shard_map/psum | solution.py:64
  422.3 2.1 copy-start
  428.2 2.4 copy-start.1
  430.5 4.4 copy-start.3
  430.5 4.4 copy-start.4
  486.3 1.0 copy-start.2
  492.6 160.5 %all-to-all-start.1 = ((bf16[128,16,3,256]{3,1,2,0:T(8,128)(2,1)}), bf16[128,16,3,256]{3,1,2,0:T(8,128)(2,1)S(1)}, u32[]{:S(2)}, u32[]{:S(2)}) async-start(bf16[128,16,3,256]{3,1,2,0:T(8,128)(2,1)} %copy.53), calls=%async_computation.2 | async-start | bytes 6291456 | tf_op jit(solution)/shard_map/all_to_all | solution.py:73
Sparse Core Ops, SparseCore 0:
  11.0 146.2 all-gather.1
  161.6 27.9 reduce-scatter.1
  433.5 51.0 all-reduce.1
where the time goes:
time: 662 us; the launch traced here: 661 us
  waiting for transfers between devices  368 us (56%)
  blocking collectives  231 us (35%)
  starting transfers between devices  17.8 us (3%)
  local copies, waits for them, and re-layouts  17.3 us (3%)
  between operations  13.9 us (2%)
  matrix products  8.8 us (1%)
    all_to_all x1, blocking collectives, local(): lax.all_to_all(outgoing, 'aux', split_axis=0, concat_axis=0, tiled=True)  231 us
    all_gather x1, waiting for transfers between devices, local(): lax.all_gather(coef_virt, 'aux', axis=0, tiled=True)  149 us
    all_to_all x1, waiting for transfers between devices, local(): lax.all_to_all(partial_value, 'aux', split_axis=0, concat_axis=0, tiled=T...  141 us
    psum x1, waiting for transfers between devices, local(): gram_whole = lax.psum(gram_part, 'occ')  49.3 us
    reduce_scatter x1, waiting for transfers between devices, local(): lax.psum_scatter(transformed, 'occ', scatter_dimension=0, tiled=True)  28.1 us
    all_to_all x1, starting transfers between devices, local(): lax.all_to_all(partial_value, 'aux', split_axis=0, concat_axis=0, tiled=T...  17.7 us
  transfers between devices with their start and end apart: 4, of which 4 were waited for; matrix products, arithmetic and copies ran while one was open for 1% of the time, Pallas kernels for 0%

commit v1 on v0

v1 whole, which is shorter than its diff:
```python
import jax
import jax.numpy as jnp
from jax import lax
from jax.sharding import Mesh
from jax.sharding import PartitionSpec as P

BF = jnp.bfloat16
F32 = jnp.float32


def swap_cores(value):
    return lax.ppermute(value, "c", [(0, 1), (1, 0)])


def local(half_ints, coef_virt, screen, occ_energy, virt_energy, batch_orbitals):
    p_rows, nocc, ao_part = half_ints.shape
    nv = virt_energy.shape[0]
    nx, nz, ny = lax.axis_size("x"), lax.axis_size("z"), lax.axis_size("y")
    nl = nz // 2
    x, z, c, y = (lax.axis_index(name) for name in ("x", "z", "c", "y"))
    zh, zl = z // nl, z % nl
    r = p_rows // ny
    wide = nv // nx
    narrow = nv // nz
    half = wide // 2
    share = half // ny

    labels = jnp.arange(occ_energy.shape[0], dtype=jnp.int32)
    onehot = (batch_orbitals[:, None] == labels[None, :]).astype(F32)
    slot_energy = jnp.sum(onehot * occ_energy[None, :], axis=1)

    with jax.named_scope("transform"):
        expanded = jnp.repeat(jnp.repeat(screen, 32, axis=0), 128, axis=1).astype(BF)
        masked = half_ints * expanded[:, None, :]
        masked = masked.reshape(ny, r, nocc, ao_part).transpose(0, 2, 1, 3)
        masked = lax.all_gather(masked, "x", axis=0)
        coef = lax.all_gather(coef_virt, ("z", "c"), axis=0, tiled=True)
        part = jnp.einsum("xyirm,am->yxira", masked, coef, preferred_element_type=F32)
        part = lax.all_to_all(part.astype(BF), "y", split_axis=0, concat_axis=0, tiled=True)
        three = jnp.sum(part.astype(F32), axis=0).astype(BF)
        three = three.transpose(0, 2, 1, 3)

    with jax.named_scope("panels"):
        row = lax.all_gather(three.reshape(nx, r, nocc * wide), "z", axis=0)
        row = row.reshape(nz * nx * r, nocc * wide)
        col = lax.all_to_all(three, "x", split_axis=0, concat_axis=0, tiled=True)
        col = col.reshape(nx, r, nocc, wide // narrow, narrow).transpose(0, 3, 1, 2, 4)
        col = col.reshape(nl, 2, r, nocc * narrow).transpose(1, 0, 2, 3)
        col = col.reshape(nz, r, nocc * narrow)
        col = lax.all_to_all(col, "z", split_axis=0, concat_axis=0, tiled=True)
        col = lax.all_gather(col, "x", axis=0)
        col = col.transpose(1, 0, 2, 3).reshape(nz * nx * r, nocc * narrow)

    with jax.named_scope("gram"):
        gram = lax.dot_general(
            row, col, (((0,), (0,)), ((), ())), preferred_element_type=F32
        )
        gram = gram.reshape(nocc, 2, half, nocc * narrow)
        mine = lax.dynamic_index_in_dim(gram, c, 1, keepdims=False)
        other = lax.dynamic_index_in_dim(gram, 1 - c, 1, keepdims=False)
        gram = mine + swap_cores(other)
        gram = gram.reshape(nocc, ny, share, nocc * narrow).transpose(1, 0, 2, 3)
        gram = lax.all_to_all(gram.astype(BF), "y", split_axis=0, concat_axis=0, tiled=True)
        gram = jnp.sum(gram.astype(F32), axis=0).reshape(nocc, share, nocc, narrow)

    with jax.named_scope("amplitudes"):
        row_energy = lax.dynamic_slice_in_dim(virt_energy, x * wide + c * half + y * share, share, 0)
        col_energy = lax.dynamic_slice_in_dim(virt_energy, (zl * 2 + zh) * narrow, narrow, 0)
        denominators = (
            slot_energy[:, None, None, None]
            + slot_energy[None, None, :, None]
            - row_energy[None, :, None, None]
            - col_energy[None, None, None, :]
        )
        amps = gram / denominators
        mixed = (2.0 * amps - jnp.transpose(amps, (2, 1, 0, 3))).astype(BF)
        swap = []
        for h in range(2):
            for l in range(nl):
                for k in range(2):
                    swap.append(((h * nl + l) * 2 + k, (k * nl + l) * 2 + h))
        own = lax.ppermute(amps, ("z", "c"), swap)
        mixed = lax.all_gather(mixed.reshape(nocc, share, nocc * narrow), "y", axis=1)
        mixed = mixed.reshape(nocc, half, nocc * narrow)
        theirs = swap_cores(mixed)
        low = jnp.where(c == 0, mixed, theirs)
        high = jnp.where(c == 0, theirs, mixed)
        mixed = jnp.concatenate([low[:, None], high[:, None]], axis=1)
        mixed = mixed.reshape(nocc * wide, nocc * narrow)

    with jax.named_scope("gamma"):
        value = jnp.dot(row, mixed, preferred_element_type=F32).astype(BF)
        value = value.reshape(nz, nx, r, nocc * narrow).transpose(1, 0, 2, 3)
        value = lax.all_to_all(value, "x", split_axis=0, concat_axis=0, tiled=True)
        value = jnp.sum(value.astype(F32), axis=0).astype(BF)
        value = lax.all_to_all(value, "z", split_axis=0, concat_axis=0, tiled=True)
        value = value.reshape(2, nl, r, nocc, narrow).transpose(2, 3, 1, 0, 4)
        gamma = value.reshape(r, nocc, nv)
    return own[None], gamma


def solution(mesh):
    fine = Mesh(mesh.devices.reshape(4, mesh.shape["aux"] // 8, 2, mesh.shape["occ"]), ("x", "z", "c", "y"))
    aux = ("x", "z", "c")
    in_specs = (P(aux, None, "y"), P(aux, "y"), P(aux, "y"), P(), P(), P())
    out_specs = (P(aux, None, "y", None, None), P(aux + ("y",), None, None))
    return jax.shard_map(local, mesh=fine, in_specs=in_specs, out_specs=out_specs, check_vma=False)
```

time: 662 us -> 274 us (0.41)
  waiting for transfers between devices: 368 us -> 69.2 us
  blocking collectives: 231 us -> 117 us
  starting transfers between devices: 17.8 us -> 47.9 us
    all_to_all x1 -> x3, blocking collectives: 231 us -> 40.4 us  [the longest x1 16 us: local(): lax.all_to_all(part.astype(BF), 'y', split_axis=0, concat_axis=0, tiled=T...]
    all_gather x1, waiting for transfers between devices: 149 us -> 26.3 us  [local(): row = lax.all_gather(three.reshape(nx, r, nocc * wide), 'z', axis=0)]
    all_to_all x1 -> x3, waiting for transfers between devices: 141 us -> 23.5 us  [the longest x1 14 us: local(): col = lax.all_to_all(col, 'z', split_axis=0, concat_axis=0, tiled=True)]
    all_gather x0 -> x4, blocking collectives: none -> 76.2 us  [the longest x1 41 us: local(): coef = lax.all_gather(coef_virt, ('z', 'c'), axis=0, tiled=True)]
    psum x1 -> x0, waiting for transfers between devices: 49.3 us -> none  [local(): gram_whole = lax.psum(gram_part, 'occ')]
    ppermute x0 -> x3, starting transfers between devices: none -> 31.4 us  [the longest x2 17.2 us: swap_cores(): return lax.ppermute(value, 'c', [(0, 1), (1, 0)])]
    reduce_scatter x1 -> x0, waiting for transfers between devices: 28.1 us -> none  [local(): lax.psum_scatter(transformed, 'occ', scatter_dimension=0, tiled=True)]
    ppermute x0 -> x3, waiting for transfers between devices: none -> 19.4 us  [the longest x1 17.1 us: local(): own = lax.ppermute(amps, ('z', 'c'), swap)]
  transfers between devices with their start and end apart: 4 -> 7, of which waited for: 4 -> 6; matrix products, arithmetic and copies ran while one was open for 1% -> 2% of each run, Pallas kernels for 0% -> 0%
where the time goes in v1:
time: 274 us; the launch traced here: 273 us
  blocking collectives  117 us (43%)
  waiting for transfers between devices  69.2 us (25%)
  starting transfers between devices  47.9 us (17%)
  local copies, waits for them, and re-layouts  14.4 us (5%)
  between operations  14.4 us (5%)
  matrix products  5.51 us (2%)
  other arithmetic  4.9 us (2%)
    all_gather x1, blocking collectives, local(): coef = lax.all_gather(coef_virt, ('z', 'c'), axis=0, tiled=True)  41 us
    all_gather x1, waiting for transfers between devices, local(): row = lax.all_gather(three.reshape(nx, r, nocc * wide), 'z', axis=0)  26.3 us
    ppermute x2, starting transfers between devices, swap_cores(): return lax.ppermute(value, 'c', [(0, 1), (1, 0)])  17.2 us
    ppermute x1, waiting for transfers between devices, local(): own = lax.ppermute(amps, ('z', 'c'), swap)  17.1 us
    all_to_all x1, blocking collectives, local(): lax.all_to_all(part.astype(BF), 'y', split_axis=0, concat_axis=0, tiled=T...  16 us
    all_to_all x1, blocking collectives, local(): value = lax.all_to_all(value, 'x', split_axis=0, concat_axis=0, tiled=True)  15 us
    ppermute x1, starting transfers between devices, local(): own = lax.ppermute(amps, ('z', 'c'), swap)  14.2 us
    all_to_all x1, waiting for transfers between devices, local(): col = lax.all_to_all(col, 'z', split_axis=0, concat_axis=0, tiled=True)  14 us
  transfers between devices with their start and end apart: 7, of which 6 were waited for; matrix products, arithmetic and copies ran while one was open for 2% of the time, Pallas kernels for 0%

profile of v1, /device:TPU:1, one launch (start us, length us, event | category | flops | bytes accessed | tf_op | source)
XLA Modules:
  0.0 272.9 jit_solution(2996840308572664077)
XLA Ops:
  8.1 1.0 broadcast_multiply_fusion
  9.1 12.7 %all-gather = bf16[16,3,16,640]{3,2,1,0:T(8,128)(2,1)S(1)} all-gather(bf16[4,3,16,640]{3,2,1,0:T(8,128)(2,1)S(1)} %copy.73), channel_id=2, replica_groups=mesh['x'=4,'z'=16,'c'=2,'y'=4] {'x'}, dimensions={0}, use_global_device_ids=true | all-gather | bytes 1228800 | tf_op jit(solution)/shard_map/transform/all_gather | solution.py:36
  21.8 41.0 %all_gather.23 = bf16[512,640]{1,0:T(8,128)(2,1)S(1)} all-gather(bf16[16,640]{1,0:T(8,128)(2,1)S(1)} %copy-done.2), channel_id=1, replica_groups=mesh['x'=4,'z'=16,'c'=2,'y'=4] {'z','c'}, dimensions={0}, use_global_device_ids=true | all-gather | bytes 675840 | tf_op jit(solution)/shard_map/transform/all_gather | solution.py:37
  62.7 0.8 fusion
  63.6 16.0 %all_to_all.30 = bf16[4,4,3,16,512]{4,3,2,1,0:T(8,128)(2,1)S(1)} all-to-all(bf16[4,4,3,16,512]{4,3,2,1,0:T(8,128)(2,1)S(1)} %copy.74), channel_id=1, replica_groups=mesh['x'=4,'z'=16,'c'=2,'y'=4] {'y'}, dimensions={0} | all-to-all | bytes 1572864 | tf_op jit(solution)/shard_map/transform/all_to_all | solution.py:39
  79.9 0.9 reshape.101
  80.8 9.5 %all_to_all.31 = bf16[4,16,3,512]{3,1,2,0:T(8,128)(2,1)S(1)} all-to-all(bf16[4,16,3,512]{3,1,2,0:T(8,128)(2,1)S(1)} %bitcast.83), channel_id=1, replica_groups=mesh['x'=4,'z'=16,'c'=2,'y'=4] {'x'}, dimensions={0} | all-to-all | bytes 393216 | tf_op jit(solution)/shard_map/panels/all_to_all | solution.py:46
  91.4 6.5 %all-to-all-start.2 = ((bf16[16,16,384]{2,1,0:T(8,128)(2,1)}), bf16[16,16,384]{2,1,0:T(8,128)(2,1)S(1)}, u32[]{:S(2)}, u32[]{:S(2)}) async-start(bf16[16,16,384]{2,1,0:T(8,128)(2,1)} %bitcast.13), calls=%async_computation.2 | async-start | bytes 393216 | tf_op jit(solution)/shard_map/panels/all_to_all | solution.py:50
  97.9 14.0 %all-to-all-done.2 = bf16[16,16,384]{2,1,0:T(8,128)(2,1)S(1)} async-done(((bf16[16,16,384]{2,1,0:T(8,128)(2,1)}), bf16[16,16,384]{2,1,0:T(8,128)(2,1)S(1)}, u32[]{:S(2)}, u32[]{:S(2)}) %all-to-all-start.2) | async-done | bytes 196640 | tf_op jit(solution)/shard_map/panels/all_to_all | solution.py:50
  111.9 11.6 %all-gather.1 = bf16[64,16,384]{2,1,0:T(8,128)(2,1)S(1)} all-gather(bf16[16,16,384]{2,1,0:T(8,128)(2,1)S(1)} %all-to-all-done.2), channel_id=3, replica_groups=mesh['x'=4,'z'=16,'c'=2,'y'=4] {'x'}, dimensions={0}, use_global_device_ids=true | all-gather | bytes 983040 | tf_op jit(solution)/shard_map/panels/all_gather | solution.py:51
  123.5 1.0 copy.79
  124.5 26.3 %all-gather.4.cloned.1.call-done = bf16[16,4,16,1536]{3,2,1,0:T(8,128)(2,1)} async-done(((bf16[1,4,16,1536]{3,2,1,0:T(8,128)(2,1)}), bf16[16,4,16,1536]{3,2,1,0:T(8,128)(2,1)}) %all-gather.4.cloned.1.call-update) | async-done | bytes 3145744 | tf_op jit(solution)/shard_map/panels/all_gather | solution.py:44
  150.9 3.2 %copy.76 = bf16[1536,1024]{1,0:T(8,128)(2,1)S(1)} copy(bf16[1536,1024]{0,1:T(8,128)(2,1)} %bitcast.75) | data formatting | bytes 6291456 | tf_op jit(solution)/shard_map/gram/dot_general | solution.py:55
  154.1 2.9 %fusion.4 = f32[3,2,256,384]{3,2,1,0:T(8,128)S(1)} fusion(bf16[3,2,256,1024]{3,2,1,0:T(8,128)(2,1)S(1)} %bitcast.77, bf16[1024,384,1,1]{1,0,3,2:T(8,128)(2,1)} %bitcast.90), kind=kOutput, calls=%fused_computation.22 | convolution fusion | flops 1207959552 | bytes 6291456 | tf_op jit(solution)/shard_map/gram/dot_general | solution.py:55
  157.1 1.3 copy-done.1
  158.5 11.0 %collective-permute-start = (f32[3,256,384]{2,1,0:T(8,128)S(1)}, f32[3,256,384]{2,1,0:T(8,128)S(1)}, u32[]{:S(2)}, u32[]{:S(2)}) collective-permute-start(f32[3,256,384]{2,1,0:T(8,128)S(1)} %dynamic-slice_bitcast_fusion), channel_id=1, source_target_pairs={{0,4},{4,0},{1,5},{5,1},{2,6},{6,2},{3,7},{7,3},{8,12},{12,8},{9,1... | collective-permute-start | bytes 3538952 | tf_op jit(solution)/shard_map/gram/ppermute | solution.py:12
  169.5 0.8 dynamic_slice.16
  171.9 1.4 fusion.1
  173.3 0.9 copy.80
  174.2 3.5 %all-to-all-start.3 = ((bf16[4,3,64,384]{3,2,1,0:T(8,128)(2,1)}), bf16[4,3,64,384]{3,2,1,0:T(8,128)(2,1)S(1)}, u32[]{:S(2)}, u32[]{:S(2)}) async-start(bf16[4,3,64,384]{3,2,1,0:T(8,128)(2,1)} %copy.80), calls=%async_computation.3 | async-start | bytes 1179648 | tf_op jit(solution)/shard_map/gram/all_to_all | solution.py:63
  177.8 9.4 %all-to-all-done.3 = bf16[4,3,64,384]{3,2,1,0:T(8,128)(2,1)S(1)} async-done(((bf16[4,3,64,384]{3,2,1,0:T(8,128)(2,1)}), bf16[4,3,64,384]{3,2,1,0:T(8,128)(2,1)S(1)}, u32[]{:S(2)}, u32[]{:S(2)}) %all-to-all-start.3) | async-done | bytes 589856 | tf_op jit(solution)/shard_map/gram/all_to_all | solution.py:63
  187.8 10.9 %all_gather.27 = bf16[3,4,64,384]{3,2,0,1:T(8,128)(2,1)S(1)} all-gather(bf16[3,1,64,384]{3,2,0,1:T(8,128)(2,1)S(1)} %reshape.108), channel_id=1, replica_groups=mesh['x'=4,'z'=16,'c'=2,'y'=4] {'y'}, dimensions={1}, use_global_device_ids=true | all-gather | bytes 737280 | tf_op jit(solution)/shard_map/amplitudes/all_gather | solution.py:83
  198.8 6.1 %collective-permute-start.2 = (bf16[3,256,384]{2,1,0:T(8,128)(2,1)S(1)}, bf16[3,256,384]{2,1,0:T(8,128)(2,1)S(1)}, u32[]{:S(2)}, u32[]{:S(2)}) collective-permute-start(bf16[3,256,384]{2,1,0:T(8,128)(2,1)S(1)} %bitcast.80), channel_id=1, source_target_pairs={{0,4},{4,0},{1,5},{5,1},{2,6},{6,2},{3,7},{7,3},{8,12},{12,8},{9,1... | collective-permute-start | bytes 1769480 | tf_op jit(solution)/shard_map/amplitudes/ppermute | solution.py:12
  205.0 1.6 collective-permute-done.2
  207.1 1.6 copy-done
  208.7 1.8 convolution_convert_fusion
  210.5 15.0 %all_to_all.32 = bf16[4,16,16,384]{3,2,1,0:T(8,128)(2,1)S(1)} all-to-all(bf16[4,16,16,384]{3,2,1,0:T(8,128)(2,1)S(1)} %bitcast.78), channel_id=1, replica_groups=mesh['x'=4,'z'=16,'c'=2,'y'=4] {'x'}, dimensions={0} | all-to-all | bytes 1572864 | tf_op jit(solution)/shard_map/gamma/all_to_all | solution.py:94
  225.5 0.8 reduce_sum.45
  226.3 6.6 %all-to-all-start.5 = ((bf16[16,16,384]{2,1,0:T(8,128)(2,1)}), bf16[16,16,384]{2,1,0:T(8,128)(2,1)S(1)}, u32[]{:S(2)}, u32[]{:S(2)}) async-start(bf16[16,16,384]{2,1,0:T(8,128)(2,1)} %reduce_sum.45), calls=%async_computation.5 | async-start | bytes 393216 | tf_op jit(solution)/shard_map/gamma/all_to_all | solution.py:96
  232.9 14.2 %collective-permute-start.1 = (f32[3,64,3,128]{3,1,0,2:T(8,128)S(1)}, f32[3,64,3,128]{3,1,0,2:T(8,128)S(1)}, u32[]{:S(2)}, u32[]{:S(2)}) collective-permute-start(f32[3,64,3,128]{3,1,0,2:T(8,128)S(1)} %bitcast_divide_fusion), channel_id=1, source_target_pairs={{0,0},{4,64},{8,8},{12,72},{16,16},{20,80},{24,24},{28,88},{32,32}... | collective-permute-start | bytes 884744 | tf_op jit(solution)/shard_map/amplitudes/ppermute | solution.py:82
  247.1 17.1 %collective-permute-done.1 = f32[3,64,3,128]{3,1,0,2:T(8,128)S(1)} collective-permute-done((f32[3,64,3,128]{3,1,0,2:T(8,128)S(1)}, f32[3,64,3,128]{3,1,0,2:T(8,128)S(1)}, u32[]{:S(2)}, u32[]{:S(2)}) %collective-permute-start.1) | collective-permute-done | bytes 294944 | tf_op jit(solution)/shard_map/amplitudes/ppermute | solution.py:82
  265.2 0.8 reshape.113
  (42 shorter events, 6.4 us)
Async XLA Ops:
  7.2 143.7 %all-gather.4.cloned.1.call-start = ((), (), s32[]{:S(2)}) async-start(), calls=%async_computation.6 | async-start | bytes 3342336 | tf_op jit(solution)/shard_map/panels/all_gather | solution.py:44
  8.1 13.7 %copy-start.2 = (bf16[16,640]{1,0:T(8,128)(2,1)S(1)}, bf16[16,640]{1,0:T(8,128)(2,1)}, u32[]{:S(2)}) copy-start(bf16[16,640]{1,0:T(8,128)(2,1)} %param.7) | copy-start | bytes 61444
  91.4 20.5 %all-to-all-start.2 = ((bf16[16,16,384]{2,1,0:T(8,128)(2,1)}), bf16[16,16,384]{2,1,0:T(8,128)(2,1)S(1)}, u32[]{:S(2)}, u32[]{:S(2)}) async-start(bf16[16,16,384]{2,1,0:T(8,128)(2,1)} %bitcast.13), calls=%async_computation.2 | async-start | bytes 393216 | tf_op jit(solution)/shard_map/panels/all_to_all | solution.py:50
  157.0 1.4 copy-start.1
  157.0 14.0 %copy-start.3 = (f32[512]{0:T(512)S(1)}, f32[512]{0:T(512)}, u32[]{:S(2)}) copy-start(f32[512]{0:T(512)} %param.9) | copy-start | bytes 6148
  157.0 14.0 %copy-start.4 = (s32[3]{0:T(128)S(1)}, s32[3]{0:T(128)}, u32[]{:S(2)}) copy-start(s32[3]{0:T(128)} %param.11) | copy-start | bytes 40
  158.5 13.5 %collective-permute-start = (f32[3,256,384]{2,1,0:T(8,128)S(1)}, f32[3,256,384]{2,1,0:T(8,128)S(1)}, u32[]{:S(2)}, u32[]{:S(2)}) collective-permute-start(f32[3,256,384]{2,1,0:T(8,128)S(1)} %dynamic-slice_bitcast_fusion), channel_id=1, source_target_pairs={{0,4},{4,0},{1,5},{5,1},{2,6},{6,2},{3,7},{7,3},{8,12},{12,8},{9,1... | collective-permute-start | bytes 3538952 | tf_op jit(solution)/shard_map/gram/ppermute | solution.py:12
  174.2 13.1 %all-to-all-start.3 = ((bf16[4,3,64,384]{3,2,1,0:T(8,128)(2,1)}), bf16[4,3,64,384]{3,2,1,0:T(8,128)(2,1)S(1)}, u32[]{:S(2)}, u32[]{:S(2)}) async-start(bf16[4,3,64,384]{3,2,1,0:T(8,128)(2,1)} %copy.80), calls=%async_computation.3 | async-start | bytes 1179648 | tf_op jit(solution)/shard_map/gram/all_to_all | solution.py:63
  198.8 7.8 %collective-permute-start.2 = (bf16[3,256,384]{2,1,0:T(8,128)(2,1)S(1)}, bf16[3,256,384]{2,1,0:T(8,128)(2,1)S(1)}, u32[]{:S(2)}, u32[]{:S(2)}) collective-permute-start(bf16[3,256,384]{2,1,0:T(8,128)(2,1)S(1)} %bitcast.80), channel_id=1, source_target_pairs={{0,4},{4,0},{1,5},{5,1},{2,6},{6,2},{3,7},{7,3},{8,12},{12,8},{9,1... | collective-permute-start | bytes 1769480 | tf_op jit(solution)/shard_map/amplitudes/ppermute | solution.py:12
  206.8 1.9 copy-start
  226.3 38.6 %all-to-all-start.5 = ((bf16[16,16,384]{2,1,0:T(8,128)(2,1)}), bf16[16,16,384]{2,1,0:T(8,128)(2,1)S(1)}, u32[]{:S(2)}, u32[]{:S(2)}) async-start(bf16[16,16,384]{2,1,0:T(8,128)(2,1)} %reduce_sum.45), calls=%async_computation.5 | async-start | bytes 393216 | tf_op jit(solution)/shard_map/gamma/all_to_all | solution.py:96
  232.9 31.3 %collective-permute-start.1 = (f32[3,64,3,128]{3,1,0,2:T(8,128)S(1)}, f32[3,64,3,128]{3,1,0,2:T(8,128)S(1)}, u32[]{:S(2)}, u32[]{:S(2)}) collective-permute-start(f32[3,64,3,128]{3,1,0,2:T(8,128)S(1)} %bitcast_divide_fusion), channel_id=1, source_target_pairs={{0,0},{4,64},{8,8},{12,72},{16,16},{20,80},{24,24},{28,88},{32,32}... | collective-permute-start | bytes 884744 | tf_op jit(solution)/shard_map/amplitudes/ppermute | solution.py:82
Sparse Core Ops, SparseCore 0:
  81.0 69.8 all-gather.3

commit v2 on v1

v2 whole, which is shorter than its diff:
```python
import jax
import jax.numpy as jnp
from jax import lax
from jax.sharding import Mesh
from jax.sharding import PartitionSpec as P

BF = jnp.bfloat16
F32 = jnp.float32


def swap_cores(value):
    return lax.ppermute(value, "c", [(0, 1), (1, 0)])


def exchange(value, axis):
    members, rows, lanes = value.shape
    value = value.reshape(members * rows, lanes)
    value = lax.all_to_all(value, axis, split_axis=0, concat_axis=0, tiled=True)
    return value.reshape(members, rows, lanes)


def by_core(mine, theirs, core):
    return jnp.where(core == 0, mine, theirs), jnp.where(core == 0, theirs, mine)


def local(half_ints, coef_virt, screen, occ_energy, virt_energy, batch_orbitals):
    p_rows, nocc, ao_part = half_ints.shape
    nv = virt_energy.shape[0]
    nx, nz, ny = lax.axis_size("x"), lax.axis_size("z"), lax.axis_size("y")
    nl = nz // 2
    x, z, c, y = (lax.axis_index(name) for name in ("x", "z", "c", "y"))
    zh, zl = z // nl, z % nl
    r = p_rows // ny
    wide = nv // nx
    narrow = nv // nz
    half = wide // 2
    share = half // ny
    ways = wide // narrow

    labels = jnp.arange(occ_energy.shape[0], dtype=jnp.int32)
    onehot = (batch_orbitals[:, None] == labels[None, :]).astype(F32)
    slot_energy = jnp.sum(onehot * occ_energy[None, :], axis=1)

    with jax.named_scope("transform"):
        copies = jnp.broadcast_to(coef_virt[None], (nz,) + coef_virt.shape)
        coef = exchange(copies, "z")
        expanded = jnp.repeat(jnp.repeat(screen, 32, axis=0), 128, axis=1).astype(BF)
        masked = half_ints * expanded[:, None, :]
        masked = masked.reshape(ny, r, nocc, ao_part).transpose(0, 2, 1, 3)
        masked = lax.all_gather(masked.reshape(-1, ao_part), "x", axis=0)
        masked = masked.reshape(nx, ny, nocc, r, ao_part)
        masked, coef = lax.optimization_barrier((masked, coef))
        low, high = by_core(coef, swap_cores(coef), c)
        coef = jnp.stack([low, high], axis=1).reshape(wide, ao_part)
        part = jnp.einsum("xyirm,am->yxira", masked, coef, preferred_element_type=F32)
        part = exchange(part.astype(BF).reshape(ny, nx * nocc * r, wide), "y")
        three = jnp.sum(part.astype(F32), axis=0).astype(BF).reshape(nx, nocc, r, wide)

    with jax.named_scope("panels"):
        row = jnp.concatenate([three[:, i] for i in range(nocc)], axis=-1)
        row = lax.all_gather(row.reshape(nx * r, nocc * wide), "z", axis=0, tiled=True)
        col = exchange(three.reshape(nx, nocc * r, wide), "x")
        col = col.reshape(nx, nocc, r, ways // 2, 2, narrow)
        col = jnp.concatenate(
            [col[:, i].transpose(3, 0, 2, 1, 4).reshape(nz, r, narrow) for i in range(nocc)], axis=-1
        )
        col = exchange(col, "z")
        col = lax.all_gather(col.reshape(nz * r, nocc * narrow), "x", axis=0)
        col = col.reshape(nx, nz, r, nocc * narrow)
        col = col.transpose(1, 0, 2, 3).reshape(nz * nx * r, nocc * narrow)

    with jax.named_scope("gram"):
        gram = lax.dot_general(
            row, col, (((0,), (0,)), ((), ())), preferred_element_type=F32
        )
        gram = gram.reshape(nocc, 2, half, nocc * narrow)
        mine = lax.dynamic_index_in_dim(gram, c, 1, keepdims=False)
        other = lax.dynamic_index_in_dim(gram, 1 - c, 1, keepdims=False)
        gram = mine + swap_cores(other)
        gram = gram.reshape(nocc, ny, share, nocc * narrow).transpose(1, 0, 2, 3)
        gram = exchange(gram.astype(BF).reshape(ny, nocc * share, nocc * narrow), "y")
        gram = jnp.sum(gram.astype(F32), axis=0).reshape(nocc, share, nocc, narrow)

    with jax.named_scope("amplitudes"):
        row_energy = lax.dynamic_slice_in_dim(virt_energy, x * wide + c * half + y * share, share, 0)
        col_energy = lax.dynamic_slice_in_dim(virt_energy, (zl * 2 + zh) * narrow, narrow, 0)
        denominators = (
            slot_energy[:, None, None, None]
            + slot_energy[None, None, :, None]
            - row_energy[None, :, None, None]
            - col_energy[None, None, None, :]
        )
        amps = gram / denominators
        mixed = (2.0 * amps - jnp.transpose(amps, (2, 1, 0, 3))).astype(BF)
        swap = []
        for h in range(2):
            for l in range(nl):
                for k in range(2):
                    swap.append(((h * nl + l) * 2 + k, (k * nl + l) * 2 + h))
        own = lax.ppermute(amps, ("z", "c"), swap)
        mixed = jnp.concatenate([mixed[:, :, j] for j in range(nocc)], axis=-1)
        mixed = lax.all_gather(mixed.reshape(nocc * share, nocc * narrow), "y", axis=0)
        mixed = mixed.reshape(ny, nocc, share, nocc * narrow).transpose(1, 0, 2, 3)
        mixed = mixed.reshape(nocc, half, nocc * narrow)
        low, high = by_core(mixed, swap_cores(mixed), c)
        mixed = jnp.stack([low, high], axis=1).reshape(nocc * wide, nocc * narrow)

    with jax.named_scope("gamma"):
        value = jnp.dot(row, mixed, preferred_element_type=F32).astype(BF)
        value = value.reshape(nz, nx, r, nocc * narrow).transpose(1, 0, 2, 3)
        value = exchange(value.reshape(nx, nz * r, nocc * narrow), "x")
        value = jnp.sum(value.astype(F32), axis=0).astype(BF)
        value = exchange(value.reshape(nz, r, nocc * narrow), "z")
        value = value.reshape(2, nl, r, nocc, narrow).transpose(2, 3, 1, 0, 4)
        gamma = value.reshape(r, nocc, nv)
    return own[None], gamma


def solution(mesh):
    fine = Mesh(mesh.devices.reshape(4, mesh.shape["aux"] // 8, 2, mesh.shape["occ"]), ("x", "z", "c", "y"))
    aux = ("x", "z", "c")
    in_specs = (P(aux, None, "y"), P(aux, "y"), P(aux, "y"), P(), P(), P())
    out_specs = (P(aux, None, "y", None, None), P(aux + ("y",), None, None))
    return jax.shard_map(local, mesh=fine, in_specs=in_specs, out_specs=out_specs, check_vma=False)
```

time: 274 us -> 265 us (0.967)
  blocking collectives: 117 us -> 76.8 us
  starting transfers between devices: 47.9 us -> 71.6 us
  waiting for transfers between devices: 69.2 us -> 75.8 us
    all_gather x4 -> x3, blocking collectives: 76.2 us -> 36.1 us  [the longest x1 13.2 us: local(): masked = lax.all_gather(masked.reshape(-1, ao_part), 'x', axis=0)]
    all_to_all x3 -> x4, starting transfers between devices: 16.5 us -> 32.4 us  [exchange(): value = lax.all_to_all(value, axis, split_axis=0, concat_axis=0, tiled=True)]
    ppermute x2 -> x3, starting transfers between devices: 17.2 us -> 25 us  [swap_cores(): return lax.ppermute(value, 'c', [(0, 1), (1, 0)])]
    ppermute x1, waiting for transfers between devices: 17.1 us -> 21.2 us  [local(): own = lax.ppermute(amps, ('z', 'c'), swap)]
    all_to_all x3 -> x4, waiting for transfers between devices: 23.5 us -> 25.5 us  [exchange(): value = lax.all_to_all(value, axis, split_axis=0, concat_axis=0, tiled=True)]
  transfers between devices with their start and end apart: 7 -> 9, of which waited for: 6 -> 8; matrix products, arithmetic and copies ran while one was open for 2% -> 2% of each run, Pallas kernels for 0% -> 0%
where the time goes in v2:
time: 265 us; the launch traced here: 264 us
  blocking collectives  76.8 us (29%)
  waiting for transfers between devices  75.8 us (29%)
  starting transfers between devices  71.6 us (27%)
  between operations  14.4 us (5%)
  local copies, waits for them, and re-layouts  14 us (5%)
  other arithmetic  5.86 us (2%)
  matrix products  5.51 us (2%)
    all_to_all x3, blocking collectives, exchange(): value = lax.all_to_all(value, axis, split_axis=0, concat_axis=0, tiled=True)  40.7 us
    all_to_all x4, starting transfers between devices, exchange(): value = lax.all_to_all(value, axis, split_axis=0, concat_axis=0, tiled=True)  32.4 us
    all_gather x1, waiting for transfers between devices, local(): lax.all_gather(row.reshape(nx * r, nocc * wide), 'z', axis=0, tiled=True)  25.6 us
    all_to_all x4, waiting for transfers between devices, exchange(): value = lax.all_to_all(value, axis, split_axis=0, concat_axis=0, tiled=True)  25.5 us
    ppermute x3, starting transfers between devices, swap_cores(): return lax.ppermute(value, 'c', [(0, 1), (1, 0)])  25 us
    ppermute x1, waiting for transfers between devices, local(): own = lax.ppermute(amps, ('z', 'c'), swap)  21.2 us
    ppermute x1, starting transfers between devices, local(): own = lax.ppermute(amps, ('z', 'c'), swap)  14.2 us
    all_gather x1, blocking collectives, local(): masked = lax.all_gather(masked.reshape(-1, ao_part), 'x', axis=0)  13.2 us
  transfers between devices with their start and end apart: 9, of which 8 were waited for; matrix products, arithmetic and copies ran while one was open for 2% of the time, Pallas kernels for 0%

profile of v2, /device:TPU:1, one launch (start us, length us, event | category | flops | bytes accessed | tf_op | source)
XLA Modules:
  0.0 264.1 jit_solution(2619876952096611985)
XLA Ops:
  7.2 1.5 broadcast_in_dim.10
  8.7 15.7 %all-to-all-start = ((bf16[16,16,640]{2,1,0:T(8,128)(2,1)}), bf16[16,16,640]{2,1,0:T(8,128)(2,1)S(1)}, u32[]{:S(2)}, u32[]{:S(2)}) async-start(bf16[16,16,640]{2,1,0:T(8,128)(2,1)} %broadcast_in_dim.10), calls=%async_computation | async-start | bytes 655360 | tf_op jit(solution)/shard_map/transform/all_to_all | solution.py:18
  25.4 13.2 %all_gather.12 = bf16[4,192,640]{2,1,0:T(8,128)(2,1)S(1)} all-gather(bf16[1,192,640]{2,1,0:T(8,128)(2,1)S(1)} %bitcast.110), channel_id=1, replica_groups=mesh['x'=4,'z'=16,'c'=2,'y'=4] {'x'}, dimensions={0}, use_global_device_ids=true | all-gather | bytes 1228800 | tf_op jit(solution)/shard_map/transform/all_gather | solution.py:50
  38.7 1.0 all-to-all-done
  39.7 8.4 %collective-permute-start = (bf16[16,16,640]{2,1,0:T(8,128)(2,1)S(1)}, bf16[16,16,640]{2,1,0:T(8,128)(2,1)S(1)}, u32[]{:S(2)}, u32[]{:S(2)}) collective-permute-start(bf16[16,16,640]{2,1,0:T(8,128)(2,1)S(1)} %all-to-all-done), channel_id=1, source_target_pairs={{0,4},{4,0},{1,5},{5,1},{2,6},{6,2},{3,7},{7,3},{8,12},{12,8},{9,1... | collective-permute-start | bytes 983048 | tf_op jit(solution)/shard_map/transform/ppermute | solution.py:12
  48.1 1.2 collective-permute-done
  50.3 15.4 %all_to_all.57 = bf16[4,192,512]{2,1,0:T(8,128)(2,1)S(1)} all-to-all(bf16[4,192,512]{2,1,0:T(8,128)(2,1)S(1)} %bitcast.100), channel_id=1, replica_groups=mesh['x'=4,'z'=16,'c'=2,'y'=4] {'y'}, dimensions={0} | all-to-all | bytes 1572864 | tf_op jit(solution)/shard_map/transform/all_to_all | solution.py:18
  66.6 9.0 %all_to_all.58 = bf16[4,48,512]{2,1,0:T(8,128)(2,1)S(1)} all-to-all(bf16[4,48,512]{2,1,0:T(8,128)(2,1)S(1)} %bitcast.107), channel_id=1, replica_groups=mesh['x'=4,'z'=16,'c'=2,'y'=4] {'x'}, dimensions={0} | all-to-all | bytes 393216 | tf_op jit(solution)/shard_map/panels/all_to_all | solution.py:18
  76.6 6.7 %all-to-all-start.3 = ((bf16[16,16,384]{2,1,0:T(8,128)(2,1)}), bf16[16,16,384]{2,1,0:T(8,128)(2,1)S(1)}, u32[]{:S(2)}, u32[]{:S(2)}) async-start(bf16[16,16,384]{2,1,0:T(8,128)(2,1)} %pad_maximum_fusion.3), calls=%async_computation.3 | async-start | bytes 393216 | tf_op jit(solution)/shard_map/panels/all_to_all | solution.py:18
  83.3 15.0 %all-to-all-done.3 = bf16[16,16,384]{2,1,0:T(8,128)(2,1)S(1)} async-done(((bf16[16,16,384]{2,1,0:T(8,128)(2,1)}), bf16[16,16,384]{2,1,0:T(8,128)(2,1)S(1)}, u32[]{:S(2)}, u32[]{:S(2)}) %all-to-all-start.3) | async-done | bytes 196640 | tf_op jit(solution)/shard_map/panels/all_to_all | solution.py:18
  98.3 11.9 %all_gather.14 = bf16[4,256,384]{2,1,0:T(8,128)(2,1)S(1)} all-gather(bf16[1,256,384]{2,1,0:T(8,128)(2,1)S(1)} %bitcast.115), channel_id=1, replica_groups=mesh['x'=4,'z'=16,'c'=2,'y'=4] {'x'}, dimensions={0}, use_global_device_ids=true | all-gather | bytes 983040 | tf_op jit(solution)/shard_map/panels/all_gather | solution.py:68
  110.1 1.0 copy.61
  111.2 25.6 %all-gather.2.cloned.1.call-done = bf16[1024,1536]{1,0:T(8,128)(2,1)} async-done(((bf16[64,1536]{1,0:T(8,128)(2,1)}), bf16[1024,1536]{1,0:T(8,128)(2,1)}) %all-gather.2.cloned.1.call-update) | async-done | bytes 3145744 | tf_op jit(solution)/shard_map/panels/all_gather | solution.py:61
  136.7 3.2 %copy.57 = bf16[1536,1024]{1,0:T(8,128)(2,1)S(1)} copy(bf16[1536,1024]{0,1:T(8,128)(2,1)} %bitcast.98) | data formatting | bytes 6291456 | tf_op jit(solution)/shard_map/gram/dot_general | solution.py:73
  139.9 2.9 %fusion.5 = f32[3,2,256,384]{3,2,1,0:T(8,128)S(1)} fusion(bf16[3,2,256,1024]{3,2,1,0:T(8,128)(2,1)S(1)} %bitcast.99, bf16[1024,384,1,1]{1,0,3,2:T(8,128)(2,1)} %bitcast.113), kind=kOutput, calls=%fused_computation.31 | convolution fusion | flops 1207959552 | bytes 6291456 | tf_op jit(solution)/shard_map/gram/dot_general | solution.py:73
  143.0 1.3 copy-done.1
  144.3 10.6 %collective-permute-start.1 = (f32[3,256,384]{2,1,0:T(8,128)S(1)}, f32[3,256,384]{2,1,0:T(8,128)S(1)}, u32[]{:S(2)}, u32[]{:S(2)}) collective-permute-start(f32[3,256,384]{2,1,0:T(8,128)S(1)} %dynamic-slice_bitcast_fusion), channel_id=1, source_target_pairs={{0,4},{4,0},{1,5},{5,1},{2,6},{6,2},{3,7},{7,3},{8,12},{12,8},{9,1... | collective-permute-start | bytes 3538952 | tf_op jit(solution)/shard_map/gram/ppermute | solution.py:12
  157.4 1.4 fusion.1
  158.7 0.9 copy.62
  159.6 3.5 %all-to-all-start.4 = ((bf16[4,192,384]{2,1,0:T(8,128)(2,1)}), bf16[4,192,384]{2,1,0:T(8,128)(2,1)S(1)}, u32[]{:S(2)}, u32[]{:S(2)}) async-start(bf16[4,192,384]{2,1,0:T(8,128)(2,1)} %bitcast.39), calls=%async_computation.4 | async-start | bytes 1179648 | tf_op jit(solution)/shard_map/gram/all_to_all | solution.py:18
  163.3 9.5 %all-to-all-done.4 = bf16[4,192,384]{2,1,0:T(8,128)(2,1)S(1)} async-done(((bf16[4,192,384]{2,1,0:T(8,128)(2,1)}), bf16[4,192,384]{2,1,0:T(8,128)(2,1)S(1)}, u32[]{:S(2)}, u32[]{:S(2)}) %all-to-all-start.4) | async-done | bytes 589856 | tf_op jit(solution)/shard_map/gram/all_to_all | solution.py:18
  173.7 11.0 %all_gather.15 = bf16[4,192,384]{2,1,0:T(8,128)(2,1)S(1)} all-gather(bf16[1,192,384]{2,1,0:T(8,128)(2,1)S(1)} %pad_maximum_fusion.4), channel_id=1, replica_groups=mesh['x'=4,'z'=16,'c'=2,'y'=4] {'y'}, dimensions={0}, use_global_device_ids=true | all-gather | bytes 737280 | tf_op jit(solution)/shard_map/amplitudes/all_gather | solution.py:102
  184.8 6.0 %collective-permute-start.3 = (bf16[3,256,384]{2,1,0:T(8,128)(2,1)S(1)}, bf16[3,256,384]{2,1,0:T(8,128)(2,1)S(1)}, u32[]{:S(2)}, u32[]{:S(2)}) collective-permute-start(bf16[3,256,384]{2,1,0:T(8,128)(2,1)S(1)} %bitcast.103), channel_id=1, source_target_pairs={{0,4},{4,0},{1,5},{5,1},{2,6},{6,2},{3,7},{7,3},{8,12},{12,8},{9,1... | collective-permute-start | bytes 1769480 | tf_op jit(solution)/shard_map/amplitudes/ppermute | solution.py:12
  190.8 1.6 collective-permute-done.3
  192.8 1.6 copy-done
  194.4 1.8 convolution_convert_fusion
  196.3 16.3 %all_to_all.59 = bf16[4,256,384]{2,1,0:T(8,128)(2,1)S(1)} all-to-all(bf16[4,256,384]{2,1,0:T(8,128)(2,1)S(1)} %bitcast.101), channel_id=1, replica_groups=mesh['x'=4,'z'=16,'c'=2,'y'=4] {'x'}, dimensions={0} | all-to-all | bytes 1572864 | tf_op jit(solution)/shard_map/gamma/all_to_all | solution.py:18
  212.6 0.8 reduce_sum.45
  213.4 6.5 %all-to-all-start.6 = ((bf16[16,16,384]{2,1,0:T(8,128)(2,1)}), bf16[16,16,384]{2,1,0:T(8,128)(2,1)S(1)}, u32[]{:S(2)}, u32[]{:S(2)}) async-start(bf16[16,16,384]{2,1,0:T(8,128)(2,1)} %bitcast.54), calls=%async_computation.6 | async-start | bytes 393216 | tf_op jit(solution)/shard_map/gamma/all_to_all | solution.py:18
  219.9 14.2 %collective-permute-start.2 = (f32[3,64,3,128]{3,2,1,0:T(4,128)S(1)}, f32[3,64,3,128]{3,2,1,0:T(4,128)S(1)}, u32[]{:S(2)}, u32[]{:S(2)}) collective-permute-start(f32[3,64,3,128]{3,2,1,0:T(4,128)S(1)} %subtract_divide_fusion), channel_id=1, source_target_pairs={{0,0},{4,64},{8,8},{12,72},{16,16},{20,80},{24,24},{28,88},{32,32}... | collective-permute-start | bytes 884744 | tf_op jit(solution)/shard_map/amplitudes/ppermute | solution.py:100
  234.2 21.2 %collective-permute-done.2 = f32[3,64,3,128]{3,2,1,0:T(4,128)S(1)} collective-permute-done((f32[3,64,3,128]{3,2,1,0:T(4,128)S(1)}, f32[3,64,3,128]{3,2,1,0:T(4,128)S(1)}, u32[]{:S(2)}, u32[]{:S(2)}) %collective-permute-start.2) | collective-permute-done | bytes 294944 | tf_op jit(solution)/shard_map/amplitudes/ppermute | solution.py:100
  256.5 0.8 reshape.185
  (54 shorter events, 8.9 us)
Async XLA Ops:
  7.2 18.2 %copy-start.2 = (bf16[64,3,640]{2,0,1:T(8,128)(2,1)S(1)}, bf16[64,3,640]{2,0,1:T(8,128)(2,1)}, u32[]{:S(2)}) copy-start(bf16[64,3,640]{2,0,1:T(8,128)(2,1)} %param.6) | copy-start | bytes 737284
  8.7 31.0 %all-to-all-start = ((bf16[16,16,640]{2,1,0:T(8,128)(2,1)}), bf16[16,16,640]{2,1,0:T(8,128)(2,1)S(1)}, u32[]{:S(2)}, u32[]{:S(2)}) async-start(bf16[16,16,640]{2,1,0:T(8,128)(2,1)} %broadcast_in_dim.10), calls=%async_computation | async-start | bytes 655360 | tf_op jit(solution)/shard_map/transform/all_to_all | solution.py:18
  24.4 112.3 %all-gather.2.cloned.1.call-start = ((), (), s32[]{:S(2)}) async-start(), calls=%async_computation.7 | async-start | bytes 3342336 | tf_op jit(solution)/shard_map/panels/all_gather | solution.py:61
  39.7 9.6 %collective-permute-start = (bf16[16,16,640]{2,1,0:T(8,128)(2,1)S(1)}, bf16[16,16,640]{2,1,0:T(8,128)(2,1)S(1)}, u32[]{:S(2)}, u32[]{:S(2)}) collective-permute-start(bf16[16,16,640]{2,1,0:T(8,128)(2,1)S(1)} %all-to-all-done), channel_id=1, source_target_pairs={{0,4},{4,0},{1,5},{5,1},{2,6},{6,2},{3,7},{7,3},{8,12},{12,8},{9,1... | collective-permute-start | bytes 983048 | tf_op jit(solution)/shard_map/transform/ppermute | solution.py:12
  76.6 21.6 %all-to-all-start.3 = ((bf16[16,16,384]{2,1,0:T(8,128)(2,1)}), bf16[16,16,384]{2,1,0:T(8,128)(2,1)S(1)}, u32[]{:S(2)}, u32[]{:S(2)}) async-start(bf16[16,16,384]{2,1,0:T(8,128)(2,1)} %pad_maximum_fusion.3), calls=%async_computation.3 | async-start | bytes 393216 | tf_op jit(solution)/shard_map/panels/all_to_all | solution.py:18
  142.9 1.5 copy-start.1
  142.9 13.6 %copy-start.3 = (f32[512]{0:T(512)S(1)}, f32[512]{0:T(512)}, u32[]{:S(2)}) copy-start(f32[512]{0:T(512)} %param.9) | copy-start | bytes 6148
  142.9 13.6 %copy-start.4 = (s32[3]{0:T(128)S(1)}, s32[3]{0:T(128)}, u32[]{:S(2)}) copy-start(s32[3]{0:T(128)} %param.11) | copy-start | bytes 40
  144.3 13.0 %collective-permute-start.1 = (f32[3,256,384]{2,1,0:T(8,128)S(1)}, f32[3,256,384]{2,1,0:T(8,128)S(1)}, u32[]{:S(2)}, u32[]{:S(2)}) collective-permute-start(f32[3,256,384]{2,1,0:T(8,128)S(1)} %dynamic-slice_bitcast_fusion), channel_id=1, source_target_pairs={{0,4},{4,0},{1,5},{5,1},{2,6},{6,2},{3,7},{7,3},{8,12},{12,8},{9,1... | collective-permute-start | bytes 3538952 | tf_op jit(solution)/shard_map/gram/ppermute | solution.py:12
  159.6 13.2 %all-to-all-start.4 = ((bf16[4,192,384]{2,1,0:T(8,128)(2,1)}), bf16[4,192,384]{2,1,0:T(8,128)(2,1)S(1)}, u32[]{:S(2)}, u32[]{:S(2)}) async-start(bf16[4,192,384]{2,1,0:T(8,128)(2,1)} %bitcast.39), calls=%async_computation.4 | async-start | bytes 1179648 | tf_op jit(solution)/shard_map/gram/all_to_all | solution.py:18
  184.8 7.6 %collective-permute-start.3 = (bf16[3,256,384]{2,1,0:T(8,128)(2,1)S(1)}, bf16[3,256,384]{2,1,0:T(8,128)(2,1)S(1)}, u32[]{:S(2)}, u32[]{:S(2)}) collective-permute-start(bf16[3,256,384]{2,1,0:T(8,128)(2,1)S(1)} %bitcast.103), channel_id=1, source_target_pairs={{0,4},{4,0},{1,5},{5,1},{2,6},{6,2},{3,7},{7,3},{8,12},{12,8},{9,1... | collective-permute-start | bytes 1769480 | tf_op jit(solution)/shard_map/amplitudes/ppermute | solution.py:12
  192.5 1.9 copy-start
  213.4 42.7 %all-to-all-start.6 = ((bf16[16,16,384]{2,1,0:T(8,128)(2,1)}), bf16[16,16,384]{2,1,0:T(8,128)(2,1)S(1)}, u32[]{:S(2)}, u32[]{:S(2)}) async-start(bf16[16,16,384]{2,1,0:T(8,128)(2,1)} %bitcast.54), calls=%async_computation.6 | async-start | bytes 393216 | tf_op jit(solution)/shard_map/gamma/all_to_all | solution.py:18
  219.9 35.5 %collective-permute-start.2 = (f32[3,64,3,128]{3,2,1,0:T(4,128)S(1)}, f32[3,64,3,128]{3,2,1,0:T(4,128)S(1)}, u32[]{:S(2)}, u32[]{:S(2)}) collective-permute-start(f32[3,64,3,128]{3,2,1,0:T(4,128)S(1)} %subtract_divide_fusion), channel_id=1, source_target_pairs={{0,0},{4,64},{8,8},{12,72},{16,16},{20,80},{24,24},{28,88},{32,32}... | collective-permute-start | bytes 884744 | tf_op jit(solution)/shard_map/amplitudes/ppermute | solution.py:100
Sparse Core Ops, SparseCore 0:
  66.7 69.9 all-gather.1

commit v3 on v2

--- a/solution.py
+++ b/solution.py
@@ -1,6 +1,8 @@
 import jax
 import jax.numpy as jnp
 from jax import lax
+from jax.experimental import pallas as pl
+from jax.experimental.pallas import tpu as pltpu
 from jax.sharding import Mesh
 from jax.sharding import PartitionSpec as P
 
@@ -21,6 +23,124 @@
 
 def by_core(mine, theirs, core):
     return jnp.where(core == 0, mine, theirs), jnp.where(core == 0, theirs, mine)
+
+
+def gram_half(row, col, which, nocc, ny):
+    k_rows, lanes = row.shape
+    half = lanes // nocc // 2
+    share = half // ny
+    width = col.shape[1]
+
+    def body(which_ref, row_ref, col_ref, out_ref):
+        tile = lax.dot_general(
+            row_ref[...], col_ref[...], (((0,), (0,)), ((), ())), preferred_element_type=F32
+        )
+        out_ref[...] = tile.reshape(ny, 1, share, width)
+
+    return pl.pallas_call(
+        body,
+        out_shape=jax.ShapeDtypeStruct((ny, nocc, share, width), F32),
+        grid_spec=pltpu.PrefetchScalarGridSpec(
+            num_scalar_prefetch=1,
+            grid=(nocc,),
+            in_specs=[
+                pl.BlockSpec((k_rows, half), lambda i, w: (0, 2 * i + w[0])),
+                pl.BlockSpec((k_rows, width), lambda i, w: (0, 0)),
+            ],
+            out_specs=pl.BlockSpec((ny, 1, share, width), lambda i, w: (0, i, 0, 0)),
+        ),
+        compiler_params=pltpu.CompilerParams(vmem_limit_bytes=12 * 1024 * 1024),
+        cost_estimate=pl.CostEstimate(
+            flops=2 * k_rows * nocc * half * width,
+            bytes_accessed=2 * k_rows * (nocc * half + width) + 4 * nocc * half * width,
+            transcendentals=0,
+        ),
+        name="gram_half",
+    )(which.reshape(1), row, col)
+
+
+def contract(row, mine, theirs, core, nx, nz):
+    k_rows, lanes = row.shape
+    ny, nocc, share, width = mine.shape
+    half = ny * share
+    r = k_rows // nx // nz
+    steps = 4
+    zs = nz // steps
+
+    def body(core_ref, row_ref, mine_ref, theirs_ref, out_ref, tile_ref):
+        @pl.when(pl.program_id(0) == 0)
+        def _():
+            for i in range(nocc):
+                for q in range(ny):
+                    for k, ref in enumerate((mine_ref, theirs_ref)):
+                        side = core_ref[0] if k == 0 else 1 - core_ref[0]
+                        start = (2 * i + side) * half + q * share
+                        tile_ref[pl.ds(pl.multiple_of(start, share), share), :] = ref[q, i]
+
+        value = jnp.dot(row_ref[...], tile_ref[...], preferred_element_type=F32).astype(BF)
+        value = value.reshape(zs, nx, r, width)
+        for k in range(nx):
+            out_ref[k] = value[:, k]
+
+    return pl.pallas_call(
+        body,
+        out_shape=jax.ShapeDtypeStruct((nx, nz, r, width), BF),
+        grid_spec=pltpu.PrefetchScalarGridSpec(
+            num_scalar_prefetch=1,
+            grid=(steps,),
+            in_specs=[
+                pl.BlockSpec((k_rows // steps, lanes), lambda s, w: (s, 0)),
+                pl.BlockSpec((ny, nocc, share, width), lambda s, w: (0, 0, 0, 0)),
+                pl.BlockSpec((ny, nocc, share, width), lambda s, w: (0, 0, 0, 0)),
+            ],
+            out_specs=pl.BlockSpec((nx, zs, r, width), lambda s, w: (0, s, 0, 0)),
+            scratch_shapes=[pltpu.VMEM((lanes, width), BF)],
+        ),
+        compiler_params=pltpu.CompilerParams(vmem_limit_bytes=12 * 1024 * 1024),
+        cost_estimate=pl.CostEstimate(
+            flops=2 * k_rows * lanes * width,
+            bytes_accessed=2 * k_rows * (lanes + width) + 2 * lanes * width,
+            transcendentals=0,
+        ),
+        name="contract",
+    )(core.reshape(1), row, mine, theirs)
+
+
+def amplitudes_of(parts, slot, row_energy, col_energy):
+    nocc = slot.shape[0]
+    share, narrow = row_energy.shape[0], col_energy.shape[1]
+    ways = parts.shape[0]
+
+    def body(slot_ref, row_ref, col_ref, parts_ref, upper_ref, lower_ref, mixed_ref):
+        amps = {}
+        for i in range(nocc):
+            for j in range(nocc):
+                at = (pl.ds(i * share, share), pl.ds(j * narrow, narrow))
+                total = parts_ref[(0,) + at].astype(F32)
+                for k in range(1, ways):
+                    total = total + parts_ref[(k,) + at].astype(F32)
+                gap = slot_ref[i] + slot_ref[j] - row_ref[...] - col_ref[...]
+                amps[i, j] = total / gap
+                upper_ref[i, j] = amps[i, j][: share // 2]
+                lower_ref[i, j] = amps[i, j][share // 2 :]
+        for i in range(nocc):
+            for j in range(nocc):
+                value = 2.0 * amps[i, j] - amps[j, i]
+                mixed_ref[i, :, pl.ds(j * narrow, narrow)] = value.astype(BF)
+
+    vmem = pl.BlockSpec(memory_space=pltpu.VMEM)
+    return pl.pallas_call(
+        body,
+        out_shape=(
+            jax.ShapeDtypeStruct((nocc, nocc, share // 2, narrow), F32),
+            jax.ShapeDtypeStruct((nocc, nocc, share // 2, narrow), F32),
+            jax.ShapeDtypeStruct((nocc, share, nocc * narrow), BF),
+        ),
+        in_specs=[pl.BlockSpec(memory_space=pltpu.SMEM), vmem, vmem, vmem],
+        out_specs=(vmem, vmem, vmem),
+        compiler_params=pltpu.CompilerParams(vmem_limit_bytes=12 * 1024 * 1024),
+        name="amplitudes_of",
+    )(slot, row_energy, col_energy, parts)
 
 
 def local(half_ints, coef_virt, screen, occ_energy, virt_energy, batch_orbitals):
@@ -70,50 +190,36 @@
         col = col.transpose(1, 0, 2, 3).reshape(nz * nx * r, nocc * narrow)
 
     with jax.named_scope("gram"):
-        gram = lax.dot_general(
-            row, col, (((0,), (0,)), ((), ())), preferred_element_type=F32
-        )
-        gram = gram.reshape(nocc, 2, half, nocc * narrow)
-        mine = lax.dynamic_index_in_dim(gram, c, 1, keepdims=False)
-        other = lax.dynamic_index_in_dim(gram, 1 - c, 1, keepdims=False)
-        gram = mine + swap_cores(other)
-        gram = gram.reshape(nocc, ny, share, nocc * narrow).transpose(1, 0, 2, 3)
+        other = swap_cores(gram_half(row, col, 1 - c, nocc, ny))
+        gram = gram_half(row, col, c, nocc, ny) + other
         gram = exchange(gram.astype(BF).reshape(ny, nocc * share, nocc * narrow), "y")
-        gram = jnp.sum(gram.astype(F32), axis=0).reshape(nocc, share, nocc, narrow)
 
     with jax.named_scope("amplitudes"):
         row_energy = lax.dynamic_slice_in_dim(virt_energy, x * wide + c * half + y * share, share, 0)
         col_energy = lax.dynamic_slice_in_dim(virt_energy, (zl * 2 + zh) * narrow, narrow, 0)
-        denominators = (
-            slot_energy[:, None, None, None]
-            + slot_energy[None, None, :, None]
-            - row_energy[None, :, None, None]
-            - col_energy[None, None, None, :]
-        )
-        amps = gram / denominators
-        mixed = (2.0 * amps - jnp.transpose(amps, (2, 1, 0, 3))).astype(BF)
+        upper, lower, mixed = amplitudes_of(gram, slot_energy, row_energy[:, None], col_energy[None, :])
         swap = []
         for h in range(2):
             for l in range(nl):
                 for k in range(2):
                     swap.append(((h * nl + l) * 2 + k, (k * nl + l) * 2 + h))
-        own = lax.ppermute(amps, ("z", "c"), swap)
-        mixed = jnp.concatenate([mixed[:, :, j] for j in range(nocc)], axis=-1)
+        upper = lax.ppermute(upper, ("z", "c"), swap)
+        lower = lax.ppermute(lower, ("z", "c"), swap)
         mixed = lax.all_gather(mixed.reshape(nocc * share, nocc * narrow), "y", axis=0)
-        mixed = mixed.reshape(ny, nocc, share, nocc * narrow).transpose(1, 0, 2, 3)
-        mixed = mixed.reshape(nocc, half, nocc * narrow)
-        low, high = by_core(mixed, swap_cores(mixed), c)
-        mixed = jnp.stack([low, high], axis=1).reshape(nocc * wide, nocc * narrow)
+        mixed, upper = lax.optimization_barrier((mixed, upper))
+        mixed = mixed.reshape(ny, nocc, share, nocc * narrow)
+        theirs = swap_cores(mixed)
 
     with jax.named_scope("gamma"):
-        value = jnp.dot(row, mixed, preferred_element_type=F32).astype(BF)
-        value = value.reshape(nz, nx, r, nocc * narrow).transpose(1, 0, 2, 3)
+        value = contract(row, mixed, theirs, c, nx, nz)
         value = exchange(value.reshape(nx, nz * r, nocc * narrow), "x")
         value = jnp.sum(value.astype(F32), axis=0).astype(BF)
+        value, lower = lax.optimization_barrier((value, lower))
         value = exchange(value.reshape(nz, r, nocc * narrow), "z")
         value = value.reshape(2, nl, r, nocc, narrow).transpose(2, 3, 1, 0, 4)
         gamma = value.reshape(r, nocc, nv)
-    return own[None], gamma
+    own = jnp.concatenate([upper, lower], axis=2)
+    return own.transpose(0, 2, 1, 3)[None], gamma
 
 
 def solution(mesh):

time: 265 us -> 252 us (0.951); the launches traced: 264 us -> 247 us
  blocking collectives: 76.8 us -> 60 us
  starting transfers between devices: 71.6 us -> 78.8 us
  Pallas kernels: 0 us -> 7.1 us
  local copies, waits for them, and re-layouts: 14 us -> 8.31 us
  matrix products: 5.51 us -> 0.81 us
  waiting for transfers between devices: 75.8 us -> 73 us
    ppermute x1 -> x2, waiting for transfers between devices: 21.2 us -> 2.52 us  [the longest x1 2.52 us: local(): lower = lax.ppermute(lower, ('z', 'c'), swap)]
    all_to_all x3 -> x2, blocking collectives: 40.7 us -> 24.4 us  [exchange(): value = lax.all_to_all(value, axis, split_axis=0, concat_axis=0, tiled=True)]
    all_to_all x4 -> x5, waiting for transfers between devices: 25.5 us -> 40.9 us  [exchange(): value = lax.all_to_all(value, axis, split_axis=0, concat_axis=0, tiled=True)]
    all_to_all x4 -> x5, starting transfers between devices: 32.4 us -> 41.3 us  [exchange(): value = lax.all_to_all(value, axis, split_axis=0, concat_axis=0, tiled=True)]
    pallas_call x0 -> x4, Pallas kernels: none -> 7.1 us  [the longest x2 3.36 us: gram_half(): pl.pallas_call(body, out_shape=jax.ShapeDtypeStruct((ny, nocc, share, wid...]
    dot_general x2 -> x0, matrix products: 4.71 us -> none  [the longest x1 2.93 us: local(): lax.dot_general(row, col, (((0,), (0,)), ((), ())), preferred_element_typ...]
    ppermute x3, starting transfers between devices: 25 us -> 20.9 us  [swap_cores(): return lax.ppermute(value, 'c', [(0, 1), (1, 0)])]
    dot_general x1 -> x0, local copies, waits for them, and re-layouts: 3.18 us -> none  [local(): lax.dot_general(row, col, (((0,), (0,)), ((), ())), preferred_element_typ...]
  transfers between devices with their start and end apart: 9 -> 11, of which waited for: 8 -> 10; matrix products, arithmetic and copies ran while one was open for 2% -> 2% of each run, Pallas kernels for 0% -> 1%
where the time goes in v3:
time: 252 us; the launch traced here: 247 us
  starting transfers between devices  78.8 us (31%)
  waiting for transfers between devices  73 us (29%)
  blocking collectives  60 us (24%)
  between operations  14.4 us (6%)
  local copies, waits for them, and re-layouts  8.31 us (3%)
  Pallas kernels  7.1 us (3%)
  other arithmetic  5.11 us (2%)
    all_to_all x5, starting transfers between devices, exchange(): value = lax.all_to_all(value, axis, split_axis=0, concat_axis=0, tiled=True)  41.3 us
    all_to_all x5, waiting for transfers between devices, exchange(): value = lax.all_to_all(value, axis, split_axis=0, concat_axis=0, tiled=True)  40.9 us
    all_gather x1, waiting for transfers between devices, local(): lax.all_gather(row.reshape(nx * r, nocc * wide), 'z', axis=0, tiled=True)  25.6 us
    all_to_all x2, blocking collectives, exchange(): value = lax.all_to_all(value, axis, split_axis=0, concat_axis=0, tiled=True)  24.4 us
    ppermute x3, starting transfers between devices, swap_cores(): return lax.ppermute(value, 'c', [(0, 1), (1, 0)])  20.9 us
    all_gather x1, blocking collectives, local(): masked = lax.all_gather(masked.reshape(-1, ao_part), 'x', axis=0)  13.2 us
    all_gather x1, blocking collectives, local(): col = lax.all_gather(col.reshape(nz * r, nocc * narrow), 'x', axis=0)  11.9 us
    all_gather x1, blocking collectives, local(): lax.all_gather(mixed.reshape(nocc * share, nocc * narrow), 'y', axis=0)  10.5 us
  transfers between devices with their start and end apart: 11, of which 10 were waited for; matrix products, arithmetic and copies ran while one was open for 2% of the time, Pallas kernels for 1%

profile of v3, /device:TPU:1, one launch (start us, length us, event | category | flops | bytes accessed | tf_op | source)
XLA Modules:
  0.0 247.4 jit_solution(1072196614484425226)
XLA Ops:
  7.2 1.5 broadcast_in_dim.29
  8.7 15.7 %all-to-all-start = ((bf16[16,16,640]{2,1,0:T(8,128)(2,1)}), bf16[16,16,640]{2,1,0:T(8,128)(2,1)S(1)}, u32[]{:S(2)}, u32[]{:S(2)}) async-start(bf16[16,16,640]{2,1,0:T(8,128)(2,1)} %broadcast_in_dim.29), calls=%async_computation | async-start | bytes 655360 | tf_op jit(solution)/shard_map/transform/all_to_all | solution.py:20
  25.4 13.2 %all_gather.12 = bf16[4,192,640]{2,1,0:T(8,128)(2,1)S(1)} all-gather(bf16[1,192,640]{2,1,0:T(8,128)(2,1)S(1)} %bitcast.81), channel_id=1, replica_groups=mesh['x'=4,'z'=16,'c'=2,'y'=4] {'x'}, dimensions={0}, use_global_device_ids=true | all-gather | bytes 1228800 | tf_op jit(solution)/shard_map/transform/all_gather | solution.py:170
  38.7 1.0 all-to-all-done
  39.7 8.4 %collective-permute-start = (bf16[16,16,640]{2,1,0:T(8,128)(2,1)S(1)}, bf16[16,16,640]{2,1,0:T(8,128)(2,1)S(1)}, u32[]{:S(2)}, u32[]{:S(2)}) collective-permute-start(bf16[16,16,640]{2,1,0:T(8,128)(2,1)S(1)} %all-to-all-done), channel_id=1, source_target_pairs={{0,4},{4,0},{1,5},{5,1},{2,6},{6,2},{3,7},{7,3},{8,12},{12,8},{9,1... | collective-permute-start | bytes 983048 | tf_op jit(solution)/shard_map/transform/ppermute | solution.py:14
  48.1 1.2 collective-permute-done
  50.4 15.4 %all_to_all.57 = bf16[4,192,512]{2,1,0:T(8,128)(2,1)S(1)} all-to-all(bf16[4,192,512]{2,1,0:T(8,128)(2,1)S(1)} %bitcast.75), channel_id=1, replica_groups=mesh['x'=4,'z'=16,'c'=2,'y'=4] {'y'}, dimensions={0} | all-to-all | bytes 1572864 | tf_op jit(solution)/shard_map/transform/all_to_all | solution.py:20
  66.7 9.0 %all_to_all.58 = bf16[4,48,512]{2,1,0:T(8,128)(2,1)S(1)} all-to-all(bf16[4,48,512]{2,1,0:T(8,128)(2,1)S(1)} %bitcast.79), channel_id=1, replica_groups=mesh['x'=4,'z'=16,'c'=2,'y'=4] {'x'}, dimensions={0} | all-to-all | bytes 393216 | tf_op jit(solution)/shard_map/panels/all_to_all | solution.py:20
  76.6 6.7 %all-to-all-start.3 = ((bf16[16,16,384]{2,1,0:T(8,128)(2,1)}), bf16[16,16,384]{2,1,0:T(8,128)(2,1)S(1)}, u32[]{:S(2)}, u32[]{:S(2)}) async-start(bf16[16,16,384]{2,1,0:T(8,128)(2,1)} %pad_maximum_fusion.2), calls=%async_computation.3 | async-start | bytes 393216 | tf_op jit(solution)/shard_map/panels/all_to_all | solution.py:20
  83.3 14.9 %all-to-all-done.3 = bf16[16,16,384]{2,1,0:T(8,128)(2,1)S(1)} async-done(((bf16[16,16,384]{2,1,0:T(8,128)(2,1)}), bf16[16,16,384]{2,1,0:T(8,128)(2,1)S(1)}, u32[]{:S(2)}, u32[]{:S(2)}) %all-to-all-start.3) | async-done | bytes 196640 | tf_op jit(solution)/shard_map/panels/all_to_all | solution.py:20
  98.3 11.9 %all_gather.14 = bf16[4,256,384]{2,1,0:T(8,128)(2,1)S(1)} all-gather(bf16[1,256,384]{2,1,0:T(8,128)(2,1)S(1)} %bitcast.84), channel_id=1, replica_groups=mesh['x'=4,'z'=16,'c'=2,'y'=4] {'x'}, dimensions={0}, use_global_device_ids=true | all-gather | bytes 983040 | tf_op jit(solution)/shard_map/panels/all_gather | solution.py:188
  110.2 1.0 copy.38
  111.2 25.6 %all-gather.2.cloned.1.call-done.row_ref = bf16[1024,1536]{1,0:T(8,128)(2,1)} async-done(((bf16[64,1536]{1,0:T(8,128)(2,1)}), bf16[1024,1536]{1,0:T(8,128)(2,1)}) %all-gather.2.cloned.1.call-update) | async-done | bytes 3145744 | tf_op jit(solution)/shard_map/panels/all_gather | solution.py:181
  136.8 1.9 copy-done.1
  138.7 1.1 copy-done.3
  139.8 1.7 gram_half.3
  141.5 10.6 %collective-permute-start.1 = (f32[4,3,64,384]{3,2,1,0:T(8,128)S(1)}, f32[4,3,64,384]{3,2,1,0:T(8,128)S(1)}, u32[]{:S(2)}, u32[]{:S(2)}) collective-permute-start(f32[4,3,64,384]{3,2,1,0:T(8,128)S(1)} %gram_half.3), channel_id=1, source_target_pairs={{0,4},{4,0},{1,5},{5,1},{2,6},{6,2},{3,7},{7,3},{8,12},{12,8},{9,1... | collective-permute-start | bytes 3538952 | tf_op jit(solution)/shard_map/gram/ppermute | solution.py:14
  152.1 1.7 gram_half.2
  155.5 4.3 %all-to-all-start.4 = ((bf16[4,192,384]{2,1,0:T(8,128)(2,1)}), bf16[4,192,384]{2,1,0:T(8,128)(2,1)}, u32[]{:S(2)}, u32[]{:S(2)}) async-start(bf16[4,192,384]{2,1,0:T(8,128)(2,1)} %bitcast.77), calls=%async_computation.4 | async-start | bytes 1179648 | tf_op jit(solution)/shard_map/gram/all_to_all | solution.py:20
  160.3 9.5 %all-to-all-done.4.parts_ref = bf16[4,192,384]{2,1,0:T(8,128)(2,1)} async-done(((bf16[4,192,384]{2,1,0:T(8,128)(2,1)}), bf16[4,192,384]{2,1,0:T(8,128)(2,1)}, u32[]{:S(2)}, u32[]{:S(2)}) %all-to-all-start.4) | async-done | bytes 589856 | tf_op jit(solution)/shard_map/gram/all_to_all | solution.py:20
  169.8 1.2 amplitudes_of.1
  171.0 8.4 %collective-permute-start.2 = (f32[3,3,32,128]{3,2,1,0:T(8,128)S(1)}, f32[3,3,32,128]{3,2,1,0:T(8,128)S(1)}, u32[]{:S(2)}, u32[]{:S(2)}) collective-permute-start(f32[3,3,32,128]{3,2,1,0:T(8,128)S(1)} %get-tuple-element.14), channel_id=1, source_target_pairs={{0,0},{4,64},{8,8},{12,72},{16,16},{20,80},{24,24},{28,88},{32,32}... | collective-permute-start | bytes 442376 | tf_op jit(solution)/shard_map/amplitudes/ppermute | solution.py:206
  179.4 10.5 %all_gather.15 = bf16[4,192,384]{2,1,0:T(8,128)(2,1)S(1)} all-gather(bf16[1,192,384]{2,1,0:T(8,128)(2,1)S(1)} %bitcast.74), channel_id=1, replica_groups=mesh['x'=4,'z'=16,'c'=2,'y'=4] {'y'}, dimensions={0}, use_global_device_ids=true | all-gather | bytes 737280 | tf_op jit(solution)/shard_map/amplitudes/all_gather | solution.py:208
  189.9 1.9 collective-permute-start.3
  191.8 2.0 collective-permute-done.3.theirs_ref
  193.8 2.5 %contract.1 = bf16[4,16,16,384]{3,2,1,0:T(8,128)(2,1)S(1)} custom-call(s32[1]{0:T(128)} %bitcast.2.which_ref.core_ref, bf16[1024,1536]{1,0:T(8,128)(2,1)S(1)} %copy-done.2, bf16[4,3,64,384]{3,2,1,0:T(8,128)(2,1)S(1)} %bitcast.73, bf16[4,3,64,384]{3,2,1,0:T(8,128)(2,1)S(1)} %collective-permute-done.3.theirs_ref), custom_call_target="tpu_custom_call" | custom-call | flops 1207959552 | bytes 5111808 | tf_op jit(solution)/shard_map/gamma/contract/pallas_call | solution.py:85
  197.2 4.5 %all-to-all-start.5 = ((bf16[4,256,384]{2,1,0:T(8,128)(2,1)}), bf16[4,256,384]{2,1,0:T(8,128)(2,1)S(1)}, u32[]{:S(2)}, u32[]{:S(2)}) async-start(bf16[4,256,384]{2,1,0:T(8,128)(2,1)} %bitcast.71), calls=%async_computation.5 | async-start | bytes 1572864 | tf_op jit(solution)/shard_map/gamma/all_to_all | solution.py:20
  201.7 8.2 %collective-permute-start.4 = (f32[3,3,32,128]{3,2,1,0:T(8,128)S(1)}, f32[3,3,32,128]{3,2,1,0:T(8,128)S(1)}, u32[]{:S(2)}, u32[]{:S(2)}) collective-permute-start(f32[3,3,32,128]{3,2,1,0:T(8,128)S(1)} %get-tuple-element.17), channel_id=1, source_target_pairs={{0,0},{4,64},{8,8},{12,72},{16,16},{20,80},{24,24},{28,88},{32,32}... | collective-permute-start | bytes 442376 | tf_op jit(solution)/shard_map/amplitudes/ppermute | solution.py:207
  209.9 3.8 %all-to-all-done.5 = bf16[4,256,384]{2,1,0:T(8,128)(2,1)S(1)} async-done(((bf16[4,256,384]{2,1,0:T(8,128)(2,1)}), bf16[4,256,384]{2,1,0:T(8,128)(2,1)S(1)}, u32[]{:S(2)}, u32[]{:S(2)}) %all-to-all-start.5) | async-done | bytes 786464 | tf_op jit(solution)/shard_map/gamma/all_to_all | solution.py:20
  214.5 2.5 %collective-permute-done.4 = f32[3,3,32,128]{3,2,1,0:T(8,128)S(1)} collective-permute-done((f32[3,3,32,128]{3,2,1,0:T(8,128)S(1)}, f32[3,3,32,128]{3,2,1,0:T(8,128)S(1)}, u32[]{:S(2)}, u32[]{:S(2)}) %collective-permute-start.4) | collective-permute-done | bytes 147488 | tf_op jit(solution)/shard_map/amplitudes/ppermute | solution.py:207
  217.0 10.1 %all-to-all-start.6 = ((bf16[16,16,384]{2,1,0:T(8,128)(2,1)}), bf16[16,16,384]{2,1,0:T(8,128)(2,1)S(1)}, u32[]{:S(2)}, u32[]{:S(2)}) async-start(bf16[16,16,384]{2,1,0:T(8,128)(2,1)} %bitcast.41), calls=%async_computation.6 | async-start | bytes 393216 | tf_op jit(solution)/shard_map/gamma/all_to_all | solution.py:20
  227.8 11.6 %all-to-all-done.6 = bf16[16,16,384]{2,1,0:T(8,128)(2,1)S(1)} async-done(((bf16[16,16,384]{2,1,0:T(8,128)(2,1)}), bf16[16,16,384]{2,1,0:T(8,128)(2,1)S(1)}, u32[]{:S(2)}, u32[]{:S(2)}) %all-to-all-start.6) | async-done | bytes 196640 | tf_op jit(solution)/shard_map/gamma/all_to_all | solution.py:20
  (47 shorter events, 9.5 us)
Async XLA Ops:
  7.2 152.6 %copy-start = (f32[2048]{0:T(1024)S(1)}, f32[2048]{0:T(1024)}, u32[]{:S(2)}) copy-start(f32[2048]{0:T(1024)} %param.10) | copy-start | bytes 24580
  7.2 18.2 %copy-start.5 = (bf16[64,3,640]{2,0,1:T(8,128)(2,1)S(1)}, bf16[64,3,640]{2,0,1:T(8,128)(2,1)}, u32[]{:S(2)}) copy-start(bf16[64,3,640]{2,0,1:T(8,128)(2,1)} %param.6) | copy-start | bytes 737284
  8.7 31.0 %all-to-all-start = ((bf16[16,16,640]{2,1,0:T(8,128)(2,1)}), bf16[16,16,640]{2,1,0:T(8,128)(2,1)S(1)}, u32[]{:S(2)}, u32[]{:S(2)}) async-start(bf16[16,16,640]{2,1,0:T(8,128)(2,1)} %broadcast_in_dim.29), calls=%async_computation | async-start | bytes 655360 | tf_op jit(solution)/shard_map/transform/all_to_all | solution.py:20
  24.5 112.3 %all-gather.2.cloned.1.call-start = ((), (), s32[]{:S(2)}) async-start(), calls=%async_computation.7 | async-start | bytes 3342336 | tf_op jit(solution)/shard_map/panels/all_gather | solution.py:181
  39.7 9.6 %collective-permute-start = (bf16[16,16,640]{2,1,0:T(8,128)(2,1)S(1)}, bf16[16,16,640]{2,1,0:T(8,128)(2,1)S(1)}, u32[]{:S(2)}, u32[]{:S(2)}) collective-permute-start(bf16[16,16,640]{2,1,0:T(8,128)(2,1)S(1)} %all-to-all-done), channel_id=1, source_target_pairs={{0,4},{4,0},{1,5},{5,1},{2,6},{6,2},{3,7},{7,3},{8,12},{12,8},{9,1... | collective-permute-start | bytes 983048 | tf_op jit(solution)/shard_map/transform/ppermute | solution.py:14
  76.6 21.6 %all-to-all-start.3 = ((bf16[16,16,384]{2,1,0:T(8,128)(2,1)}), bf16[16,16,384]{2,1,0:T(8,128)(2,1)S(1)}, u32[]{:S(2)}, u32[]{:S(2)}) async-start(bf16[16,16,384]{2,1,0:T(8,128)(2,1)} %pad_maximum_fusion.2), calls=%async_computation.3 | async-start | bytes 393216 | tf_op jit(solution)/shard_map/panels/all_to_all | solution.py:20
  136.8 1.9 copy-start.1
  138.7 1.1 copy-start.3
  139.8 12.2 %copy-start.2 = (bf16[1024,1536]{1,0:T(8,128)(2,1)S(1)}, bf16[1024,1536]{1,0:T(8,128)(2,1)}, u32[]{:S(2)}) copy-start(bf16[1024,1536]{1,0:T(8,128)(2,1)} %all-gather.2.cloned.1.call-done.row_ref) | copy-start | bytes 9437188
  141.5 13.0 %collective-permute-start.1 = (f32[4,3,64,384]{3,2,1,0:T(8,128)S(1)}, f32[4,3,64,384]{3,2,1,0:T(8,128)S(1)}, u32[]{:S(2)}, u32[]{:S(2)}) collective-permute-start(f32[4,3,64,384]{3,2,1,0:T(8,128)S(1)} %gram_half.3), channel_id=1, source_target_pairs={{0,4},{4,0},{1,5},{5,1},{2,6},{6,2},{3,7},{7,3},{8,12},{12,8},{9,1... | collective-permute-start | bytes 3538952 | tf_op jit(solution)/shard_map/gram/ppermute | solution.py:14
  155.5 4.6 %copy-start.6 = (f32[512]{0:T(512)S(1)}, f32[512]{0:T(512)}, u32[]{:S(2)}) copy-start(f32[512]{0:T(512)} %param.9) | copy-start | bytes 6148
  155.5 4.6 %copy-start.7 = (s32[3]{0:T(128)S(1)}, s32[3]{0:T(128)}, u32[]{:S(2)}) copy-start(s32[3]{0:T(128)} %param.11) | copy-start | bytes 40
  155.5 14.3 %all-to-all-start.4 = ((bf16[4,192,384]{2,1,0:T(8,128)(2,1)}), bf16[4,192,384]{2,1,0:T(8,128)(2,1)}, u32[]{:S(2)}, u32[]{:S(2)}) async-start(bf16[4,192,384]{2,1,0:T(8,128)(2,1)} %bitcast.77), calls=%async_computation.4 | async-start | bytes 1179648 | tf_op jit(solution)/shard_map/gram/all_to_all | solution.py:20
  171.0 18.9 %collective-permute-start.2 = (f32[3,3,32,128]{3,2,1,0:T(8,128)S(1)}, f32[3,3,32,128]{3,2,1,0:T(8,128)S(1)}, u32[]{:S(2)}, u32[]{:S(2)}) collective-permute-start(f32[3,3,32,128]{3,2,1,0:T(8,128)S(1)} %get-tuple-element.14), channel_id=1, source_target_pairs={{0,0},{4,64},{8,8},{12,72},{16,16},{20,80},{24,24},{28,88},{32,32}... | collective-permute-start | bytes 442376 | tf_op jit(solution)/shard_map/amplitudes/ppermute | solution.py:206
  189.9 3.9 %collective-permute-start.3 = (bf16[4,3,64,384]{3,2,1,0:T(8,128)(2,1)S(1)}, bf16[4,3,64,384]{3,2,1,0:T(8,128)(2,1)S(1)}, u32[]{:S(2)}, u32[]{:S(2)}) collective-permute-start(bf16[4,3,64,384]{3,2,1,0:T(8,128)(2,1)S(1)} %bitcast.72), channel_id=1, source_target_pairs={{0,4},{4,0},{1,5},{5,1},{2,6},{6,2},{3,7},{7,3},{8,12},{12,8},{9,1... | collective-permute-start | bytes 1769480 | tf_op jit(solution)/shard_map/amplitudes/ppermute | solution.py:14
  196.3 0.9 copy-start.4
  197.2 16.5 %all-to-all-start.5 = ((bf16[4,256,384]{2,1,0:T(8,128)(2,1)}), bf16[4,256,384]{2,1,0:T(8,128)(2,1)S(1)}, u32[]{:S(2)}, u32[]{:S(2)}) async-start(bf16[4,256,384]{2,1,0:T(8,128)(2,1)} %bitcast.71), calls=%async_computation.5 | async-start | bytes 1572864 | tf_op jit(solution)/shard_map/gamma/all_to_all | solution.py:20
  201.7 15.3 %collective-permute-start.4 = (f32[3,3,32,128]{3,2,1,0:T(8,128)S(1)}, f32[3,3,32,128]{3,2,1,0:T(8,128)S(1)}, u32[]{:S(2)}, u32[]{:S(2)}) collective-permute-start(f32[3,3,32,128]{3,2,1,0:T(8,128)S(1)} %get-tuple-element.17), channel_id=1, source_target_pairs={{0,0},{4,64},{8,8},{12,72},{16,16},{20,80},{24,24},{28,88},{32,32}... | collective-permute-start | bytes 442376 | tf_op jit(solution)/shard_map/amplitudes/ppermute | solution.py:207
  217.0 22.4 %all-to-all-start.6 = ((bf16[16,16,384]{2,1,0:T(8,128)(2,1)}), bf16[16,16,384]{2,1,0:T(8,128)(2,1)S(1)}, u32[]{:S(2)}, u32[]{:S(2)}) async-start(bf16[16,16,384]{2,1,0:T(8,128)(2,1)} %bitcast.41), calls=%async_computation.6 | async-start | bytes 393216 | tf_op jit(solution)/shard_map/gamma/all_to_all | solution.py:20
Sparse Core Ops, SparseCore 0:
  66.8 69.9 all-gather.1

commit v4 on v3

--- a/solution.py
+++ b/solution.py
@@ -8,6 +8,7 @@
 
 BF = jnp.bfloat16
 F32 = jnp.float32
+ROOM = 63 * 1024 * 1024
 
 
 def swap_cores(value):
@@ -31,25 +32,28 @@
     share = half // ny
     width = col.shape[1]
 
-    def body(which_ref, row_ref, col_ref, out_ref):
-        tile = lax.dot_general(
-            row_ref[...], col_ref[...], (((0,), (0,)), ((), ())), preferred_element_type=F32
-        )
-        out_ref[...] = tile.reshape(ny, 1, share, width)
-
+    def body(which_ref, row_ref, col_ref, out_ref, tiles_ref, sems):
+        def fetch(i):
+            start = pl.multiple_of((2 * i + which_ref[0]) * half, half)
+            return pltpu.make_async_copy(row_ref.at[:, pl.ds(start, half)], tiles_ref.at[i], sems.at[i])
+
+        for i in range(nocc):
+            fetch(i).start()
+        for i in range(nocc):
+            fetch(i).wait()
+            tile = lax.dot_general(
+                tiles_ref[i], col_ref[...], (((0,), (0,)), ((), ())), preferred_element_type=F32
+            )
+            out_ref[:, i] = tile.reshape(ny, share, width)
+
+    vmem = pl.BlockSpec(memory_space=pltpu.VMEM)
     return pl.pallas_call(
         body,
         out_shape=jax.ShapeDtypeStruct((ny, nocc, share, width), F32),
-        grid_spec=pltpu.PrefetchScalarGridSpec(
-            num_scalar_prefetch=1,
-            grid=(nocc,),
-            in_specs=[
-                pl.BlockSpec((k_rows, half), lambda i, w: (0, 2 * i + w[0])),
-                pl.BlockSpec((k_rows, width), lambda i, w: (0, 0)),
-            ],
-            out_specs=pl.BlockSpec((ny, 1, share, width), lambda i, w: (0, i, 0, 0)),
-        ),
-        compiler_params=pltpu.CompilerParams(vmem_limit_bytes=12 * 1024 * 1024),
+        in_specs=[pl.BlockSpec(memory_space=pltpu.SMEM), pl.BlockSpec(memory_space=pltpu.HBM), vmem],
+        out_specs=vmem,
+        scratch_shapes=[pltpu.VMEM((nocc, k_rows, half), BF), pltpu.SemaphoreType.DMA((nocc,))],
+        compiler_params=pltpu.CompilerParams(vmem_limit_bytes=ROOM),
         cost_estimate=pl.CostEstimate(
             flops=2 * k_rows * nocc * half * width,
             bytes_accessed=2 * k_rows * (nocc * half + width) + 4 * nocc * half * width,
@@ -67,36 +71,38 @@
     steps = 4
     zs = nz // steps
 
-    def body(core_ref, row_ref, mine_ref, theirs_ref, out_ref, tile_ref):
-        @pl.when(pl.program_id(0) == 0)
-        def _():
-            for i in range(nocc):
-                for q in range(ny):
-                    for k, ref in enumerate((mine_ref, theirs_ref)):
-                        side = core_ref[0] if k == 0 else 1 - core_ref[0]
-                        start = (2 * i + side) * half + q * share
-                        tile_ref[pl.ds(pl.multiple_of(start, share), share), :] = ref[q, i]
-
-        value = jnp.dot(row_ref[...], tile_ref[...], preferred_element_type=F32).astype(BF)
-        value = value.reshape(zs, nx, r, width)
-        for k in range(nx):
-            out_ref[k] = value[:, k]
-
+    def body(core_ref, row_ref, mine_ref, theirs_ref, out_ref, rows_ref, tile_ref, sems):
+        def fetch(s):
+            size = k_rows // steps
+            return pltpu.make_async_copy(row_ref.at[pl.ds(s * size, size), :], rows_ref.at[s], sems.at[s])
+
+        for s in range(steps):
+            fetch(s).start()
+        for i in range(nocc):
+            for q in range(ny):
+                for k, ref in enumerate((mine_ref, theirs_ref)):
+                    side = core_ref[0] if k == 0 else 1 - core_ref[0]
+                    start = (2 * i + side) * half + q * share
+                    tile_ref[pl.ds(pl.multiple_of(start, share), share), :] = ref[q, i]
+        for s in range(steps):
+            fetch(s).wait()
+            value = jnp.dot(rows_ref[s], tile_ref[...], preferred_element_type=F32).astype(BF)
+            value = value.reshape(zs, nx, r, width)
+            for k in range(nx):
+                out_ref[k, s * zs : (s + 1) * zs] = value[:, k]
+
+    vmem = pl.BlockSpec(memory_space=pltpu.VMEM)
     return pl.pallas_call(
         body,
         out_shape=jax.ShapeDtypeStruct((nx, nz, r, width), BF),
-        grid_spec=pltpu.PrefetchScalarGridSpec(
-            num_scalar_prefetch=1,
-            grid=(steps,),
-            in_specs=[
-                pl.BlockSpec((k_rows // steps, lanes), lambda s, w: (s, 0)),
-                pl.BlockSpec((ny, nocc, share, width), lambda s, w: (0, 0, 0, 0)),
-                pl.BlockSpec((ny, nocc, share, width), lambda s, w: (0, 0, 0, 0)),
-            ],
-            out_specs=pl.BlockSpec((nx, zs, r, width), lambda s, w: (0, s, 0, 0)),
-            scratch_shapes=[pltpu.VMEM((lanes, width), BF)],
-        ),
-        compiler_params=pltpu.CompilerParams(vmem_limit_bytes=12 * 1024 * 1024),
+        in_specs=[pl.BlockSpec(memory_space=pltpu.SMEM), pl.BlockSpec(memory_space=pltpu.HBM), vmem, vmem],
+        out_specs=vmem,
+        scratch_shapes=[
+            pltpu.VMEM((steps, k_rows // steps, lanes), BF),
+            pltpu.VMEM((lanes, width), BF),
+            pltpu.SemaphoreType.DMA((steps,)),
+        ],
+        compiler_params=pltpu.CompilerParams(vmem_limit_bytes=ROOM),
         cost_estimate=pl.CostEstimate(
             flops=2 * k_rows * lanes * width,
             bytes_accessed=2 * k_rows * (lanes + width) + 2 * lanes * width,
@@ -141,6 +147,28 @@
         compiler_params=pltpu.CompilerParams(vmem_limit_bytes=12 * 1024 * 1024),
         name="amplitudes_of",
     )(slot, row_energy, col_energy, parts)
+
+
+def place(value, nocc):
+    nz, r, lanes = value.shape
+    narrow = lanes // nocc
+    nl = nz // 2
+
+    def body(value_ref, out_ref):
+        for i in range(nocc):
+            for k in range(nz):
+                block = (k % nl + nl // 2) % nl * 2 + k // nl
+                out_ref[i, :, pl.ds(block * narrow, narrow)] = value_ref[k, :, pl.ds(i * narrow, narrow)]
+
+    vmem = pl.BlockSpec(memory_space=pltpu.VMEM)
+    return pl.pallas_call(
+        body,
+        out_shape=jax.ShapeDtypeStruct((nocc, r, nz * narrow), BF),
+        in_specs=[vmem],
+        out_specs=vmem,
+        compiler_params=pltpu.CompilerParams(vmem_limit_bytes=12 * 1024 * 1024),
+        name="place",
+    )(value)
 
 
 def local(half_ints, coef_virt, screen, occ_energy, virt_energy, batch_orbitals):
@@ -180,7 +208,7 @@
         row = jnp.concatenate([three[:, i] for i in range(nocc)], axis=-1)
         row = lax.all_gather(row.reshape(nx * r, nocc * wide), "z", axis=0, tiled=True)
         col = exchange(three.reshape(nx, nocc * r, wide), "x")
-        col = col.reshape(nx, nocc, r, ways // 2, 2, narrow)
+        col = jnp.roll(col, nx // 2, axis=0).reshape(nx, nocc, r, ways // 2, 2, narrow)
         col = jnp.concatenate(
             [col[:, i].transpose(3, 0, 2, 1, 4).reshape(nz, r, narrow) for i in range(nocc)], axis=-1
         )
@@ -196,13 +224,13 @@
 
     with jax.named_scope("amplitudes"):
         row_energy = lax.dynamic_slice_in_dim(virt_energy, x * wide + c * half + y * share, share, 0)
-        col_energy = lax.dynamic_slice_in_dim(virt_energy, (zl * 2 + zh) * narrow, narrow, 0)
+        col_energy = lax.dynamic_slice_in_dim(virt_energy, ((zl + nl // 2) % nl * 2 + zh) * narrow, narrow, 0)
         upper, lower, mixed = amplitudes_of(gram, slot_energy, row_energy[:, None], col_energy[None, :])
         swap = []
         for h in range(2):
             for l in range(nl):
                 for k in range(2):
-                    swap.append(((h * nl + l) * 2 + k, (k * nl + l) * 2 + h))
+                    swap.append(((h * nl + l) * 2 + k, (k * nl + (l + nl // 2) % nl) * 2 + h))
         upper = lax.ppermute(upper, ("z", "c"), swap)
         lower = lax.ppermute(lower, ("z", "c"), swap)
         mixed = lax.all_gather(mixed.reshape(nocc * share, nocc * narrow), "y", axis=0)
@@ -216,10 +244,9 @@
         value = jnp.sum(value.astype(F32), axis=0).astype(BF)
         value, lower = lax.optimization_barrier((value, lower))
         value = exchange(value.reshape(nz, r, nocc * narrow), "z")
-        value = value.reshape(2, nl, r, nocc, narrow).transpose(2, 3, 1, 0, 4)
-        gamma = value.reshape(r, nocc, nv)
+        gamma = place(value, nocc)
     own = jnp.concatenate([upper, lower], axis=2)
-    return own.transpose(0, 2, 1, 3)[None], gamma
+    return own.transpose(0, 2, 1, 3)[None], gamma.transpose(1, 0, 2)
 
 
 def solution(mesh):

time: 252 us -> 253 us (level)
  the two profiles are of different devices: /device:TPU:1 before, /device:TPU:2 now
where the time goes in v4:
time: 253 us; the launch traced here: 252 us
  waiting for transfers between devices  86.3 us (34%)
  blocking collectives  67.3 us (27%)
  starting transfers between devices  56.1 us (22%)
  Pallas kernels  16.4 us (6%)
  between operations  14.4 us (6%)
  other arithmetic  6.74 us (3%)
  local copies, waits for them, and re-layouts  3.49 us (1%)
    all_to_all x5, waiting for transfers between devices, exchange(): value = lax.all_to_all(value, axis, split_axis=0, concat_axis=0, tiled=True)  53.8 us
    all_to_all x5, starting transfers between devices, exchange(): value = lax.all_to_all(value, axis, split_axis=0, concat_axis=0, tiled=True)  41 us
    all_gather x1, waiting for transfers between devices, local(): lax.all_gather(row.reshape(nx * r, nocc * wide), 'z', axis=0, tiled=True)  28.8 us
    all_to_all x2, blocking collectives, exchange(): value = lax.all_to_all(value, axis, split_axis=0, concat_axis=0, tiled=True)  26.3 us
    all_gather x1, blocking collectives, local(): masked = lax.all_gather(masked.reshape(-1, ao_part), 'x', axis=0)  15.1 us
    all_gather x1, blocking collectives, local(): lax.all_gather(mixed.reshape(nocc * share, nocc * narrow), 'y', axis=0)  13.1 us
    all_gather x1, blocking collectives, local(): col = lax.all_gather(col.reshape(nz * r, nocc * narrow), 'x', axis=0)  12.8 us
    pallas_call x2, Pallas kernels, gram_half(): pl.pallas_call(body, out_shape=jax.ShapeDtypeStruct((ny, nocc, share, wid...  9.34 us
  transfers between devices with their start and end apart: 11, of which 8 were waited for; matrix products, arithmetic and copies ran while one was open for 2% of the time, Pallas kernels for 2%

profile of v4, /device:TPU:2, one launch (start us, length us, event | category | flops | bytes accessed | tf_op | source)
XLA Modules:
  0.0 251.6 jit_solution(16543389666193648036)
XLA Ops:
  7.2 1.5 broadcast_in_dim.29
  8.7 15.2 %all-to-all-start = ((bf16[16,16,640]{2,1,0:T(8,128)(2,1)}), bf16[16,16,640]{2,1,0:T(8,128)(2,1)S(1)}, u32[]{:S(2)}, u32[]{:S(2)}) async-start(bf16[16,16,640]{2,1,0:T(8,128)(2,1)} %broadcast_in_dim.29), calls=%async_computation | async-start | bytes 655360 | tf_op jit(solution)/shard_map/transform/all_to_all | solution.py:21
  24.9 15.1 %all_gather.12 = bf16[4,192,640]{2,1,0:T(8,128)(2,1)S(1)} all-gather(bf16[1,192,640]{2,1,0:T(8,128)(2,1)S(1)} %bitcast.77), channel_id=1, replica_groups=mesh['x'=4,'z'=16,'c'=2,'y'=4] {'x'}, dimensions={0}, use_global_device_ids=true | all-gather | bytes 1228800 | tf_op jit(solution)/shard_map/transform/all_gather | solution.py:198
  40.0 4.7 %all-to-all-done = bf16[16,16,640]{2,1,0:T(8,128)(2,1)S(1)} async-done(((bf16[16,16,640]{2,1,0:T(8,128)(2,1)}), bf16[16,16,640]{2,1,0:T(8,128)(2,1)S(1)}, u32[]{:S(2)}, u32[]{:S(2)}) %all-to-all-start) | async-done | bytes 327712 | tf_op jit(solution)/shard_map/transform/all_to_all | solution.py:21
  44.7 1.9 collective-permute-start
  46.6 1.6 collective-permute-done
  48.4 0.8 fusion
  49.2 16.9 %all_to_all.57 = bf16[4,192,512]{2,1,0:T(8,128)(2,1)S(1)} all-to-all(bf16[4,192,512]{2,1,0:T(8,128)(2,1)S(1)} %bitcast.70), channel_id=1, replica_groups=mesh['x'=4,'z'=16,'c'=2,'y'=4] {'y'}, dimensions={0} | all-to-all | bytes 1572864 | tf_op jit(solution)/shard_map/transform/all_to_all | solution.py:21
  67.0 9.5 %all_to_all.58 = bf16[4,48,512]{2,1,0:T(8,128)(2,1)S(1)} all-to-all(bf16[4,48,512]{2,1,0:T(8,128)(2,1)S(1)} %bitcast.76), channel_id=1, replica_groups=mesh['x'=4,'z'=16,'c'=2,'y'=4] {'x'}, dimensions={0} | all-to-all | bytes 393216 | tf_op jit(solution)/shard_map/panels/all_to_all | solution.py:21
  77.7 7.0 %all-to-all-start.3 = ((bf16[16,16,384]{2,1,0:T(8,128)(2,1)}), bf16[16,16,384]{2,1,0:T(8,128)(2,1)S(1)}, u32[]{:S(2)}, u32[]{:S(2)}) async-start(bf16[16,16,384]{2,1,0:T(8,128)(2,1)} %pad_maximum_fusion.2), calls=%async_computation.3 | async-start | bytes 393216 | tf_op jit(solution)/shard_map/panels/all_to_all | solution.py:21
  84.6 17.4 %all-to-all-done.3 = bf16[16,16,384]{2,1,0:T(8,128)(2,1)S(1)} async-done(((bf16[16,16,384]{2,1,0:T(8,128)(2,1)}), bf16[16,16,384]{2,1,0:T(8,128)(2,1)S(1)}, u32[]{:S(2)}, u32[]{:S(2)}) %all-to-all-start.3) | async-done | bytes 196640 | tf_op jit(solution)/shard_map/panels/all_to_all | solution.py:21
  102.0 12.8 %all_gather.14 = bf16[4,256,384]{2,1,0:T(8,128)(2,1)S(1)} all-gather(bf16[1,256,384]{2,1,0:T(8,128)(2,1)S(1)} %bitcast.80), channel_id=1, replica_groups=mesh['x'=4,'z'=16,'c'=2,'y'=4] {'x'}, dimensions={0}, use_global_device_ids=true | all-gather | bytes 983040 | tf_op jit(solution)/shard_map/panels/all_gather | solution.py:216
  114.8 1.0 copy.36
  115.8 28.8 %all-gather.2.cloned.1.call-done.row_ref = bf16[1024,1536]{1,0:T(8,128)(2,1)} async-done(((bf16[64,1536]{1,0:T(8,128)(2,1)}), bf16[1024,1536]{1,0:T(8,128)(2,1)}) %all-gather.2.cloned.1.call-update) | async-done | bytes 3145744 | tf_op jit(solution)/shard_map/panels/all_gather | solution.py:209
  144.7 4.7 %gram_half.3 = f32[4,3,64,384]{3,2,1,0:T(8,128)} custom-call(s32[1]{0:T(128)} %bitcast.34.which_ref, bf16[1024,1536]{1,0:T(8,128)(2,1)} %all-gather.2.cloned.1.call-done.row_ref, bf16[1024,384]{1,0:T(8,128)(2,1)} %bitcast.68), custom_call_target="tpu_custom_call" | custom-call | flops 603979776 | bytes 3538944 | tf_op jit(solution)/shard_map/gram/gram_half/pallas_call | solution.py:50
  149.4 1.9 collective-permute-start.1
  151.3 4.6 %gram_half.2 = f32[4,3,64,384]{3,2,1,0:T(8,128)} custom-call(s32[1]{0:T(128)} %bitcast.2.which_ref.core_ref, bf16[1024,1536]{1,0:T(8,128)(2,1)} %all-gather.2.cloned.1.call-done.row_ref, bf16[1024,384]{1,0:T(8,128)(2,1)} %bitcast.69), custom_call_target="tpu_custom_call" | custom-call | flops 603979776 | bytes 3538944 | tf_op jit(solution)/shard_map/gram/gram_half/pallas_call | solution.py:50
  156.0 2.6 %add_convert_fusion = bf16[4,3,64,384]{3,2,1,0:T(8,128)(2,1)} fusion(f32[4,3,64,384]{3,2,1,0:T(8,128)} %gram_half.2, f32[4,3,64,384]{3,2,1,0:T(8,128)} %collective-permute-done.1), kind=kLoop, calls=%fused_computation.2 | loop fusion | flops 589824 | bytes 2949120 | tf_op jit(solution)/shard_map/gram/convert_element_type | solution.py:223
  158.6 3.6 %all-to-all-start.4 = ((bf16[4,192,384]{2,1,0:T(8,128)(2,1)}), bf16[4,192,384]{2,1,0:T(8,128)(2,1)S(1)}, u32[]{:S(2)}, u32[]{:S(2)}) async-start(bf16[4,192,384]{2,1,0:T(8,128)(2,1)} %bitcast.35), calls=%async_computation.4 | async-start | bytes 1179648 | tf_op jit(solution)/shard_map/gram/all_to_all | solution.py:21
  162.7 10.6 %all-to-all-done.4.parts_ref = bf16[4,192,384]{2,1,0:T(8,128)(2,1)S(1)} async-done(((bf16[4,192,384]{2,1,0:T(8,128)(2,1)}), bf16[4,192,384]{2,1,0:T(8,128)(2,1)S(1)}, u32[]{:S(2)}, u32[]{:S(2)}) %all-to-all-start.4) | async-done | bytes 589856 | tf_op jit(solution)/shard_map/gram/all_to_all | solution.py:21
  174.0 4.4 %collective-permute-start.2 = (f32[3,3,32,128]{3,2,1,0:T(8,128)S(1)}, f32[3,3,32,128]{3,2,1,0:T(8,128)S(1)}, u32[]{:S(2)}, u32[]{:S(2)}) collective-permute-start(f32[3,3,32,128]{3,2,1,0:T(8,128)S(1)} %get-tuple-element.14), channel_id=1, source_target_pairs={{0,32},{4,96},{8,40},{12,104},{16,48},{20,112},{24,56},{28,120},{3... | collective-permute-start | bytes 442376 | tf_op jit(solution)/shard_map/amplitudes/ppermute | solution.py:234
  178.4 13.1 %all_gather.15 = bf16[4,192,384]{2,1,0:T(8,128)(2,1)S(1)} all-gather(bf16[1,192,384]{2,1,0:T(8,128)(2,1)S(1)} %bitcast.67), channel_id=1, replica_groups=mesh['x'=4,'z'=16,'c'=2,'y'=4] {'y'}, dimensions={0}, use_global_device_ids=true | all-gather | bytes 737280 | tf_op jit(solution)/shard_map/amplitudes/all_gather | solution.py:236
  191.5 1.9 collective-permute-start.3
  193.4 2.1 collective-permute-done.3.theirs_ref
  195.5 5.7 %contract.1 = bf16[4,16,16,384]{3,2,1,0:T(8,128)(2,1)} custom-call(s32[1]{0:T(128)} %bitcast.2.which_ref.core_ref, bf16[1024,1536]{1,0:T(8,128)(2,1)} %all-gather.2.cloned.1.call-done.row_ref, bf16[4,3,64,384]{3,2,1,0:T(8,128)(2,1)} %bitcast.74, bf16[4,3,64,384]{3,2,1,0:T(8,128)(2,1)} %collective-permute-done.3.theirs_ref), custom_call_target="tpu_custom_call" | custom-call | flops 1207959552 | bytes 5111808 | tf_op jit(solution)/shard_map/gamma/contract/pallas_call | solution.py:95
  201.2 5.4 %all-to-all-start.5 = ((bf16[4,256,384]{2,1,0:T(8,128)(2,1)}), bf16[4,256,384]{2,1,0:T(8,128)(2,1)S(1)}, u32[]{:S(2)}, u32[]{:S(2)}) async-start(bf16[4,256,384]{2,1,0:T(8,128)(2,1)} %bitcast.72), calls=%async_computation.5 | async-start | bytes 1572864 | tf_op jit(solution)/shard_map/gamma/all_to_all | solution.py:21
  206.6 4.9 %collective-permute-start.4 = (f32[3,3,32,128]{3,2,1,0:T(8,128)S(1)}, f32[3,3,32,128]{3,2,1,0:T(8,128)S(1)}, u32[]{:S(2)}, u32[]{:S(2)}) collective-permute-start(f32[3,3,32,128]{3,2,1,0:T(8,128)S(1)} %get-tuple-element.17), channel_id=1, source_target_pairs={{0,32},{4,96},{8,40},{12,104},{16,48},{20,112},{24,56},{28,120},{3... | collective-permute-start | bytes 442376 | tf_op jit(solution)/shard_map/amplitudes/ppermute | solution.py:235
  211.5 6.2 %all-to-all-done.5 = bf16[4,256,384]{2,1,0:T(8,128)(2,1)S(1)} async-done(((bf16[4,256,384]{2,1,0:T(8,128)(2,1)}), bf16[4,256,384]{2,1,0:T(8,128)(2,1)S(1)}, u32[]{:S(2)}, u32[]{:S(2)}) %all-to-all-start.5) | async-done | bytes 786464 | tf_op jit(solution)/shard_map/gamma/all_to_all | solution.py:21
  217.8 0.8 reduce_sum.35
  218.6 9.9 %all-to-all-start.6 = ((bf16[16,16,384]{2,1,0:T(8,128)(2,1)}), bf16[16,16,384]{2,1,0:T(8,128)(2,1)S(1)}, u32[]{:S(2)}, u32[]{:S(2)}) async-start(bf16[16,16,384]{2,1,0:T(8,128)(2,1)} %bitcast.41), calls=%async_computation.6 | async-start | bytes 393216 | tf_op jit(solution)/shard_map/gamma/all_to_all | solution.py:21
  228.4 0.7 maximum_bitcast_fusion
  229.2 14.9 %all-to-all-done.6.value_ref = bf16[16,16,384]{2,1,0:T(8,128)(2,1)S(1)} async-done(((bf16[16,16,384]{2,1,0:T(8,128)(2,1)}), bf16[16,16,384]{2,1,0:T(8,128)(2,1)S(1)}, u32[]{:S(2)}, u32[]{:S(2)}) %all-to-all-start.6) | async-done | bytes 196640 | tf_op jit(solution)/shard_map/gamma/all_to_all | solution.py:21
  (43 shorter events, 5.0 us)
Async XLA Ops:
  7.2 155.1 %copy-start = (f32[2048]{0:T(1024)S(1)}, f32[2048]{0:T(1024)}, u32[]{:S(2)}) copy-start(f32[2048]{0:T(1024)} %param.10) | copy-start | bytes 24580
  7.2 17.6 %copy-start.2 = (bf16[64,3,640]{2,0,1:T(8,128)(2,1)S(1)}, bf16[64,3,640]{2,0,1:T(8,128)(2,1)}, u32[]{:S(2)}) copy-start(bf16[64,3,640]{2,0,1:T(8,128)(2,1)} %param.6) | copy-start | bytes 737284
  8.7 36.0 %all-to-all-start = ((bf16[16,16,640]{2,1,0:T(8,128)(2,1)}), bf16[16,16,640]{2,1,0:T(8,128)(2,1)S(1)}, u32[]{:S(2)}, u32[]{:S(2)}) async-start(bf16[16,16,640]{2,1,0:T(8,128)(2,1)} %broadcast_in_dim.29), calls=%async_computation | async-start | bytes 655360 | tf_op jit(solution)/shard_map/transform/all_to_all | solution.py:21
  23.9 120.8 %all-gather.2.cloned.1.call-start = ((), (), s32[]{:S(2)}) async-start(), calls=%async_computation.7 | async-start | bytes 3342336 | tf_op jit(solution)/shard_map/panels/all_gather | solution.py:209
  44.7 3.5 %collective-permute-start = (bf16[16,16,640]{2,1,0:T(8,128)(2,1)S(1)}, bf16[16,16,640]{2,1,0:T(8,128)(2,1)S(1)}, u32[]{:S(2)}, u32[]{:S(2)}) collective-permute-start(bf16[16,16,640]{2,1,0:T(8,128)(2,1)S(1)} %all-to-all-done), channel_id=1, source_target_pairs={{0,4},{4,0},{1,5},{5,1},{2,6},{6,2},{3,7},{7,3},{8,12},{12,8},{9,1... | collective-permute-start | bytes 983048 | tf_op jit(solution)/shard_map/transform/ppermute | solution.py:15
  77.7 24.4 %all-to-all-start.3 = ((bf16[16,16,384]{2,1,0:T(8,128)(2,1)}), bf16[16,16,384]{2,1,0:T(8,128)(2,1)S(1)}, u32[]{:S(2)}, u32[]{:S(2)}) async-start(bf16[16,16,384]{2,1,0:T(8,128)(2,1)} %pad_maximum_fusion.2), calls=%async_computation.3 | async-start | bytes 393216 | tf_op jit(solution)/shard_map/panels/all_to_all | solution.py:21
  149.4 6.6 %collective-permute-start.1 = (f32[4,3,64,384]{3,2,1,0:T(8,128)}, f32[4,3,64,384]{3,2,1,0:T(8,128)}, u32[]{:S(2)}, u32[]{:S(2)}) collective-permute-start(f32[4,3,64,384]{3,2,1,0:T(8,128)} %gram_half.3), channel_id=1, source_target_pairs={{0,4},{4,0},{1,5},{5,1},{2,6},{6,2},{3,7},{7,3},{8,12},{12,8},{9,1... | collective-permute-start | bytes 3538952 | tf_op jit(solution)/shard_map/gram/ppermute | solution.py:15
  158.6 3.9 %copy-start.3 = (f32[512]{0:T(512)S(1)}, f32[512]{0:T(512)}, u32[]{:S(2)}) copy-start(f32[512]{0:T(512)} %param.9) | copy-start | bytes 6148
  158.6 3.9 %copy-start.4 = (s32[3]{0:T(128)S(1)}, s32[3]{0:T(128)}, u32[]{:S(2)}) copy-start(s32[3]{0:T(128)} %param.11) | copy-start | bytes 40
  158.6 14.7 %all-to-all-start.4 = ((bf16[4,192,384]{2,1,0:T(8,128)(2,1)}), bf16[4,192,384]{2,1,0:T(8,128)(2,1)S(1)}, u32[]{:S(2)}, u32[]{:S(2)}) async-start(bf16[4,192,384]{2,1,0:T(8,128)(2,1)} %bitcast.35), calls=%async_computation.4 | async-start | bytes 1179648 | tf_op jit(solution)/shard_map/gram/all_to_all | solution.py:21
  174.0 17.5 %collective-permute-start.2 = (f32[3,3,32,128]{3,2,1,0:T(8,128)S(1)}, f32[3,3,32,128]{3,2,1,0:T(8,128)S(1)}, u32[]{:S(2)}, u32[]{:S(2)}) collective-permute-start(f32[3,3,32,128]{3,2,1,0:T(8,128)S(1)} %get-tuple-element.14), channel_id=1, source_target_pairs={{0,32},{4,96},{8,40},{12,104},{16,48},{20,112},{24,56},{28,120},{3... | collective-permute-start | bytes 442376 | tf_op jit(solution)/shard_map/amplitudes/ppermute | solution.py:234
  191.5 4.0 %copy-start.1 = (bf16[4,192,384]{2,1,0:T(8,128)(2,1)}, bf16[4,192,384]{2,1,0:T(8,128)(2,1)S(1)}, u32[]{:S(2)}) copy-start(bf16[4,192,384]{2,1,0:T(8,128)(2,1)S(1)} %all_gather.15) | copy-start | bytes 1769476
  191.5 4.0 %collective-permute-start.3 = (bf16[4,3,64,384]{3,2,1,0:T(8,128)(2,1)S(1)}, bf16[4,3,64,384]{3,2,1,0:T(8,128)(2,1)}, u32[]{:S(2)}, u32[]{:S(2)}) collective-permute-start(bf16[4,3,64,384]{3,2,1,0:T(8,128)(2,1)S(1)} %bitcast.73), channel_id=1, source_target_pairs={{0,4},{4,0},{1,5},{5,1},{2,6},{6,2},{3,7},{7,3},{8,12},{12,8},{9,1... | collective-permute-start | bytes 1769480 | tf_op jit(solution)/shard_map/amplitudes/ppermute | solution.py:15
  201.2 16.5 %all-to-all-start.5 = ((bf16[4,256,384]{2,1,0:T(8,128)(2,1)}), bf16[4,256,384]{2,1,0:T(8,128)(2,1)S(1)}, u32[]{:S(2)}, u32[]{:S(2)}) async-start(bf16[4,256,384]{2,1,0:T(8,128)(2,1)} %bitcast.72), calls=%async_computation.5 | async-start | bytes 1572864 | tf_op jit(solution)/shard_map/gamma/all_to_all | solution.py:21
  206.6 12.0 %collective-permute-start.4 = (f32[3,3,32,128]{3,2,1,0:T(8,128)S(1)}, f32[3,3,32,128]{3,2,1,0:T(8,128)S(1)}, u32[]{:S(2)}, u32[]{:S(2)}) collective-permute-start(f32[3,3,32,128]{3,2,1,0:T(8,128)S(1)} %get-tuple-element.17), channel_id=1, source_target_pairs={{0,32},{4,96},{8,40},{12,104},{16,48},{20,112},{24,56},{28,120},{3... | collective-permute-start | bytes 442376 | tf_op jit(solution)/shard_map/amplitudes/ppermute | solution.py:235
  218.6 25.4 %all-to-all-start.6 = ((bf16[16,16,384]{2,1,0:T(8,128)(2,1)}), bf16[16,16,384]{2,1,0:T(8,128)(2,1)S(1)}, u32[]{:S(2)}, u32[]{:S(2)}) async-start(bf16[16,16,384]{2,1,0:T(8,128)(2,1)} %bitcast.41), calls=%async_computation.6 | async-start | bytes 393216 | tf_op jit(solution)/shard_map/gamma/all_to_all | solution.py:21
Sparse Core Ops, SparseCore 0:
  67.1 77.5 all-gather.1

commit v5 on v3

--- a/solution.py
+++ b/solution.py
@@ -111,7 +111,7 @@
     share, narrow = row_energy.shape[0], col_energy.shape[1]
     ways = parts.shape[0]
 
-    def body(slot_ref, row_ref, col_ref, parts_ref, upper_ref, lower_ref, mixed_ref):
+    def body(slot_ref, row_ref, col_ref, parts_ref, amps_ref, mixed_ref):
         amps = {}
         for i in range(nocc):
             for j in range(nocc):
@@ -121,8 +121,7 @@
                     total = total + parts_ref[(k,) + at].astype(F32)
                 gap = slot_ref[i] + slot_ref[j] - row_ref[...] - col_ref[...]
                 amps[i, j] = total / gap
-                upper_ref[i, j] = amps[i, j][: share // 2]
-                lower_ref[i, j] = amps[i, j][share // 2 :]
+                amps_ref[i, j] = amps[i, j].astype(BF)
         for i in range(nocc):
             for j in range(nocc):
                 value = 2.0 * amps[i, j] - amps[j, i]
@@ -132,15 +131,36 @@
     return pl.pallas_call(
         body,
         out_shape=(
-            jax.ShapeDtypeStruct((nocc, nocc, share // 2, narrow), F32),
-            jax.ShapeDtypeStruct((nocc, nocc, share // 2, narrow), F32),
+            jax.ShapeDtypeStruct((nocc, nocc, share, narrow), BF),
             jax.ShapeDtypeStruct((nocc, share, nocc * narrow), BF),
         ),
         in_specs=[pl.BlockSpec(memory_space=pltpu.SMEM), vmem, vmem, vmem],
-        out_specs=(vmem, vmem, vmem),
+        out_specs=(vmem, vmem),
         compiler_params=pltpu.CompilerParams(vmem_limit_bytes=12 * 1024 * 1024),
         name="amplitudes_of",
     )(slot, row_energy, col_energy, parts)
+
+
+def place(value, nocc):
+    nz, r, lanes = value.shape
+    narrow = lanes // nocc
+    nl = nz // 2
+
+    def body(value_ref, out_ref):
+        for i in range(nocc):
+            for k in range(nz):
+                block = (k % nl + nl // 2) % nl * 2 + k // nl
+                out_ref[i, :, pl.ds(block * narrow, narrow)] = value_ref[k, :, pl.ds(i * narrow, narrow)]
+
+    vmem = pl.BlockSpec(memory_space=pltpu.VMEM)
+    return pl.pallas_call(
+        body,
+        out_shape=jax.ShapeDtypeStruct((nocc, r, nz * narrow), BF),
+        in_specs=[vmem],
+        out_specs=vmem,
+        compiler_params=pltpu.CompilerParams(vmem_limit_bytes=12 * 1024 * 1024),
+        name="place",
+    )(value)
 
 
 def local(half_ints, coef_virt, screen, occ_energy, virt_energy, batch_orbitals):
@@ -180,7 +200,7 @@
         row = jnp.concatenate([three[:, i] for i in range(nocc)], axis=-1)
         row = lax.all_gather(row.reshape(nx * r, nocc * wide), "z", axis=0, tiled=True)
         col = exchange(three.reshape(nx, nocc * r, wide), "x")
-        col = col.reshape(nx, nocc, r, ways // 2, 2, narrow)
+        col = jnp.roll(col, nx // 2, axis=0).reshape(nx, nocc, r, ways // 2, 2, narrow)
         col = jnp.concatenate(
             [col[:, i].transpose(3, 0, 2, 1, 4).reshape(nz, r, narrow) for i in range(nocc)], axis=-1
         )
@@ -196,17 +216,15 @@
 
     with jax.named_scope("amplitudes"):
         row_energy = lax.dynamic_slice_in_dim(virt_energy, x * wide + c * half + y * share, share, 0)
-        col_energy = lax.dynamic_slice_in_dim(virt_energy, (zl * 2 + zh) * narrow, narrow, 0)
-        upper, lower, mixed = amplitudes_of(gram, slot_energy, row_energy[:, None], col_energy[None, :])
+        col_energy = lax.dynamic_slice_in_dim(virt_energy, ((zl + nl // 2) % nl * 2 + zh) * narrow, narrow, 0)
+        amps, mixed = amplitudes_of(gram, slot_energy, row_energy[:, None], col_energy[None, :])
         swap = []
         for h in range(2):
             for l in range(nl):
                 for k in range(2):
-                    swap.append(((h * nl + l) * 2 + k, (k * nl + l) * 2 + h))
-        upper = lax.ppermute(upper, ("z", "c"), swap)
-        lower = lax.ppermute(lower, ("z", "c"), swap)
+                    swap.append(((h * nl + l) * 2 + k, (k * nl + (l + nl // 2) % nl) * 2 + h))
+        own = lax.ppermute(amps, ("z", "c"), swap)
         mixed = lax.all_gather(mixed.reshape(nocc * share, nocc * narrow), "y", axis=0)
-        mixed, upper = lax.optimization_barrier((mixed, upper))
         mixed = mixed.reshape(ny, nocc, share, nocc * narrow)
         theirs = swap_cores(mixed)
 
@@ -214,12 +232,10 @@
         value = contract(row, mixed, theirs, c, nx, nz)
         value = exchange(value.reshape(nx, nz * r, nocc * narrow), "x")
         value = jnp.sum(value.astype(F32), axis=0).astype(BF)
-        value, lower = lax.optimization_barrier((value, lower))
+        value, own = lax.optimization_barrier((value, own))
         value = exchange(value.reshape(nz, r, nocc * narrow), "z")
-        value = value.reshape(2, nl, r, nocc, narrow).transpose(2, 3, 1, 0, 4)
-        gamma = value.reshape(r, nocc, nv)
-    own = jnp.concatenate([upper, lower], axis=2)
-    return own.transpose(0, 2, 1, 3)[None], gamma
+        gamma = place(value, nocc)
+    return own.astype(F32).transpose(0, 2, 1, 3)[None], gamma.transpose(1, 0, 2)
 
 
 def solution(mesh):

time: 252 us -> 243 us (0.964)
  starting transfers between devices: 78.8 us -> 70.4 us
    ppermute x2 -> x1, starting transfers between devices: 16.5 us -> 5.19 us  [local(): own = lax.ppermute(amps, ('z', 'c'), swap)]
    ppermute x3, starting transfers between devices: 20.9 us -> 25.4 us  [swap_cores(): return lax.ppermute(value, 'c', [(0, 1), (1, 0)])]
  transfers between devices with their start and end apart: 11 -> 10, of which waited for: 10 -> 9; matrix products, arithmetic and copies ran while one was open for 2% -> 2% of each run, Pallas kernels for 1% -> 1%
where the time goes in v5:
time: 243 us; the launch traced here: 239 us
  waiting for transfers between devices  72.8 us (30%)
  starting transfers between devices  70.4 us (29%)
  blocking collectives  60 us (25%)
  between operations  14.4 us (6%)
  Pallas kernels  7.8 us (3%)
  local copies, waits for them, and re-layouts  7.38 us (3%)
  other arithmetic  5.12 us (2%)
    all_to_all x5, waiting for transfers between devices, exchange(): value = lax.all_to_all(value, axis, split_axis=0, concat_axis=0, tiled=True)  43.2 us
    all_to_all x5, starting transfers between devices, exchange(): value = lax.all_to_all(value, axis, split_axis=0, concat_axis=0, tiled=True)  39.8 us
    all_gather x1, waiting for transfers between devices, local(): lax.all_gather(row.reshape(nx * r, nocc * wide), 'z', axis=0, tiled=True)  26 us
    ppermute x3, starting transfers between devices, swap_cores(): return lax.ppermute(value, 'c', [(0, 1), (1, 0)])  25.4 us
    all_to_all x2, blocking collectives, exchange(): value = lax.all_to_all(value, axis, split_axis=0, concat_axis=0, tiled=True)  24.4 us
    all_gather x1, blocking collectives, local(): masked = lax.all_gather(masked.reshape(-1, ao_part), 'x', axis=0)  13.2 us
    all_gather x1, blocking collectives, local(): col = lax.all_gather(col.reshape(nz * r, nocc * narrow), 'x', axis=0)  11.6 us
    all_gather x1, blocking collectives, local(): lax.all_gather(mixed.reshape(nocc * share, nocc * narrow), 'y', axis=0)  10.7 us
  transfers between devices with their start and end apart: 10, of which 9 were waited for; matrix products, arithmetic and copies ran while one was open for 2% of the time, Pallas kernels for 1%

profile of v5, /device:TPU:1, one launch (start us, length us, event | category | flops | bytes accessed | tf_op | source)
XLA Modules:
  0.0 238.6 jit_solution(3795676920121992953)
XLA Ops:
  7.2 1.5 broadcast_in_dim.30
  8.7 15.7 %all-to-all-start = ((bf16[16,16,640]{2,1,0:T(8,128)(2,1)}), bf16[16,16,640]{2,1,0:T(8,128)(2,1)S(1)}, u32[]{:S(2)}, u32[]{:S(2)}) async-start(bf16[16,16,640]{2,1,0:T(8,128)(2,1)} %broadcast_in_dim.30), calls=%async_computation | async-start | bytes 655360 | tf_op jit(solution)/shard_map/transform/all_to_all | solution.py:20
  25.4 13.2 %all_gather.12 = bf16[4,192,640]{2,1,0:T(8,128)(2,1)S(1)} all-gather(bf16[1,192,640]{2,1,0:T(8,128)(2,1)S(1)} %bitcast.78), channel_id=1, replica_groups=mesh['x'=4,'z'=16,'c'=2,'y'=4] {'x'}, dimensions={0}, use_global_device_ids=true | all-gather | bytes 1228800 | tf_op jit(solution)/shard_map/transform/all_gather | solution.py:190
  38.7 1.0 all-to-all-done
  39.7 8.4 %collective-permute-start = (bf16[16,16,640]{2,1,0:T(8,128)(2,1)S(1)}, bf16[16,16,640]{2,1,0:T(8,128)(2,1)S(1)}, u32[]{:S(2)}, u32[]{:S(2)}) collective-permute-start(bf16[16,16,640]{2,1,0:T(8,128)(2,1)S(1)} %all-to-all-done), channel_id=1, source_target_pairs={{0,4},{4,0},{1,5},{5,1},{2,6},{6,2},{3,7},{7,3},{8,12},{12,8},{9,1... | collective-permute-start | bytes 983048 | tf_op jit(solution)/shard_map/transform/ppermute | solution.py:14
  48.1 1.2 collective-permute-done
  50.4 15.4 %all_to_all.57 = bf16[4,192,512]{2,1,0:T(8,128)(2,1)S(1)} all-to-all(bf16[4,192,512]{2,1,0:T(8,128)(2,1)S(1)} %bitcast.73), channel_id=1, replica_groups=mesh['x'=4,'z'=16,'c'=2,'y'=4] {'y'}, dimensions={0} | all-to-all | bytes 1572864 | tf_op jit(solution)/shard_map/transform/all_to_all | solution.py:20
  66.7 9.0 %all_to_all.58 = bf16[4,48,512]{2,1,0:T(8,128)(2,1)S(1)} all-to-all(bf16[4,48,512]{2,1,0:T(8,128)(2,1)S(1)} %bitcast.77), channel_id=1, replica_groups=mesh['x'=4,'z'=16,'c'=2,'y'=4] {'x'}, dimensions={0} | all-to-all | bytes 393216 | tf_op jit(solution)/shard_map/panels/all_to_all | solution.py:20
  76.8 6.7 %all-to-all-start.3 = ((bf16[16,16,384]{2,1,0:T(8,128)(2,1)}), bf16[16,16,384]{2,1,0:T(8,128)(2,1)S(1)}, u32[]{:S(2)}, u32[]{:S(2)}) async-start(bf16[16,16,384]{2,1,0:T(8,128)(2,1)} %pad_maximum_fusion.2), calls=%async_computation.3 | async-start | bytes 393216 | tf_op jit(solution)/shard_map/panels/all_to_all | solution.py:20
  83.5 14.6 %all-to-all-done.3 = bf16[16,16,384]{2,1,0:T(8,128)(2,1)S(1)} async-done(((bf16[16,16,384]{2,1,0:T(8,128)(2,1)}), bf16[16,16,384]{2,1,0:T(8,128)(2,1)S(1)}, u32[]{:S(2)}, u32[]{:S(2)}) %all-to-all-start.3) | async-done | bytes 196640 | tf_op jit(solution)/shard_map/panels/all_to_all | solution.py:20
  98.1 11.6 %all_gather.14 = bf16[4,256,384]{2,1,0:T(8,128)(2,1)S(1)} all-gather(bf16[1,256,384]{2,1,0:T(8,128)(2,1)S(1)} %bitcast.81), channel_id=1, replica_groups=mesh['x'=4,'z'=16,'c'=2,'y'=4] {'x'}, dimensions={0}, use_global_device_ids=true | all-gather | bytes 983040 | tf_op jit(solution)/shard_map/panels/all_gather | solution.py:208
  109.8 1.0 copy.36
  110.8 26.0 %all-gather.2.cloned.1.call-done.row_ref = bf16[1024,1536]{1,0:T(8,128)(2,1)} async-done(((bf16[64,1536]{1,0:T(8,128)(2,1)}), bf16[1024,1536]{1,0:T(8,128)(2,1)}) %all-gather.2.cloned.1.call-update) | async-done | bytes 3145744 | tf_op jit(solution)/shard_map/panels/all_gather | solution.py:201
  136.8 1.9 copy-done.1
  138.6 1.1 copy-done.3
  139.8 1.7 gram_half.3
  141.5 10.9 %collective-permute-start.1 = (f32[4,3,64,384]{3,2,1,0:T(8,128)S(1)}, f32[4,3,64,384]{3,2,1,0:T(8,128)S(1)}, u32[]{:S(2)}, u32[]{:S(2)}) collective-permute-start(f32[4,3,64,384]{3,2,1,0:T(8,128)S(1)} %gram_half.3), channel_id=1, source_target_pairs={{0,4},{4,0},{1,5},{5,1},{2,6},{6,2},{3,7},{7,3},{8,12},{12,8},{9,1... | collective-permute-start | bytes 3538952 | tf_op jit(solution)/shard_map/gram/ppermute | solution.py:14
  152.4 1.7 gram_half.2
  154.8 1.0 add_convert_fusion
  155.8 4.3 %all-to-all-start.4 = ((bf16[4,192,384]{2,1,0:T(8,128)(2,1)}), bf16[4,192,384]{2,1,0:T(8,128)(2,1)}, u32[]{:S(2)}, u32[]{:S(2)}) async-start(bf16[4,192,384]{2,1,0:T(8,128)(2,1)} %bitcast.75), calls=%async_computation.4 | async-start | bytes 1179648 | tf_op jit(solution)/shard_map/gram/all_to_all | solution.py:20
  160.6 9.5 %all-to-all-done.4.parts_ref = bf16[4,192,384]{2,1,0:T(8,128)(2,1)} async-done(((bf16[4,192,384]{2,1,0:T(8,128)(2,1)}), bf16[4,192,384]{2,1,0:T(8,128)(2,1)}, u32[]{:S(2)}, u32[]{:S(2)}) %all-to-all-start.4) | async-done | bytes 589856 | tf_op jit(solution)/shard_map/gram/all_to_all | solution.py:20
  170.1 1.2 amplitudes_of.1
  171.3 10.7 %all_gather.15 = bf16[4,192,384]{2,1,0:T(8,128)(2,1)S(1)} all-gather(bf16[1,192,384]{2,1,0:T(8,128)(2,1)S(1)} %bitcast.72), channel_id=1, replica_groups=mesh['x'=4,'z'=16,'c'=2,'y'=4] {'y'}, dimensions={0}, use_global_device_ids=true | all-gather | bytes 737280 | tf_op jit(solution)/shard_map/amplitudes/all_gather | solution.py:227
  182.1 6.1 %collective-permute-start.2 = (bf16[4,3,64,384]{3,2,1,0:T(8,128)(2,1)S(1)}, bf16[4,3,64,384]{3,2,1,0:T(8,128)(2,1)S(1)}, u32[]{:S(2)}, u32[]{:S(2)}) collective-permute-start(bf16[4,3,64,384]{3,2,1,0:T(8,128)(2,1)S(1)} %bitcast.70), channel_id=1, source_target_pairs={{0,4},{4,0},{1,5},{5,1},{2,6},{6,2},{3,7},{7,3},{8,12},{12,8},{9,1... | collective-permute-start | bytes 1769480 | tf_op jit(solution)/shard_map/amplitudes/ppermute | solution.py:14
  188.1 1.6 collective-permute-done.2.theirs_ref
  189.7 2.5 %contract.1 = bf16[4,16,16,384]{3,2,1,0:T(8,128)(2,1)S(1)} custom-call(s32[1]{0:T(128)} %bitcast.which_ref.core_ref, bf16[1024,1536]{1,0:T(8,128)(2,1)S(1)} %copy-done.2, bf16[4,3,64,384]{3,2,1,0:T(8,128)(2,1)S(1)} %bitcast.71, bf16[4,3,64,384]{3,2,1,0:T(8,128)(2,1)S(1)} %collective-permute-done.2.theirs_ref), custom_call_target="tpu_custom_call" | custom-call | flops 1207959552 | bytes 5111808 | tf_op jit(solution)/shard_map/gamma/contract/pallas_call | solution.py:85
  192.3 0.9 copy-done.4
  193.1 4.0 %all-to-all-start.5 = ((bf16[4,256,384]{2,1,0:T(8,128)(2,1)}), bf16[4,256,384]{2,1,0:T(8,128)(2,1)S(1)}, u32[]{:S(2)}, u32[]{:S(2)}) async-start(bf16[4,256,384]{2,1,0:T(8,128)(2,1)} %bitcast.69), calls=%async_computation.5 | async-start | bytes 1572864 | tf_op jit(solution)/shard_map/gamma/all_to_all | solution.py:20
  197.1 5.2 %collective-permute-start.3 = (bf16[3,3,64,128]{3,2,1,0:T(8,128)(2,1)S(1)}, bf16[3,3,64,128]{3,2,1,0:T(8,128)(2,1)S(1)}, u32[]{:S(2)}, u32[]{:S(2)}) collective-permute-start(bf16[3,3,64,128]{3,2,1,0:T(8,128)(2,1)S(1)} %get-tuple-element.11), channel_id=1, source_target_pairs={{0,32},{4,96},{8,40},{12,104},{16,48},{20,112},{24,56},{28,120},{3... | collective-permute-start | bytes 442376 | tf_op jit(solution)/shard_map/amplitudes/ppermute | solution.py:226
  202.3 6.5 %all-to-all-done.5 = bf16[4,256,384]{2,1,0:T(8,128)(2,1)S(1)} async-done(((bf16[4,256,384]{2,1,0:T(8,128)(2,1)}), bf16[4,256,384]{2,1,0:T(8,128)(2,1)S(1)}, u32[]{:S(2)}, u32[]{:S(2)}) %all-to-all-start.5) | async-done | bytes 786464 | tf_op jit(solution)/shard_map/gamma/all_to_all | solution.py:20
  209.7 9.0 %all-to-all-start.6 = ((bf16[16,16,384]{2,1,0:T(8,128)(2,1)}), bf16[16,16,384]{2,1,0:T(8,128)(2,1)S(1)}, u32[]{:S(2)}, u32[]{:S(2)}) async-start(bf16[16,16,384]{2,1,0:T(8,128)(2,1)} %bitcast.41), calls=%async_computation.6 | async-start | bytes 393216 | tf_op jit(solution)/shard_map/gamma/all_to_all | solution.py:20
  219.4 11.6 %all-to-all-done.6.value_ref = bf16[16,16,384]{2,1,0:T(8,128)(2,1)S(1)} async-done(((bf16[16,16,384]{2,1,0:T(8,128)(2,1)}), bf16[16,16,384]{2,1,0:T(8,128)(2,1)S(1)}, u32[]{:S(2)}, u32[]{:S(2)}) %all-to-all-start.6) | async-done | bytes 196640 | tf_op jit(solution)/shard_map/gamma/all_to_all | solution.py:20
  (47 shorter events, 7.4 us)
Async XLA Ops:
  7.2 153.0 %copy-start = (f32[2048]{0:T(1024)S(1)}, f32[2048]{0:T(1024)}, u32[]{:S(2)}) copy-start(f32[2048]{0:T(1024)} %param.10) | copy-start | bytes 24580
  7.2 18.2 %copy-start.5 = (bf16[64,3,640]{2,0,1:T(8,128)(2,1)S(1)}, bf16[64,3,640]{2,0,1:T(8,128)(2,1)}, u32[]{:S(2)}) copy-start(bf16[64,3,640]{2,0,1:T(8,128)(2,1)} %param.6) | copy-start | bytes 737284
  8.7 31.0 %all-to-all-start = ((bf16[16,16,640]{2,1,0:T(8,128)(2,1)}), bf16[16,16,640]{2,1,0:T(8,128)(2,1)S(1)}, u32[]{:S(2)}, u32[]{:S(2)}) async-start(bf16[16,16,640]{2,1,0:T(8,128)(2,1)} %broadcast_in_dim.30), calls=%async_computation | async-start | bytes 655360 | tf_op jit(solution)/shard_map/transform/all_to_all | solution.py:20
  24.5 112.3 %all-gather.2.cloned.1.call-start = ((), (), s32[]{:S(2)}) async-start(), calls=%async_computation.7 | async-start | bytes 3342336 | tf_op jit(solution)/shard_map/panels/all_gather | solution.py:201
  39.7 9.6 %collective-permute-start = (bf16[16,16,640]{2,1,0:T(8,128)(2,1)S(1)}, bf16[16,16,640]{2,1,0:T(8,128)(2,1)S(1)}, u32[]{:S(2)}, u32[]{:S(2)}) collective-permute-start(bf16[16,16,640]{2,1,0:T(8,128)(2,1)S(1)} %all-to-all-done), channel_id=1, source_target_pairs={{0,4},{4,0},{1,5},{5,1},{2,6},{6,2},{3,7},{7,3},{8,12},{12,8},{9,1... | collective-permute-start | bytes 983048 | tf_op jit(solution)/shard_map/transform/ppermute | solution.py:14
  76.8 21.3 %all-to-all-start.3 = ((bf16[16,16,384]{2,1,0:T(8,128)(2,1)}), bf16[16,16,384]{2,1,0:T(8,128)(2,1)S(1)}, u32[]{:S(2)}, u32[]{:S(2)}) async-start(bf16[16,16,384]{2,1,0:T(8,128)(2,1)} %pad_maximum_fusion.2), calls=%async_computation.3 | async-start | bytes 393216 | tf_op jit(solution)/shard_map/panels/all_to_all | solution.py:20
  136.7 1.9 copy-start.1
  138.6 1.1 copy-start.3
  139.8 12.6 %copy-start.2 = (bf16[1024,1536]{1,0:T(8,128)(2,1)S(1)}, bf16[1024,1536]{1,0:T(8,128)(2,1)}, u32[]{:S(2)}) copy-start(bf16[1024,1536]{1,0:T(8,128)(2,1)} %all-gather.2.cloned.1.call-done.row_ref) | copy-start | bytes 9437188
  141.5 13.4 %collective-permute-start.1 = (f32[4,3,64,384]{3,2,1,0:T(8,128)S(1)}, f32[4,3,64,384]{3,2,1,0:T(8,128)S(1)}, u32[]{:S(2)}, u32[]{:S(2)}) collective-permute-start(f32[4,3,64,384]{3,2,1,0:T(8,128)S(1)} %gram_half.3), channel_id=1, source_target_pairs={{0,4},{4,0},{1,5},{5,1},{2,6},{6,2},{3,7},{7,3},{8,12},{12,8},{9,1... | collective-permute-start | bytes 3538952 | tf_op jit(solution)/shard_map/gram/ppermute | solution.py:14
  155.8 4.6 %copy-start.6 = (f32[512]{0:T(512)S(1)}, f32[512]{0:T(512)}, u32[]{:S(2)}) copy-start(f32[512]{0:T(512)} %param.9) | copy-start | bytes 6148
  155.8 4.6 %copy-start.7 = (s32[3]{0:T(128)S(1)}, s32[3]{0:T(128)}, u32[]{:S(2)}) copy-start(s32[3]{0:T(128)} %param.11) | copy-start | bytes 40
  155.8 14.3 %all-to-all-start.4 = ((bf16[4,192,384]{2,1,0:T(8,128)(2,1)}), bf16[4,192,384]{2,1,0:T(8,128)(2,1)}, u32[]{:S(2)}, u32[]{:S(2)}) async-start(bf16[4,192,384]{2,1,0:T(8,128)(2,1)} %bitcast.75), calls=%async_computation.4 | async-start | bytes 1179648 | tf_op jit(solution)/shard_map/gram/all_to_all | solution.py:20
  182.1 7.7 %collective-permute-start.2 = (bf16[4,3,64,384]{3,2,1,0:T(8,128)(2,1)S(1)}, bf16[4,3,64,384]{3,2,1,0:T(8,128)(2,1)S(1)}, u32[]{:S(2)}, u32[]{:S(2)}) collective-permute-start(bf16[4,3,64,384]{3,2,1,0:T(8,128)(2,1)S(1)} %bitcast.70), channel_id=1, source_target_pairs={{0,4},{4,0},{1,5},{5,1},{2,6},{6,2},{3,7},{7,3},{8,12},{12,8},{9,1... | collective-permute-start | bytes 1769480 | tf_op jit(solution)/shard_map/amplitudes/ppermute | solution.py:14
  192.3 0.9 copy-start.4
  193.1 15.7 %all-to-all-start.5 = ((bf16[4,256,384]{2,1,0:T(8,128)(2,1)}), bf16[4,256,384]{2,1,0:T(8,128)(2,1)S(1)}, u32[]{:S(2)}, u32[]{:S(2)}) async-start(bf16[4,256,384]{2,1,0:T(8,128)(2,1)} %bitcast.69), calls=%async_computation.5 | async-start | bytes 1572864 | tf_op jit(solution)/shard_map/gamma/all_to_all | solution.py:20
  197.1 12.5 %collective-permute-start.3 = (bf16[3,3,64,128]{3,2,1,0:T(8,128)(2,1)S(1)}, bf16[3,3,64,128]{3,2,1,0:T(8,128)(2,1)S(1)}, u32[]{:S(2)}, u32[]{:S(2)}) collective-permute-start(bf16[3,3,64,128]{3,2,1,0:T(8,128)(2,1)S(1)} %get-tuple-element.11), channel_id=1, source_target_pairs={{0,32},{4,96},{8,40},{12,104},{16,48},{20,112},{24,56},{28,120},{3... | collective-permute-start | bytes 442376 | tf_op jit(solution)/shard_map/amplitudes/ppermute | solution.py:226
  209.7 21.4 %all-to-all-start.6 = ((bf16[16,16,384]{2,1,0:T(8,128)(2,1)}), bf16[16,16,384]{2,1,0:T(8,128)(2,1)S(1)}, u32[]{:S(2)}, u32[]{:S(2)}) async-start(bf16[16,16,384]{2,1,0:T(8,128)(2,1)} %bitcast.41), calls=%async_computation.6 | async-start | bytes 393216 | tf_op jit(solution)/shard_map/gamma/all_to_all | solution.py:20
Sparse Core Ops, SparseCore 0:
  66.8 69.9 all-gather.1

commit v6 on v5

--- a/solution.py
+++ b/solution.py
@@ -25,15 +25,21 @@
     return jnp.where(core == 0, mine, theirs), jnp.where(core == 0, theirs, mine)
 
 
-def gram_half(row, col, which, nocc, ny):
+def gram_half(row, col, which, nocc, ny, room):
     k_rows, lanes = row.shape
     half = lanes // nocc // 2
     share = half // ny
-    width = col.shape[1]
-
-    def body(which_ref, row_ref, col_ref, out_ref):
+    nx, nz, r, width = col.shape
+
+    def body(which_ref, row_ref, col_ref, out_ref, order_ref):
+        @pl.when(pl.program_id(0) == 0)
+        def _():
+            for k in range(nz):
+                for m in range(nx):
+                    order_ref[(k * nx + m) * r : (k * nx + m + 1) * r, :] = col_ref[m, k]
+
         tile = lax.dot_general(
-            row_ref[...], col_ref[...], (((0,), (0,)), ((), ())), preferred_element_type=F32
+            row_ref[...], order_ref[...], (((0,), (0,)), ((), ())), preferred_element_type=F32
         )
         out_ref[...] = tile.reshape(ny, 1, share, width)
 
@@ -45,11 +51,12 @@
             grid=(nocc,),
             in_specs=[
                 pl.BlockSpec((k_rows, half), lambda i, w: (0, 2 * i + w[0])),
-                pl.BlockSpec((k_rows, width), lambda i, w: (0, 0)),
+                pl.BlockSpec((nx, nz, r, width), lambda i, w: (0, 0, 0, 0)),
             ],
             out_specs=pl.BlockSpec((ny, 1, share, width), lambda i, w: (0, i, 0, 0)),
-        ),
-        compiler_params=pltpu.CompilerParams(vmem_limit_bytes=12 * 1024 * 1024),
+            scratch_shapes=[pltpu.VMEM((k_rows, width), BF)],
+        ),
+        compiler_params=pltpu.CompilerParams(vmem_limit_bytes=room * 1024 * 1024),
         cost_estimate=pl.CostEstimate(
             flops=2 * k_rows * nocc * half * width,
             bytes_accessed=2 * k_rows * (nocc * half + width) + 4 * nocc * half * width,
@@ -207,11 +214,10 @@
         col = exchange(col, "z")
         col = lax.all_gather(col.reshape(nz * r, nocc * narrow), "x", axis=0)
         col = col.reshape(nx, nz, r, nocc * narrow)
-        col = col.transpose(1, 0, 2, 3).reshape(nz * nx * r, nocc * narrow)
 
     with jax.named_scope("gram"):
-        other = swap_cores(gram_half(row, col, 1 - c, nocc, ny))
-        gram = gram_half(row, col, c, nocc, ny) + other
+        other = swap_cores(gram_half(row, col, 1 - c, nocc, ny, 58))
+        gram = gram_half(row, col, c, nocc, ny, 12) + other
         gram = exchange(gram.astype(BF).reshape(ny, nocc * share, nocc * narrow), "y")
 
     with jax.named_scope("amplitudes"):

time: 243 us -> 244 us (level)
  the two profiles are of different devices: /device:TPU:1 before, /device:TPU:2 now
where the time goes in v6:
time: 244 us; the launch traced here: 243 us
  waiting for transfers between devices  89.2 us (37%)
  blocking collectives  68.9 us (28%)
  starting transfers between devices  50.4 us (21%)
  between operations  14.4 us (6%)
  Pallas kernels  10.6 us (4%)
  other arithmetic  5.15 us (2%)
  local copies, waits for them, and re-layouts  3.36 us (1%)
    all_to_all x5, waiting for transfers between devices, exchange(): value = lax.all_to_all(value, axis, split_axis=0, concat_axis=0, tiled=True)  54.2 us
    all_to_all x5, starting transfers between devices, exchange(): value = lax.all_to_all(value, axis, split_axis=0, concat_axis=0, tiled=True)  39.9 us
    all_gather x1, waiting for transfers between devices, local(): lax.all_gather(row.reshape(nx * r, nocc * wide), 'z', axis=0, tiled=True)  28.4 us
    all_to_all x2, blocking collectives, exchange(): value = lax.all_to_all(value, axis, split_axis=0, concat_axis=0, tiled=True)  26.4 us
    all_gather x1, blocking collectives, local(): masked = lax.all_gather(masked.reshape(-1, ao_part), 'x', axis=0)  15.1 us
    all_gather x1, blocking collectives, local(): col = lax.all_gather(col.reshape(nz * r, nocc * narrow), 'x', axis=0)  13.9 us
    all_gather x1, blocking collectives, local(): lax.all_gather(mixed.reshape(nocc * share, nocc * narrow), 'y', axis=0)  13.6 us
    pallas_call x2, Pallas kernels, gram_half(): pl.pallas_call(body, out_shape=jax.ShapeDtypeStruct((ny, nocc, share, wid...  6.17 us
  transfers between devices with their start and end apart: 10, of which 10 were waited for; matrix products, arithmetic and copies ran while one was open for 2% of the time, Pallas kernels for 1%

profile of v6, /device:TPU:2, one launch (start us, length us, event | category | flops | bytes accessed | tf_op | source)
XLA Modules:
  0.0 242.8 jit_solution(3536067991176216632)
XLA Ops:
  7.2 1.5 broadcast_in_dim.30
  8.7 15.2 %all-to-all-start = ((bf16[16,16,640]{2,1,0:T(8,128)(2,1)}), bf16[16,16,640]{2,1,0:T(8,128)(2,1)S(1)}, u32[]{:S(2)}, u32[]{:S(2)}) async-start(bf16[16,16,640]{2,1,0:T(8,128)(2,1)} %broadcast_in_dim.30), calls=%async_computation | async-start | bytes 655360 | tf_op jit(solution)/shard_map/transform/all_to_all | solution.py:20
  24.9 15.1 %all_gather.12 = bf16[4,192,640]{2,1,0:T(8,128)(2,1)S(1)} all-gather(bf16[1,192,640]{2,1,0:T(8,128)(2,1)S(1)} %bitcast.74), channel_id=1, replica_groups=mesh['x'=4,'z'=16,'c'=2,'y'=4] {'x'}, dimensions={0}, use_global_device_ids=true | all-gather | bytes 1228800 | tf_op jit(solution)/shard_map/transform/all_gather | solution.py:197
  40.0 4.7 %all-to-all-done = bf16[16,16,640]{2,1,0:T(8,128)(2,1)S(1)} async-done(((bf16[16,16,640]{2,1,0:T(8,128)(2,1)}), bf16[16,16,640]{2,1,0:T(8,128)(2,1)S(1)}, u32[]{:S(2)}, u32[]{:S(2)}) %all-to-all-start) | async-done | bytes 327712 | tf_op jit(solution)/shard_map/transform/all_to_all | solution.py:20
  44.7 1.9 collective-permute-start
  46.6 1.6 collective-permute-done
  49.2 16.9 %all_to_all.57 = bf16[4,192,512]{2,1,0:T(8,128)(2,1)S(1)} all-to-all(bf16[4,192,512]{2,1,0:T(8,128)(2,1)S(1)} %bitcast.70), channel_id=1, replica_groups=mesh['x'=4,'z'=16,'c'=2,'y'=4] {'y'}, dimensions={0} | all-to-all | bytes 1572864 | tf_op jit(solution)/shard_map/transform/all_to_all | solution.py:20
  67.0 9.5 %all_to_all.58 = bf16[4,48,512]{2,1,0:T(8,128)(2,1)S(1)} all-to-all(bf16[4,48,512]{2,1,0:T(8,128)(2,1)S(1)} %bitcast.73), channel_id=1, replica_groups=mesh['x'=4,'z'=16,'c'=2,'y'=4] {'x'}, dimensions={0} | all-to-all | bytes 393216 | tf_op jit(solution)/shard_map/panels/all_to_all | solution.py:20
  77.7 7.0 %all-to-all-start.3 = ((bf16[16,16,384]{2,1,0:T(8,128)(2,1)}), bf16[16,16,384]{2,1,0:T(8,128)(2,1)S(1)}, u32[]{:S(2)}, u32[]{:S(2)}) async-start(bf16[16,16,384]{2,1,0:T(8,128)(2,1)} %pad_maximum_fusion.2), calls=%async_computation.3 | async-start | bytes 393216 | tf_op jit(solution)/shard_map/panels/all_to_all | solution.py:20
  84.6 17.4 %all-to-all-done.3 = bf16[16,16,384]{2,1,0:T(8,128)(2,1)S(1)} async-done(((bf16[16,16,384]{2,1,0:T(8,128)(2,1)}), bf16[16,16,384]{2,1,0:T(8,128)(2,1)S(1)}, u32[]{:S(2)}, u32[]{:S(2)}) %all-to-all-start.3) | async-done | bytes 196640 | tf_op jit(solution)/shard_map/panels/all_to_all | solution.py:20
  102.0 13.9 %all_gather.14 = bf16[4,256,384]{2,1,0:T(8,128)(2,1)} all-gather(bf16[1,256,384]{2,1,0:T(8,128)(2,1)S(1)} %bitcast.77), channel_id=1, replica_groups=mesh['x'=4,'z'=16,'c'=2,'y'=4] {'x'}, dimensions={0}, use_global_device_ids=true | all-gather | bytes 983040 | tf_op jit(solution)/shard_map/panels/all_gather | solution.py:215
  115.9 28.4 %all-gather.2.cloned.1.call-done.row_ref = bf16[1024,1536]{1,0:T(8,128)(2,1)} async-done(((bf16[64,1536]{1,0:T(8,128)(2,1)}), bf16[1024,1536]{1,0:T(8,128)(2,1)}) %all-gather.2.cloned.1.call-update) | async-done | bytes 3145744 | tf_op jit(solution)/shard_map/panels/all_gather | solution.py:208
  144.3 4.4 %gram_half.3 = f32[4,3,64,384]{3,2,1,0:T(8,128)} custom-call(s32[1]{0:T(128)} %bitcast.32.which_ref, bf16[1024,1536]{1,0:T(8,128)(2,1)} %all-gather.2.cloned.1.call-done.row_ref, bf16[4,16,16,384]{3,2,1,0:T(8,128)(2,1)} %bitcast.64), custom_call_target="tpu_custom_call" | custom-call | flops 603979776 | bytes 3538944 | tf_op jit(solution)/shard_map/gram/gram_half/pallas_call | solution.py:46
  148.8 1.9 collective-permute-start.1
  150.7 1.7 gram_half.2
  152.4 1.3 collective-permute-done.1
  153.7 1.0 add_convert_fusion
  154.7 4.3 %all-to-all-start.4 = ((bf16[4,192,384]{2,1,0:T(8,128)(2,1)}), bf16[4,192,384]{2,1,0:T(8,128)(2,1)}, u32[]{:S(2)}, u32[]{:S(2)}) async-start(bf16[4,192,384]{2,1,0:T(8,128)(2,1)} %bitcast.71), calls=%async_computation.4 | async-start | bytes 1179648 | tf_op jit(solution)/shard_map/gram/all_to_all | solution.py:20
  159.5 10.3 %all-to-all-done.4.parts_ref = bf16[4,192,384]{2,1,0:T(8,128)(2,1)} async-done(((bf16[4,192,384]{2,1,0:T(8,128)(2,1)}), bf16[4,192,384]{2,1,0:T(8,128)(2,1)}, u32[]{:S(2)}, u32[]{:S(2)}) %all-to-all-start.4) | async-done | bytes 589856 | tf_op jit(solution)/shard_map/gram/all_to_all | solution.py:20
  169.8 1.2 amplitudes_of.1
  171.1 13.6 %all_gather.15 = bf16[4,192,384]{2,1,0:T(8,128)(2,1)S(1)} all-gather(bf16[1,192,384]{2,1,0:T(8,128)(2,1)S(1)} %bitcast.69), channel_id=1, replica_groups=mesh['x'=4,'z'=16,'c'=2,'y'=4] {'y'}, dimensions={0}, use_global_device_ids=true | all-gather | bytes 737280 | tf_op jit(solution)/shard_map/amplitudes/all_gather | solution.py:233
  184.7 1.9 collective-permute-start.2
  186.6 2.0 collective-permute-done.2.theirs_ref
  188.5 2.5 %contract.1 = bf16[4,16,16,384]{3,2,1,0:T(8,128)(2,1)S(1)} custom-call(s32[1]{0:T(128)} %bitcast.which_ref.core_ref, bf16[1024,1536]{1,0:T(8,128)(2,1)S(1)} %copy-done.1, bf16[4,3,64,384]{3,2,1,0:T(8,128)(2,1)S(1)} %bitcast.68, bf16[4,3,64,384]{3,2,1,0:T(8,128)(2,1)S(1)} %collective-permute-done.2.theirs_ref), custom_call_target="tpu_custom_call" | custom-call | flops 1207959552 | bytes 5111808 | tf_op jit(solution)/shard_map/gamma/contract/pallas_call | solution.py:92
  191.1 0.9 copy-done.3
  191.9 4.9 %all-to-all-start.5 = ((bf16[4,256,384]{2,1,0:T(8,128)(2,1)}), bf16[4,256,384]{2,1,0:T(8,128)(2,1)S(1)}, u32[]{:S(2)}, u32[]{:S(2)}) async-start(bf16[4,256,384]{2,1,0:T(8,128)(2,1)} %bitcast.66), calls=%async_computation.5 | async-start | bytes 1572864 | tf_op jit(solution)/shard_map/gamma/all_to_all | solution.py:20
  196.8 4.7 %collective-permute-start.3 = (bf16[3,3,64,128]{3,2,1,0:T(8,128)(2,1)S(1)}, bf16[3,3,64,128]{3,2,1,0:T(8,128)(2,1)S(1)}, u32[]{:S(2)}, u32[]{:S(2)}) collective-permute-start(bf16[3,3,64,128]{3,2,1,0:T(8,128)(2,1)S(1)} %get-tuple-element.11), channel_id=1, source_target_pairs={{0,32},{4,96},{8,40},{12,104},{16,48},{20,112},{24,56},{28,120},{3... | collective-permute-start | bytes 442376 | tf_op jit(solution)/shard_map/amplitudes/ppermute | solution.py:232
  201.5 6.5 %all-to-all-done.5 = bf16[4,256,384]{2,1,0:T(8,128)(2,1)S(1)} async-done(((bf16[4,256,384]{2,1,0:T(8,128)(2,1)}), bf16[4,256,384]{2,1,0:T(8,128)(2,1)S(1)}, u32[]{:S(2)}, u32[]{:S(2)}) %all-to-all-start.5) | async-done | bytes 786464 | tf_op jit(solution)/shard_map/gamma/all_to_all | solution.py:20
  208.0 0.8 reduce_sum.35
  208.8 1.8 collective-permute-done.3
  210.6 8.6 %all-to-all-start.6 = ((bf16[16,16,384]{2,1,0:T(8,128)(2,1)}), bf16[16,16,384]{2,1,0:T(8,128)(2,1)S(1)}, u32[]{:S(2)}, u32[]{:S(2)}) async-start(bf16[16,16,384]{2,1,0:T(8,128)(2,1)} %bitcast.39), calls=%async_computation.6 | async-start | bytes 393216 | tf_op jit(solution)/shard_map/gamma/all_to_all | solution.py:20
  219.9 15.3 %all-to-all-done.6.value_ref = bf16[16,16,384]{2,1,0:T(8,128)(2,1)S(1)} async-done(((bf16[16,16,384]{2,1,0:T(8,128)(2,1)}), bf16[16,16,384]{2,1,0:T(8,128)(2,1)S(1)}, u32[]{:S(2)}, u32[]{:S(2)}) %all-to-all-start.6) | async-done | bytes 196640 | tf_op jit(solution)/shard_map/gamma/all_to_all | solution.py:20
  (44 shorter events, 5.8 us)
Async XLA Ops:
  7.2 151.9 %copy-start = (f32[2048]{0:T(1024)S(1)}, f32[2048]{0:T(1024)}, u32[]{:S(2)}) copy-start(f32[2048]{0:T(1024)} %param.10) | copy-start | bytes 24580
  7.2 17.6 %copy-start.4 = (bf16[64,3,640]{2,0,1:T(8,128)(2,1)S(1)}, bf16[64,3,640]{2,0,1:T(8,128)(2,1)}, u32[]{:S(2)}) copy-start(bf16[64,3,640]{2,0,1:T(8,128)(2,1)} %param.6) | copy-start | bytes 737284
  8.7 36.0 %all-to-all-start = ((bf16[16,16,640]{2,1,0:T(8,128)(2,1)}), bf16[16,16,640]{2,1,0:T(8,128)(2,1)S(1)}, u32[]{:S(2)}, u32[]{:S(2)}) async-start(bf16[16,16,640]{2,1,0:T(8,128)(2,1)} %broadcast_in_dim.30), calls=%async_computation | async-start | bytes 655360 | tf_op jit(solution)/shard_map/transform/all_to_all | solution.py:20
  23.9 120.4 %all-gather.2.cloned.1.call-start = ((), (), s32[]{:S(2)}) async-start(), calls=%async_computation.7 | async-start | bytes 3342336 | tf_op jit(solution)/shard_map/panels/all_gather | solution.py:208
  44.7 3.5 %collective-permute-start = (bf16[16,16,640]{2,1,0:T(8,128)(2,1)S(1)}, bf16[16,16,640]{2,1,0:T(8,128)(2,1)S(1)}, u32[]{:S(2)}, u32[]{:S(2)}) collective-permute-start(bf16[16,16,640]{2,1,0:T(8,128)(2,1)S(1)} %all-to-all-done), channel_id=1, source_target_pairs={{0,4},{4,0},{1,5},{5,1},{2,6},{6,2},{3,7},{7,3},{8,12},{12,8},{9,1... | collective-permute-start | bytes 983048 | tf_op jit(solution)/shard_map/transform/ppermute | solution.py:14
  77.7 24.4 %all-to-all-start.3 = ((bf16[16,16,384]{2,1,0:T(8,128)(2,1)}), bf16[16,16,384]{2,1,0:T(8,128)(2,1)S(1)}, u32[]{:S(2)}, u32[]{:S(2)}) async-start(bf16[16,16,384]{2,1,0:T(8,128)(2,1)} %pad_maximum_fusion.2), calls=%async_computation.3 | async-start | bytes 393216 | tf_op jit(solution)/shard_map/panels/all_to_all | solution.py:20
  144.3 6.4 %copy-start.1 = (bf16[1024,1536]{1,0:T(8,128)(2,1)S(1)}, bf16[1024,1536]{1,0:T(8,128)(2,1)}, u32[]{:S(2)}) copy-start(bf16[1024,1536]{1,0:T(8,128)(2,1)} %all-gather.2.cloned.1.call-done.row_ref) | copy-start | bytes 9437188
  144.3 6.4 %copy-start.2 = (bf16[4,256,384]{2,1,0:T(8,128)(2,1)S(1)}, bf16[4,256,384]{2,1,0:T(8,128)(2,1)}, u32[]{:S(2)}) copy-start(bf16[4,256,384]{2,1,0:T(8,128)(2,1)} %all_gather.14) | copy-start | bytes 2359300
  148.8 4.9 %collective-permute-start.1 = (f32[4,3,64,384]{3,2,1,0:T(8,128)}, f32[4,3,64,384]{3,2,1,0:T(8,128)S(1)}, u32[]{:S(2)}, u32[]{:S(2)}) collective-permute-start(f32[4,3,64,384]{3,2,1,0:T(8,128)} %gram_half.3), channel_id=1, source_target_pairs={{0,4},{4,0},{1,5},{5,1},{2,6},{6,2},{3,7},{7,3},{8,12},{12,8},{9,1... | collective-permute-start | bytes 3538952 | tf_op jit(solution)/shard_map/gram/ppermute | solution.py:14
  154.7 4.6 %copy-start.5 = (f32[512]{0:T(512)S(1)}, f32[512]{0:T(512)}, u32[]{:S(2)}) copy-start(f32[512]{0:T(512)} %param.9) | copy-start | bytes 6148
  154.7 4.6 %copy-start.6 = (s32[3]{0:T(128)S(1)}, s32[3]{0:T(128)}, u32[]{:S(2)}) copy-start(s32[3]{0:T(128)} %param.11) | copy-start | bytes 40
  154.7 15.1 %all-to-all-start.4 = ((bf16[4,192,384]{2,1,0:T(8,128)(2,1)}), bf16[4,192,384]{2,1,0:T(8,128)(2,1)}, u32[]{:S(2)}, u32[]{:S(2)}) async-start(bf16[4,192,384]{2,1,0:T(8,128)(2,1)} %bitcast.71), calls=%async_computation.4 | async-start | bytes 1179648 | tf_op jit(solution)/shard_map/gram/all_to_all | solution.py:20
  184.7 3.9 %collective-permute-start.2 = (bf16[4,3,64,384]{3,2,1,0:T(8,128)(2,1)S(1)}, bf16[4,3,64,384]{3,2,1,0:T(8,128)(2,1)S(1)}, u32[]{:S(2)}, u32[]{:S(2)}) collective-permute-start(bf16[4,3,64,384]{3,2,1,0:T(8,128)(2,1)S(1)} %bitcast.67), channel_id=1, source_target_pairs={{0,4},{4,0},{1,5},{5,1},{2,6},{6,2},{3,7},{7,3},{8,12},{12,8},{9,1... | collective-permute-start | bytes 1769480 | tf_op jit(solution)/shard_map/amplitudes/ppermute | solution.py:14
  191.1 0.9 copy-start.3
  191.9 16.0 %all-to-all-start.5 = ((bf16[4,256,384]{2,1,0:T(8,128)(2,1)}), bf16[4,256,384]{2,1,0:T(8,128)(2,1)S(1)}, u32[]{:S(2)}, u32[]{:S(2)}) async-start(bf16[4,256,384]{2,1,0:T(8,128)(2,1)} %bitcast.66), calls=%async_computation.5 | async-start | bytes 1572864 | tf_op jit(solution)/shard_map/gamma/all_to_all | solution.py:20
  196.8 13.7 %collective-permute-start.3 = (bf16[3,3,64,128]{3,2,1,0:T(8,128)(2,1)S(1)}, bf16[3,3,64,128]{3,2,1,0:T(8,128)(2,1)S(1)}, u32[]{:S(2)}, u32[]{:S(2)}) collective-permute-start(bf16[3,3,64,128]{3,2,1,0:T(8,128)(2,1)S(1)} %get-tuple-element.11), channel_id=1, source_target_pairs={{0,32},{4,96},{8,40},{12,104},{16,48},{20,112},{24,56},{28,120},{3... | collective-permute-start | bytes 442376 | tf_op jit(solution)/shard_map/amplitudes/ppermute | solution.py:232
  210.6 24.7 %all-to-all-start.6 = ((bf16[16,16,384]{2,1,0:T(8,128)(2,1)}), bf16[16,16,384]{2,1,0:T(8,128)(2,1)S(1)}, u32[]{:S(2)}, u32[]{:S(2)}) async-start(bf16[16,16,384]{2,1,0:T(8,128)(2,1)} %bitcast.39), calls=%async_computation.6 | async-start | bytes 393216 | tf_op jit(solution)/shard_map/gamma/all_to_all | solution.py:20
Sparse Core Ops, SparseCore 0:
  67.1 77.1 all-gather.1

commit v7 on v6

--- a/solution.py
+++ b/solution.py
@@ -25,7 +25,7 @@
     return jnp.where(core == 0, mine, theirs), jnp.where(core == 0, theirs, mine)
 
 
-def gram_half(row, col, which, nocc, ny, room):
+def gram_half(row, col, which, nocc, ny, kind):
     k_rows, lanes = row.shape
     half = lanes // nocc // 2
     share = half // ny
@@ -41,11 +41,11 @@
         tile = lax.dot_general(
             row_ref[...], order_ref[...], (((0,), (0,)), ((), ())), preferred_element_type=F32
         )
-        out_ref[...] = tile.reshape(ny, 1, share, width)
-
-    return pl.pallas_call(
-        body,
-        out_shape=jax.ShapeDtypeStruct((ny, nocc, share, width), F32),
+        out_ref[...] = tile.reshape(ny, 1, share, width).astype(kind)
+
+    return pl.pallas_call(
+        body,
+        out_shape=jax.ShapeDtypeStruct((ny, nocc, share, width), kind),
         grid_spec=pltpu.PrefetchScalarGridSpec(
             num_scalar_prefetch=1,
             grid=(nocc,),
@@ -56,7 +56,7 @@
             out_specs=pl.BlockSpec((ny, 1, share, width), lambda i, w: (0, i, 0, 0)),
             scratch_shapes=[pltpu.VMEM((k_rows, width), BF)],
         ),
-        compiler_params=pltpu.CompilerParams(vmem_limit_bytes=room * 1024 * 1024),
+        compiler_params=pltpu.CompilerParams(vmem_limit_bytes=12 * 1024 * 1024),
         cost_estimate=pl.CostEstimate(
             flops=2 * k_rows * nocc * half * width,
             bytes_accessed=2 * k_rows * (nocc * half + width) + 4 * nocc * half * width,
@@ -66,51 +66,55 @@
     )(which.reshape(1), row, col)
 
 
-def contract(row, mine, theirs, core, nx, nz):
+def contract(row, tile, side, nx, nz, base=None):
     k_rows, lanes = row.shape
-    ny, nocc, share, width = mine.shape
+    ny, nocc, share, width = tile.shape
     half = ny * share
     r = k_rows // nx // nz
     steps = 4
     zs = nz // steps
-
-    def body(core_ref, row_ref, mine_ref, theirs_ref, out_ref, tile_ref):
-        @pl.when(pl.program_id(0) == 0)
-        def _():
-            for i in range(nocc):
-                for q in range(ny):
-                    for k, ref in enumerate((mine_ref, theirs_ref)):
-                        side = core_ref[0] if k == 0 else 1 - core_ref[0]
-                        start = (2 * i + side) * half + q * share
-                        tile_ref[pl.ds(pl.multiple_of(start, share), share), :] = ref[q, i]
-
-        value = jnp.dot(row_ref[...], tile_ref[...], preferred_element_type=F32).astype(BF)
-        value = value.reshape(zs, nx, r, width)
-        for k in range(nx):
-            out_ref[k] = value[:, k]
-
-    return pl.pallas_call(
-        body,
-        out_shape=jax.ShapeDtypeStruct((nx, nz, r, width), BF),
+    size = k_rows // steps
+
+    def body(side_ref, *refs):
+        rows, tile_ref, rest = refs[:nocc], refs[nocc], refs[nocc + 1 :]
+        total = jnp.zeros((size, width), F32) if base is None else rest[0][...]
+        for i in range(nocc):
+            total = total + jnp.dot(
+                rows[i][...], tile_ref[:, i].reshape(half, width), preferred_element_type=F32
+            )
+        if base is None:
+            rest[-1][...] = total
+        else:
+            value = total.astype(BF).reshape(zs, nx, r, width)
+            for k in range(nx):
+                rest[-1][k] = value[:, k]
+
+    def lane_block(i):
+        return pl.BlockSpec((size, half), lambda s, w: (s, 2 * i + w[0]))
+
+    flat = pl.BlockSpec((size, width), lambda s, w: (s, 0))
+    in_specs = [lane_block(i) for i in range(nocc)]
+    in_specs.append(pl.BlockSpec((ny, nocc, share, width), lambda s, w: (0, 0, 0, 0)))
+    if base is None:
+        out_shape, out_specs, extra = jax.ShapeDtypeStruct((k_rows, width), F32), flat, ()
+    else:
+        in_specs.append(flat)
+        out_shape = jax.ShapeDtypeStruct((nx, nz, r, width), BF)
+        out_specs, extra = pl.BlockSpec((nx, zs, r, width), lambda s, w: (0, s, 0, 0)), (base,)
+    return pl.pallas_call(
+        body,
+        out_shape=out_shape,
         grid_spec=pltpu.PrefetchScalarGridSpec(
-            num_scalar_prefetch=1,
-            grid=(steps,),
-            in_specs=[
-                pl.BlockSpec((k_rows // steps, lanes), lambda s, w: (s, 0)),
-                pl.BlockSpec((ny, nocc, share, width), lambda s, w: (0, 0, 0, 0)),
-                pl.BlockSpec((ny, nocc, share, width), lambda s, w: (0, 0, 0, 0)),
-            ],
-            out_specs=pl.BlockSpec((nx, zs, r, width), lambda s, w: (0, s, 0, 0)),
-            scratch_shapes=[pltpu.VMEM((lanes, width), BF)],
+            num_scalar_prefetch=1, grid=(steps,), in_specs=in_specs, out_specs=out_specs
         ),
         compiler_params=pltpu.CompilerParams(vmem_limit_bytes=12 * 1024 * 1024),
         cost_estimate=pl.CostEstimate(
-            flops=2 * k_rows * lanes * width,
-            bytes_accessed=2 * k_rows * (lanes + width) + 2 * lanes * width,
+            flops=k_rows * lanes * width,
+            bytes_accessed=k_rows * (lanes + 4 * width) + lanes * width,
             transcendentals=0,
         ),
         name="contract",
-    )(core.reshape(1), row, mine, theirs)
+    )(side.reshape(1), *([row] * nocc), tile, *extra)
 
 
 def amplitudes_of(parts, slot, row_energy, col_energy):
@@ -216,8 +220,8 @@
         col = col.reshape(nx, nz, r, nocc * narrow)
 
     with jax.named_scope("gram"):
-        other = swap_cores(gram_half(row, col, 1 - c, nocc, ny, 58))
-        gram = gram_half(row, col, c, nocc, ny, 12) + other
+        other = swap_cores(gram_half(row, col, 1 - c, nocc, ny, BF))
+        gram = gram_half(row, col, c, nocc, ny, F32) + other.astype(F32)
         gram = exchange(gram.astype(BF).reshape(ny, nocc * share, nocc * narrow), "y")
 
     with jax.named_scope("amplitudes"):
@@ -235,7 +239,7 @@
         theirs = swap_cores(mixed)
 
     with jax.named_scope("gamma"):
-        value = contract(row, mixed, theirs, c, nx, nz)
+        value = contract(row, theirs, 1 - c, nx, nz, contract(row, mixed, c, nx, nz))
         value = exchange(value.reshape(nx, nz * r, nocc * narrow), "x")
         value = jnp.sum(value.astype(F32), axis=0).astype(BF)
         value, own = lax.optimization_barrier((value, own))

time: 244 us -> 242 us (level)
  the two profiles are of different devices: /device:TPU:2 before, /device:TPU:1 now
where the time goes in v7:
time: 242 us; the launch traced here: 237 us
  waiting for transfers between devices  71.5 us (30%)
  starting transfers between devices  69.4 us (29%)
  blocking collectives  60.9 us (25%)
  between operations  14.4 us (6%)
  Pallas kernels  8.91 us (4%)
  local copies, waits for them, and re-layouts  6.37 us (3%)
  other arithmetic  5.12 us (2%)
    all_to_all x5, waiting for transfers between devices, exchange(): value = lax.all_to_all(value, axis, split_axis=0, concat_axis=0, tiled=True)  44 us
    all_to_all x5, starting transfers between devices, exchange(): value = lax.all_to_all(value, axis, split_axis=0, concat_axis=0, tiled=True)  40.1 us
    all_gather x1, waiting for transfers between devices, local(): lax.all_gather(row.reshape(nx * r, nocc * wide), 'z', axis=0, tiled=True)  26.2 us
    ppermute x3, starting transfers between devices, swap_cores(): return lax.ppermute(value, 'c', [(0, 1), (1, 0)])  24.5 us
    all_to_all x2, blocking collectives, exchange(): value = lax.all_to_all(value, axis, split_axis=0, concat_axis=0, tiled=True)  24.4 us
    all_gather x1, blocking collectives, local(): masked = lax.all_gather(masked.reshape(-1, ao_part), 'x', axis=0)  13.2 us
    all_gather x1, blocking collectives, local(): col = lax.all_gather(col.reshape(nz * r, nocc * narrow), 'x', axis=0)  12.5 us
    all_gather x1, blocking collectives, local(): lax.all_gather(mixed.reshape(nocc * share, nocc * narrow), 'y', axis=0)  10.8 us
  transfers between devices with their start and end apart: 10, of which 7 were waited for; matrix products, arithmetic and copies ran while one was open for 2% of the time, Pallas kernels for 1%

profile of v7, /device:TPU:1, one launch (start us, length us, event | category | flops | bytes accessed | tf_op | source)
XLA Modules:
  0.0 237.4 jit_solution(4816200405630793221)
XLA Ops:
  7.2 1.5 broadcast_in_dim.30
  8.7 15.7 %all-to-all-start = ((bf16[16,16,640]{2,1,0:T(8,128)(2,1)}), bf16[16,16,640]{2,1,0:T(8,128)(2,1)S(1)}, u32[]{:S(2)}, u32[]{:S(2)}) async-start(bf16[16,16,640]{2,1,0:T(8,128)(2,1)} %broadcast_in_dim.30), calls=%async_computation | async-start | bytes 655360 | tf_op jit(solution)/shard_map/transform/all_to_all | solution.py:20
  25.4 13.2 %all_gather.12 = bf16[4,192,640]{2,1,0:T(8,128)(2,1)S(1)} all-gather(bf16[1,192,640]{2,1,0:T(8,128)(2,1)S(1)} %bitcast.74), channel_id=1, replica_groups=mesh['x'=4,'z'=16,'c'=2,'y'=4] {'x'}, dimensions={0}, use_global_device_ids=true | all-gather | bytes 1228800 | tf_op jit(solution)/shard_map/transform/all_gather | solution.py:201
  38.7 1.0 all-to-all-done
  39.7 8.4 %collective-permute-start = (bf16[16,16,640]{2,1,0:T(8,128)(2,1)S(1)}, bf16[16,16,640]{2,1,0:T(8,128)(2,1)S(1)}, u32[]{:S(2)}, u32[]{:S(2)}) collective-permute-start(bf16[16,16,640]{2,1,0:T(8,128)(2,1)S(1)} %all-to-all-done), channel_id=1, source_target_pairs={{0,4},{4,0},{1,5},{5,1},{2,6},{6,2},{3,7},{7,3},{8,12},{12,8},{9,1... | collective-permute-start | bytes 983048 | tf_op jit(solution)/shard_map/transform/ppermute | solution.py:14
  48.1 1.2 collective-permute-done
  50.4 15.4 %all_to_all.57 = bf16[4,192,512]{2,1,0:T(8,128)(2,1)S(1)} all-to-all(bf16[4,192,512]{2,1,0:T(8,128)(2,1)S(1)} %bitcast.70), channel_id=1, replica_groups=mesh['x'=4,'z'=16,'c'=2,'y'=4] {'y'}, dimensions={0} | all-to-all | bytes 1572864 | tf_op jit(solution)/shard_map/transform/all_to_all | solution.py:20
  66.7 9.0 %all_to_all.58 = bf16[4,48,512]{2,1,0:T(8,128)(2,1)S(1)} all-to-all(bf16[4,48,512]{2,1,0:T(8,128)(2,1)S(1)} %bitcast.73), channel_id=1, replica_groups=mesh['x'=4,'z'=16,'c'=2,'y'=4] {'x'}, dimensions={0} | all-to-all | bytes 393216 | tf_op jit(solution)/shard_map/panels/all_to_all | solution.py:20
  76.8 6.7 %all-to-all-start.3 = ((bf16[16,16,384]{2,1,0:T(8,128)(2,1)}), bf16[16,16,384]{2,1,0:T(8,128)(2,1)S(1)}, u32[]{:S(2)}, u32[]{:S(2)}) async-start(bf16[16,16,384]{2,1,0:T(8,128)(2,1)} %pad_maximum_fusion.2), calls=%async_computation.3 | async-start | bytes 393216 | tf_op jit(solution)/shard_map/panels/all_to_all | solution.py:20
  83.5 14.6 %all-to-all-done.3 = bf16[16,16,384]{2,1,0:T(8,128)(2,1)S(1)} async-done(((bf16[16,16,384]{2,1,0:T(8,128)(2,1)}), bf16[16,16,384]{2,1,0:T(8,128)(2,1)S(1)}, u32[]{:S(2)}, u32[]{:S(2)}) %all-to-all-start.3) | async-done | bytes 196640 | tf_op jit(solution)/shard_map/panels/all_to_all | solution.py:20
  98.1 12.5 %all_gather.14 = bf16[4,256,384]{2,1,0:T(8,128)(2,1)} all-gather(bf16[1,256,384]{2,1,0:T(8,128)(2,1)S(1)} %bitcast.77), channel_id=1, replica_groups=mesh['x'=4,'z'=16,'c'=2,'y'=4] {'x'}, dimensions={0}, use_global_device_ids=true | all-gather | bytes 983040 | tf_op jit(solution)/shard_map/panels/all_gather | solution.py:219
  110.6 26.2 %all-gather.2.cloned.1.call-done.row_ref.refs_0_.refs_1_.refs_2_ = bf16[1024,1536]{1,0:T(8,128)(2,1)} async-done(((bf16[64,1536]{1,0:T(8,128)(2,1)}), bf16[1024,1536]{1,0:T(8,128)(2,1)}) %all-gather.2.cloned.1.call-update) | async-done | bytes 3145744 | tf_op jit(solution)/shard_map/panels/all_gather | solution.py:212
  136.8 1.9 copy-done.1
  138.7 1.1 copy-done.3
  139.9 1.7 gram_half.3
  141.6 10.6 %collective-permute-start.1 = (bf16[4,3,64,384]{3,2,1,0:T(8,128)(2,1)S(1)}, bf16[4,3,64,384]{3,2,1,0:T(8,128)(2,1)S(1)}, u32[]{:S(2)}, u32[]{:S(2)}) collective-permute-start(bf16[4,3,64,384]{3,2,1,0:T(8,128)(2,1)S(1)} %gram_half.3), channel_id=1, source_target_pairs={{0,4},{4,0},{1,5},{5,1},{2,6},{6,2},{3,7},{7,3},{8,12},{12,8},{9,1... | collective-permute-start | bytes 1769480 | tf_op jit(solution)/shard_map/gram/ppermute | solution.py:14
  152.2 1.8 gram_half.2
  154.0 1.0 add_convert_fusion
  155.0 4.3 %all-to-all-start.4 = ((bf16[4,192,384]{2,1,0:T(8,128)(2,1)}), bf16[4,192,384]{2,1,0:T(8,128)(2,1)}, u32[]{:S(2)}, u32[]{:S(2)}) async-start(bf16[4,192,384]{2,1,0:T(8,128)(2,1)} %bitcast.71), calls=%async_computation.4 | async-start | bytes 1179648 | tf_op jit(solution)/shard_map/gram/all_to_all | solution.py:20
  159.8 9.7 %all-to-all-done.4.parts_ref = bf16[4,192,384]{2,1,0:T(8,128)(2,1)} async-done(((bf16[4,192,384]{2,1,0:T(8,128)(2,1)}), bf16[4,192,384]{2,1,0:T(8,128)(2,1)}, u32[]{:S(2)}, u32[]{:S(2)}) %all-to-all-start.4) | async-done | bytes 589856 | tf_op jit(solution)/shard_map/gram/all_to_all | solution.py:20
  169.5 1.2 amplitudes_of.1
  170.7 10.8 %all_gather.15 = bf16[4,192,384]{2,1,0:T(8,128)(2,1)S(1)} all-gather(bf16[1,192,384]{2,1,0:T(8,128)(2,1)S(1)} %bitcast.69), channel_id=1, replica_groups=mesh['x'=4,'z'=16,'c'=2,'y'=4] {'y'}, dimensions={0}, use_global_device_ids=true | all-gather | bytes 737280 | tf_op jit(solution)/shard_map/amplitudes/all_gather | solution.py:237
  181.5 5.4 %collective-permute-start.2 = (bf16[4,3,64,384]{3,2,1,0:T(8,128)(2,1)S(1)}, bf16[4,3,64,384]{3,2,1,0:T(8,128)(2,1)S(1)}, u32[]{:S(2)}, u32[]{:S(2)}) collective-permute-start(bf16[4,3,64,384]{3,2,1,0:T(8,128)(2,1)S(1)} %bitcast.67), channel_id=1, source_target_pairs={{0,4},{4,0},{1,5},{5,1},{2,6},{6,2},{3,7},{7,3},{8,12},{12,8},{9,1... | collective-permute-start | bytes 1769480 | tf_op jit(solution)/shard_map/amplitudes/ppermute | solution.py:14
  186.9 1.7 contract.2.refs_4_
  188.7 1.8 contract.3
  190.5 0.9 copy-done.4
  191.3 4.6 %all-to-all-start.5 = ((bf16[4,256,384]{2,1,0:T(8,128)(2,1)}), bf16[4,256,384]{2,1,0:T(8,128)(2,1)S(1)}, u32[]{:S(2)}, u32[]{:S(2)}) async-start(bf16[4,256,384]{2,1,0:T(8,128)(2,1)} %bitcast.66), calls=%async_computation.5 | async-start | bytes 1572864 | tf_op jit(solution)/shard_map/gamma/all_to_all | solution.py:20
  195.9 4.8 %collective-permute-start.3 = (bf16[3,3,64,128]{3,2,1,0:T(8,128)(2,1)S(1)}, bf16[3,3,64,128]{3,2,1,0:T(8,128)(2,1)S(1)}, u32[]{:S(2)}, u32[]{:S(2)}) collective-permute-start(bf16[3,3,64,128]{3,2,1,0:T(8,128)(2,1)S(1)} %get-tuple-element.11), channel_id=1, source_target_pairs={{0,32},{4,96},{8,40},{12,104},{16,48},{20,112},{24,56},{28,120},{3... | collective-permute-start | bytes 442376 | tf_op jit(solution)/shard_map/amplitudes/ppermute | solution.py:236
  200.7 7.1 %all-to-all-done.5 = bf16[4,256,384]{2,1,0:T(8,128)(2,1)S(1)} async-done(((bf16[4,256,384]{2,1,0:T(8,128)(2,1)}), bf16[4,256,384]{2,1,0:T(8,128)(2,1)S(1)}, u32[]{:S(2)}, u32[]{:S(2)}) %all-to-all-start.5) | async-done | bytes 786464 | tf_op jit(solution)/shard_map/gamma/all_to_all | solution.py:20
  207.8 0.8 reduce_sum.35
  208.6 8.9 %all-to-all-start.6 = ((bf16[16,16,384]{2,1,0:T(8,128)(2,1)}), bf16[16,16,384]{2,1,0:T(8,128)(2,1)S(1)}, u32[]{:S(2)}, u32[]{:S(2)}) async-start(bf16[16,16,384]{2,1,0:T(8,128)(2,1)} %bitcast.39), calls=%async_computation.6 | async-start | bytes 393216 | tf_op jit(solution)/shard_map/gamma/all_to_all | solution.py:20
  218.2 11.6 %all-to-all-done.6.value_ref = bf16[16,16,384]{2,1,0:T(8,128)(2,1)S(1)} async-done(((bf16[16,16,384]{2,1,0:T(8,128)(2,1)}), bf16[16,16,384]{2,1,0:T(8,128)(2,1)S(1)}, u32[]{:S(2)}, u32[]{:S(2)}) %all-to-all-start.6) | async-done | bytes 196640 | tf_op jit(solution)/shard_map/gamma/all_to_all | solution.py:20
  (47 shorter events, 5.9 us)
Async XLA Ops:
  7.2 152.2 %copy-start = (f32[2048]{0:T(1024)S(1)}, f32[2048]{0:T(1024)}, u32[]{:S(2)}) copy-start(f32[2048]{0:T(1024)} %param.10) | copy-start | bytes 24580
  7.2 18.2 %copy-start.5 = (bf16[64,3,640]{2,0,1:T(8,128)(2,1)S(1)}, bf16[64,3,640]{2,0,1:T(8,128)(2,1)}, u32[]{:S(2)}) copy-start(bf16[64,3,640]{2,0,1:T(8,128)(2,1)} %param.6) | copy-start | bytes 737284
  8.7 31.0 %all-to-all-start = ((bf16[16,16,640]{2,1,0:T(8,128)(2,1)}), bf16[16,16,640]{2,1,0:T(8,128)(2,1)S(1)}, u32[]{:S(2)}, u32[]{:S(2)}) async-start(bf16[16,16,640]{2,1,0:T(8,128)(2,1)} %broadcast_in_dim.30), calls=%async_computation | async-start | bytes 655360 | tf_op jit(solution)/shard_map/transform/all_to_all | solution.py:20
  24.5 112.4 %all-gather.2.cloned.1.call-start = ((), (), s32[]{:S(2)}) async-start(), calls=%async_computation.7 | async-start | bytes 3342336 | tf_op jit(solution)/shard_map/panels/all_gather | solution.py:212
  39.7 9.6 %collective-permute-start = (bf16[16,16,640]{2,1,0:T(8,128)(2,1)S(1)}, bf16[16,16,640]{2,1,0:T(8,128)(2,1)S(1)}, u32[]{:S(2)}, u32[]{:S(2)}) collective-permute-start(bf16[16,16,640]{2,1,0:T(8,128)(2,1)S(1)} %all-to-all-done), channel_id=1, source_target_pairs={{0,4},{4,0},{1,5},{5,1},{2,6},{6,2},{3,7},{7,3},{8,12},{12,8},{9,1... | collective-permute-start | bytes 983048 | tf_op jit(solution)/shard_map/transform/ppermute | solution.py:14
  76.8 21.3 %all-to-all-start.3 = ((bf16[16,16,384]{2,1,0:T(8,128)(2,1)}), bf16[16,16,384]{2,1,0:T(8,128)(2,1)S(1)}, u32[]{:S(2)}, u32[]{:S(2)}) async-start(bf16[16,16,384]{2,1,0:T(8,128)(2,1)} %pad_maximum_fusion.2), calls=%async_computation.3 | async-start | bytes 393216 | tf_op jit(solution)/shard_map/panels/all_to_all | solution.py:20
  136.8 1.9 copy-start.1
  138.7 1.1 copy-start.3
  139.9 12.3 %copy-start.2 = (bf16[1024,1536]{1,0:T(8,128)(2,1)S(1)}, bf16[1024,1536]{1,0:T(8,128)(2,1)}, u32[]{:S(2)}) copy-start(bf16[1024,1536]{1,0:T(8,128)(2,1)} %all-gather.2.cloned.1.call-done.row_ref.refs_0_.refs_1_.refs_2_) | copy-start | bytes 9437188
  141.6 12.4 %collective-permute-start.1 = (bf16[4,3,64,384]{3,2,1,0:T(8,128)(2,1)S(1)}, bf16[4,3,64,384]{3,2,1,0:T(8,128)(2,1)S(1)}, u32[]{:S(2)}, u32[]{:S(2)}) collective-permute-start(bf16[4,3,64,384]{3,2,1,0:T(8,128)(2,1)S(1)} %gram_half.3), channel_id=1, source_target_pairs={{0,4},{4,0},{1,5},{5,1},{2,6},{6,2},{3,7},{7,3},{8,12},{12,8},{9,1... | collective-permute-start | bytes 1769480 | tf_op jit(solution)/shard_map/gram/ppermute | solution.py:14
  155.0 4.6 %copy-start.6 = (f32[512]{0:T(512)S(1)}, f32[512]{0:T(512)}, u32[]{:S(2)}) copy-start(f32[512]{0:T(512)} %param.9) | copy-start | bytes 6148
  155.0 4.6 %copy-start.7 = (s32[3]{0:T(128)S(1)}, s32[3]{0:T(128)}, u32[]{:S(2)}) copy-start(s32[3]{0:T(128)} %param.11) | copy-start | bytes 40
  155.0 14.5 %all-to-all-start.4 = ((bf16[4,192,384]{2,1,0:T(8,128)(2,1)}), bf16[4,192,384]{2,1,0:T(8,128)(2,1)}, u32[]{:S(2)}, u32[]{:S(2)}) async-start(bf16[4,192,384]{2,1,0:T(8,128)(2,1)} %bitcast.71), calls=%async_computation.4 | async-start | bytes 1179648 | tf_op jit(solution)/shard_map/gram/all_to_all | solution.py:20
  181.5 7.2 %collective-permute-start.2 = (bf16[4,3,64,384]{3,2,1,0:T(8,128)(2,1)S(1)}, bf16[4,3,64,384]{3,2,1,0:T(8,128)(2,1)S(1)}, u32[]{:S(2)}, u32[]{:S(2)}) collective-permute-start(bf16[4,3,64,384]{3,2,1,0:T(8,128)(2,1)S(1)} %bitcast.67), channel_id=1, source_target_pairs={{0,4},{4,0},{1,5},{5,1},{2,6},{6,2},{3,7},{7,3},{8,12},{12,8},{9,1... | collective-permute-start | bytes 1769480 | tf_op jit(solution)/shard_map/amplitudes/ppermute | solution.py:14
  190.5 0.9 copy-start.4
  191.3 16.5 %all-to-all-start.5 = ((bf16[4,256,384]{2,1,0:T(8,128)(2,1)}), bf16[4,256,384]{2,1,0:T(8,128)(2,1)S(1)}, u32[]{:S(2)}, u32[]{:S(2)}) async-start(bf16[4,256,384]{2,1,0:T(8,128)(2,1)} %bitcast.66), calls=%async_computation.5 | async-start | bytes 1572864 | tf_op jit(solution)/shard_map/gamma/all_to_all | solution.py:20
  195.9 12.7 %collective-permute-start.3 = (bf16[3,3,64,128]{3,2,1,0:T(8,128)(2,1)S(1)}, bf16[3,3,64,128]{3,2,1,0:T(8,128)(2,1)S(1)}, u32[]{:S(2)}, u32[]{:S(2)}) collective-permute-start(bf16[3,3,64,128]{3,2,1,0:T(8,128)(2,1)S(1)} %get-tuple-element.11), channel_id=1, source_target_pairs={{0,32},{4,96},{8,40},{12,104},{16,48},{20,112},{24,56},{28,120},{3... | collective-permute-start | bytes 442376 | tf_op jit(solution)/shard_map/amplitudes/ppermute | solution.py:236
  208.6 21.2 %all-to-all-start.6 = ((bf16[16,16,384]{2,1,0:T(8,128)(2,1)}), bf16[16,16,384]{2,1,0:T(8,128)(2,1)S(1)}, u32[]{:S(2)}, u32[]{:S(2)}) async-start(bf16[16,16,384]{2,1,0:T(8,128)(2,1)} %bitcast.39), calls=%async_computation.6 | async-start | bytes 393216 | tf_op jit(solution)/shard_map/gamma/all_to_all | solution.py:20
Sparse Core Ops, SparseCore 0:
  66.8 70.0 all-gather.1

commit v8 on v7

--- a/solution.py
+++ b/solution.py
@@ -23,6 +23,25 @@
 
 def by_core(mine, theirs, core):
     return jnp.where(core == 0, mine, theirs), jnp.where(core == 0, theirs, mine)
+
+
+def spread(value, copies):
+    def body(value_ref, out_ref, sems):
+        moves = [pltpu.make_async_copy(value_ref, out_ref.at[k], sems.at[k]) for k in range(copies)]
+        for move in moves:
+            move.start()
+        for move in moves:
+            move.wait()
+
+    return pl.pallas_call(
+        body,
+        out_shape=pltpu.HBM((copies,) + value.shape, value.dtype),
+        in_specs=[pl.BlockSpec(memory_space=pltpu.VMEM)],
+        out_specs=pl.BlockSpec(memory_space=pltpu.HBM),
+        scratch_shapes=[pltpu.SemaphoreType.DMA((copies,))],
+        compiler_params=pltpu.CompilerParams(vmem_limit_bytes=12 * 1024 * 1024),
+        name="spread",
+    )(value)
 
 
 def gram_half(row, col, which, nocc, ny, kind):
@@ -99,7 +118,7 @@
         out_shape, out_specs, extra = jax.ShapeDtypeStruct((k_rows, width), F32), flat, ()
     else:
         in_specs.append(flat)
-        out_shape = jax.ShapeDtypeStruct((nx, nz, r, width), BF)
+        out_shape = pltpu.HBM((nx, nz, r, width), BF)
         out_specs, extra = pl.BlockSpec((nx, zs, r, width), lambda s, w: (0, s, 0, 0)), (base,)
     return pl.pallas_call(
         body,
@@ -193,8 +212,7 @@
     slot_energy = jnp.sum(onehot * occ_energy[None, :], axis=1)
 
     with jax.named_scope("transform"):
-        copies = jnp.broadcast_to(coef_virt[None], (nz,) + coef_virt.shape)
-        coef = exchange(copies, "z")
+        coef = exchange(spread(coef_virt, nz), "z")
         expanded = jnp.repeat(jnp.repeat(screen, 32, axis=0), 128, axis=1).astype(BF)
         masked = half_ints * expanded[:, None, :]
         masked = masked.reshape(ny, r, nocc, ao_part).transpose(0, 2, 1, 3)

time: 242 us -> 242 us (level)
  the two profiles are of different devices: /device:TPU:1 before, /device:TPU:2 now
where the time goes in v8:
time: 242 us; the launch traced here: 241 us
  waiting for transfers between devices  86.9 us (36%)
  blocking collectives  68.9 us (28%)
  starting transfers between devices  49.9 us (21%)
  between operations  14.4 us (6%)
  Pallas kernels  10.6 us (4%)
  other arithmetic  5.12 us (2%)
  local copies, waits for them, and re-layouts  4.76 us (2%)
    all_to_all x5, waiting for transfers between devices, exchange(): value = lax.all_to_all(value, axis, split_axis=0, concat_axis=0, tiled=True)  54.6 us
    all_to_all x5, starting transfers between devices, exchange(): value = lax.all_to_all(value, axis, split_axis=0, concat_axis=0, tiled=True)  39.6 us
    all_gather x1, waiting for transfers between devices, local(): lax.all_gather(row.reshape(nx * r, nocc * wide), 'z', axis=0, tiled=True)  28.4 us
    all_to_all x2, blocking collectives, exchange(): value = lax.all_to_all(value, axis, split_axis=0, concat_axis=0, tiled=True)  26.3 us
    all_gather x1, blocking collectives, local(): masked = lax.all_gather(masked.reshape(-1, ao_part), 'x', axis=0)  15.1 us
    all_gather x1, blocking collectives, local(): col = lax.all_gather(col.reshape(nz * r, nocc * narrow), 'x', axis=0)  13.9 us
    all_gather x1, blocking collectives, local(): lax.all_gather(mixed.reshape(nocc * share, nocc * narrow), 'y', axis=0)  13.6 us
    ppermute x3, starting transfers between devices, swap_cores(): return lax.ppermute(value, 'c', [(0, 1), (1, 0)])  5.74 us
  transfers between devices with their start and end apart: 10, of which 10 were waited for; matrix products, arithmetic and copies ran while one was open for 2% of the time, Pallas kernels for 1%

profile of v8, /device:TPU:2, one launch (start us, length us, event | category | flops | bytes accessed | tf_op | source)
XLA Modules:
  0.0 241.4 jit_solution(11879437838564825810)
XLA Ops:
  7.9 0.9 spread.1
  8.8 15.2 %all-to-all-start = ((bf16[16,16,640]{2,1,0:T(8,128)(2,1)}), bf16[16,16,640]{2,1,0:T(8,128)(2,1)S(1)}, u32[]{:S(2)}, u32[]{:S(2)}) async-start(bf16[16,16,640]{2,1,0:T(8,128)(2,1)} %spread.1), calls=%async_computation | async-start | bytes 655360 | tf_op jit(solution)/shard_map/transform/all_to_all | solution.py:20
  25.0 15.1 %all_gather.12 = bf16[4,192,640]{2,1,0:T(8,128)(2,1)S(1)} all-gather(bf16[1,192,640]{2,1,0:T(8,128)(2,1)S(1)} %bitcast.72), channel_id=1, replica_groups=mesh['x'=4,'z'=16,'c'=2,'y'=4] {'x'}, dimensions={0}, use_global_device_ids=true | all-gather | bytes 1228800 | tf_op jit(solution)/shard_map/transform/all_gather | solution.py:219
  40.1 4.7 %all-to-all-done = bf16[16,16,640]{2,1,0:T(8,128)(2,1)S(1)} async-done(((bf16[16,16,640]{2,1,0:T(8,128)(2,1)}), bf16[16,16,640]{2,1,0:T(8,128)(2,1)S(1)}, u32[]{:S(2)}, u32[]{:S(2)}) %all-to-all-start) | async-done | bytes 327712 | tf_op jit(solution)/shard_map/transform/all_to_all | solution.py:20
  44.8 1.9 collective-permute-start
  46.7 1.6 collective-permute-done
  49.4 16.8 %all_to_all.57 = bf16[4,192,512]{2,1,0:T(8,128)(2,1)S(1)} all-to-all(bf16[4,192,512]{2,1,0:T(8,128)(2,1)S(1)} %bitcast.68), channel_id=1, replica_groups=mesh['x'=4,'z'=16,'c'=2,'y'=4] {'y'}, dimensions={0} | all-to-all | bytes 1572864 | tf_op jit(solution)/shard_map/transform/all_to_all | solution.py:20
  67.1 9.5 %all_to_all.58 = bf16[4,48,512]{2,1,0:T(8,128)(2,1)S(1)} all-to-all(bf16[4,48,512]{2,1,0:T(8,128)(2,1)S(1)} %bitcast.71), channel_id=1, replica_groups=mesh['x'=4,'z'=16,'c'=2,'y'=4] {'x'}, dimensions={0} | all-to-all | bytes 393216 | tf_op jit(solution)/shard_map/panels/all_to_all | solution.py:20
  77.8 7.0 %all-to-all-start.3 = ((bf16[16,16,384]{2,1,0:T(8,128)(2,1)}), bf16[16,16,384]{2,1,0:T(8,128)(2,1)S(1)}, u32[]{:S(2)}, u32[]{:S(2)}) async-start(bf16[16,16,384]{2,1,0:T(8,128)(2,1)} %pad_maximum_fusion.2), calls=%async_computation.3 | async-start | bytes 393216 | tf_op jit(solution)/shard_map/panels/all_to_all | solution.py:20
  84.8 17.4 %all-to-all-done.3 = bf16[16,16,384]{2,1,0:T(8,128)(2,1)S(1)} async-done(((bf16[16,16,384]{2,1,0:T(8,128)(2,1)}), bf16[16,16,384]{2,1,0:T(8,128)(2,1)S(1)}, u32[]{:S(2)}, u32[]{:S(2)}) %all-to-all-start.3) | async-done | bytes 196640 | tf_op jit(solution)/shard_map/panels/all_to_all | solution.py:20
  102.2 13.9 %all_gather.14 = bf16[4,256,384]{2,1,0:T(8,128)(2,1)} all-gather(bf16[1,256,384]{2,1,0:T(8,128)(2,1)S(1)} %bitcast.75), channel_id=1, replica_groups=mesh['x'=4,'z'=16,'c'=2,'y'=4] {'x'}, dimensions={0}, use_global_device_ids=true | all-gather | bytes 983040 | tf_op jit(solution)/shard_map/panels/all_gather | solution.py:237
  116.1 28.4 %all-gather.2.cloned.1.call-done.row_ref.refs_0_.refs_1_.refs_2_ = bf16[1024,1536]{1,0:T(8,128)(2,1)} async-done(((bf16[64,1536]{1,0:T(8,128)(2,1)}), bf16[1024,1536]{1,0:T(8,128)(2,1)}) %all-gather.2.cloned.1.call-update) | async-done | bytes 3145744 | tf_op jit(solution)/shard_map/panels/all_gather | solution.py:230
  144.5 1.9 copy-done.1
  146.4 1.1 copy-done.3
  147.5 1.7 gram_half.3
  149.2 1.9 collective-permute-start.1
  151.2 1.8 gram_half.2
  153.1 1.0 add_convert_fusion
  154.1 4.3 %all-to-all-start.4 = ((bf16[4,192,384]{2,1,0:T(8,128)(2,1)}), bf16[4,192,384]{2,1,0:T(8,128)(2,1)}, u32[]{:S(2)}, u32[]{:S(2)}) async-start(bf16[4,192,384]{2,1,0:T(8,128)(2,1)} %bitcast.69), calls=%async_computation.4 | async-start | bytes 1179648 | tf_op jit(solution)/shard_map/gram/all_to_all | solution.py:20
  158.9 10.5 %all-to-all-done.4.parts_ref = bf16[4,192,384]{2,1,0:T(8,128)(2,1)} async-done(((bf16[4,192,384]{2,1,0:T(8,128)(2,1)}), bf16[4,192,384]{2,1,0:T(8,128)(2,1)}, u32[]{:S(2)}, u32[]{:S(2)}) %all-to-all-start.4) | async-done | bytes 589856 | tf_op jit(solution)/shard_map/gram/all_to_all | solution.py:20
  169.4 1.2 amplitudes_of.1
  170.6 13.6 %all_gather.15 = bf16[4,192,384]{2,1,0:T(8,128)(2,1)S(1)} all-gather(bf16[1,192,384]{2,1,0:T(8,128)(2,1)S(1)} %bitcast.66), channel_id=1, replica_groups=mesh['x'=4,'z'=16,'c'=2,'y'=4] {'y'}, dimensions={0}, use_global_device_ids=true | all-gather | bytes 737280 | tf_op jit(solution)/shard_map/amplitudes/all_gather | solution.py:255
  184.2 1.9 collective-permute-start.2
  186.1 1.7 contract.2.refs_4_
  188.1 2.7 %contract.3 = bf16[4,16,16,384]{3,2,1,0:T(8,128)(2,1)} custom-call(s32[1]{0:T(128)} %bitcast.which_ref.side_ref, bf16[1024,1536]{1,0:T(8,128)(2,1)S(1)} %copy-done.2, bf16[1024,1536]{1,0:T(8,128)(2,1)S(1)} %copy-done.2, bf16[1024,1536]{1,0:T(8,128)(2,1)S(1)} %copy-done.2, bf16[4,3,64,384]{3,2,1,0:T(8,128)(2,1)S(1)} %collective-permute-done.2.refs_3_, ...), custom_call_target="tpu_custom_call" | custom-call | flops 603979776 | bytes 3735552 | tf_op jit(solution)/shard_map/gamma/contract/pallas_call | solution.py:123
  190.8 4.8 %all-to-all-start.5 = ((bf16[4,256,384]{2,1,0:T(8,128)(2,1)}), bf16[4,256,384]{2,1,0:T(8,128)(2,1)S(1)}, u32[]{:S(2)}, u32[]{:S(2)}) async-start(bf16[4,256,384]{2,1,0:T(8,128)(2,1)} %bitcast.67), calls=%async_computation.5 | async-start | bytes 1572864 | tf_op jit(solution)/shard_map/gamma/all_to_all | solution.py:20
  195.6 4.4 %collective-permute-start.3 = (bf16[3,3,64,128]{3,2,1,0:T(8,128)(2,1)S(1)}, bf16[3,3,64,128]{3,2,1,0:T(8,128)(2,1)S(1)}, u32[]{:S(2)}, u32[]{:S(2)}) collective-permute-start(bf16[3,3,64,128]{3,2,1,0:T(8,128)(2,1)S(1)} %get-tuple-element.11), channel_id=1, source_target_pairs={{0,32},{4,96},{8,40},{12,104},{16,48},{20,112},{24,56},{28,120},{3... | collective-permute-start | bytes 442376 | tf_op jit(solution)/shard_map/amplitudes/ppermute | solution.py:254
  200.0 6.9 %all-to-all-done.5 = bf16[4,256,384]{2,1,0:T(8,128)(2,1)S(1)} async-done(((bf16[4,256,384]{2,1,0:T(8,128)(2,1)}), bf16[4,256,384]{2,1,0:T(8,128)(2,1)S(1)}, u32[]{:S(2)}, u32[]{:S(2)}) %all-to-all-start.5) | async-done | bytes 786464 | tf_op jit(solution)/shard_map/gamma/all_to_all | solution.py:20
  206.9 0.8 reduce_sum.35
  207.7 1.8 collective-permute-done.3
  209.5 8.4 %all-to-all-start.6 = ((bf16[16,16,384]{2,1,0:T(8,128)(2,1)}), bf16[16,16,384]{2,1,0:T(8,128)(2,1)S(1)}, u32[]{:S(2)}, u32[]{:S(2)}) async-start(bf16[16,16,384]{2,1,0:T(8,128)(2,1)} %bitcast.38), calls=%async_computation.6 | async-start | bytes 393216 | tf_op jit(solution)/shard_map/gamma/all_to_all | solution.py:20
  218.6 15.2 %all-to-all-done.6.value_ref = bf16[16,16,384]{2,1,0:T(8,128)(2,1)S(1)} async-done(((bf16[16,16,384]{2,1,0:T(8,128)(2,1)}), bf16[16,16,384]{2,1,0:T(8,128)(2,1)S(1)}, u32[]{:S(2)}, u32[]{:S(2)}) %all-to-all-start.6) | async-done | bytes 196640 | tf_op jit(solution)/shard_map/gamma/all_to_all | solution.py:20
  (48 shorter events, 7.1 us)
Async XLA Ops:
  7.2 151.3 %copy-start = (f32[2048]{0:T(1024)S(1)}, f32[2048]{0:T(1024)}, u32[]{:S(2)}) copy-start(f32[2048]{0:T(1024)} %param.10) | copy-start | bytes 24580
  7.2 0.7 copy-start.4
  7.9 17.0 %copy-start.5 = (bf16[64,3,640]{2,0,1:T(8,128)(2,1)S(1)}, bf16[64,3,640]{2,0,1:T(8,128)(2,1)}, u32[]{:S(2)}) copy-start(bf16[64,3,640]{2,0,1:T(8,128)(2,1)} %param.6) | copy-start | bytes 737284
  8.8 36.0 %all-to-all-start = ((bf16[16,16,640]{2,1,0:T(8,128)(2,1)}), bf16[16,16,640]{2,1,0:T(8,128)(2,1)S(1)}, u32[]{:S(2)}, u32[]{:S(2)}) async-start(bf16[16,16,640]{2,1,0:T(8,128)(2,1)} %spread.1), calls=%async_computation | async-start | bytes 655360 | tf_op jit(solution)/shard_map/transform/all_to_all | solution.py:20
  24.0 120.5 %all-gather.2.cloned.1.call-start = ((), (), s32[]{:S(2)}) async-start(), calls=%async_computation.7 | async-start | bytes 3342336 | tf_op jit(solution)/shard_map/panels/all_gather | solution.py:230
  44.8 3.5 %collective-permute-start = (bf16[16,16,640]{2,1,0:T(8,128)(2,1)S(1)}, bf16[16,16,640]{2,1,0:T(8,128)(2,1)S(1)}, u32[]{:S(2)}, u32[]{:S(2)}) collective-permute-start(bf16[16,16,640]{2,1,0:T(8,128)(2,1)S(1)} %all-to-all-done), channel_id=1, source_target_pairs={{0,4},{4,0},{1,5},{5,1},{2,6},{6,2},{3,7},{7,3},{8,12},{12,8},{9,1... | collective-permute-start | bytes 983048 | tf_op jit(solution)/shard_map/transform/ppermute | solution.py:14
  77.8 24.4 %all-to-all-start.3 = ((bf16[16,16,384]{2,1,0:T(8,128)(2,1)}), bf16[16,16,384]{2,1,0:T(8,128)(2,1)S(1)}, u32[]{:S(2)}, u32[]{:S(2)}) async-start(bf16[16,16,384]{2,1,0:T(8,128)(2,1)} %pad_maximum_fusion.2), calls=%async_computation.3 | async-start | bytes 393216 | tf_op jit(solution)/shard_map/panels/all_to_all | solution.py:20
  144.5 1.9 copy-start.1
  146.4 1.1 copy-start.3
  147.5 3.6 %copy-start.2 = (bf16[1024,1536]{1,0:T(8,128)(2,1)S(1)}, bf16[1024,1536]{1,0:T(8,128)(2,1)}, u32[]{:S(2)}) copy-start(bf16[1024,1536]{1,0:T(8,128)(2,1)} %all-gather.2.cloned.1.call-done.row_ref.refs_0_.refs_1_.refs_2_) | copy-start | bytes 9437188
  149.2 3.9 %collective-permute-start.1 = (bf16[4,3,64,384]{3,2,1,0:T(8,128)(2,1)S(1)}, bf16[4,3,64,384]{3,2,1,0:T(8,128)(2,1)S(1)}, u32[]{:S(2)}, u32[]{:S(2)}) collective-permute-start(bf16[4,3,64,384]{3,2,1,0:T(8,128)(2,1)S(1)} %gram_half.3), channel_id=1, source_target_pairs={{0,4},{4,0},{1,5},{5,1},{2,6},{6,2},{3,7},{7,3},{8,12},{12,8},{9,1... | collective-permute-start | bytes 1769480 | tf_op jit(solution)/shard_map/gram/ppermute | solution.py:14
  154.1 4.6 %copy-start.6 = (f32[512]{0:T(512)S(1)}, f32[512]{0:T(512)}, u32[]{:S(2)}) copy-start(f32[512]{0:T(512)} %param.9) | copy-start | bytes 6148
  154.1 4.6 %copy-start.7 = (s32[3]{0:T(128)S(1)}, s32[3]{0:T(128)}, u32[]{:S(2)}) copy-start(s32[3]{0:T(128)} %param.11) | copy-start | bytes 40
  154.1 15.3 %all-to-all-start.4 = ((bf16[4,192,384]{2,1,0:T(8,128)(2,1)}), bf16[4,192,384]{2,1,0:T(8,128)(2,1)}, u32[]{:S(2)}, u32[]{:S(2)}) async-start(bf16[4,192,384]{2,1,0:T(8,128)(2,1)} %bitcast.69), calls=%async_computation.4 | async-start | bytes 1179648 | tf_op jit(solution)/shard_map/gram/all_to_all | solution.py:20
  184.2 3.9 %collective-permute-start.2 = (bf16[4,3,64,384]{3,2,1,0:T(8,128)(2,1)S(1)}, bf16[4,3,64,384]{3,2,1,0:T(8,128)(2,1)S(1)}, u32[]{:S(2)}, u32[]{:S(2)}) collective-permute-start(bf16[4,3,64,384]{3,2,1,0:T(8,128)(2,1)S(1)} %bitcast.64), channel_id=1, source_target_pairs={{0,4},{4,0},{1,5},{5,1},{2,6},{6,2},{3,7},{7,3},{8,12},{12,8},{9,1... | collective-permute-start | bytes 1769480 | tf_op jit(solution)/shard_map/amplitudes/ppermute | solution.py:14
  190.8 16.1 %all-to-all-start.5 = ((bf16[4,256,384]{2,1,0:T(8,128)(2,1)}), bf16[4,256,384]{2,1,0:T(8,128)(2,1)S(1)}, u32[]{:S(2)}, u32[]{:S(2)}) async-start(bf16[4,256,384]{2,1,0:T(8,128)(2,1)} %bitcast.67), calls=%async_computation.5 | async-start | bytes 1572864 | tf_op jit(solution)/shard_map/gamma/all_to_all | solution.py:20
  195.6 13.9 %collective-permute-start.3 = (bf16[3,3,64,128]{3,2,1,0:T(8,128)(2,1)S(1)}, bf16[3,3,64,128]{3,2,1,0:T(8,128)(2,1)S(1)}, u32[]{:S(2)}, u32[]{:S(2)}) collective-permute-start(bf16[3,3,64,128]{3,2,1,0:T(8,128)(2,1)S(1)} %get-tuple-element.11), channel_id=1, source_target_pairs={{0,32},{4,96},{8,40},{12,104},{16,48},{20,112},{24,56},{28,120},{3... | collective-permute-start | bytes 442376 | tf_op jit(solution)/shard_map/amplitudes/ppermute | solution.py:254
  209.5 24.3 %all-to-all-start.6 = ((bf16[16,16,384]{2,1,0:T(8,128)(2,1)}), bf16[16,16,384]{2,1,0:T(8,128)(2,1)S(1)}, u32[]{:S(2)}, u32[]{:S(2)}) async-start(bf16[16,16,384]{2,1,0:T(8,128)(2,1)} %bitcast.38), calls=%async_computation.6 | async-start | bytes 393216 | tf_op jit(solution)/shard_map/gamma/all_to_all | solution.py:20
Sparse Core Ops, SparseCore 0:
  67.3 77.1 all-gather.1

commit v9 on v8

--- a/solution.py
+++ b/solution.py
@@ -36,12 +36,42 @@
     return pl.pallas_call(
         body,
         out_shape=pltpu.HBM((copies,) + value.shape, value.dtype),
-        in_specs=[pl.BlockSpec(memory_space=pltpu.VMEM)],
+        in_specs=[pl.BlockSpec(memory_space=pl.ANY)],
         out_specs=pl.BlockSpec(memory_space=pltpu.HBM),
         scratch_shapes=[pltpu.SemaphoreType.DMA((copies,))],
         compiler_params=pltpu.CompilerParams(vmem_limit_bytes=12 * 1024 * 1024),
         name="spread",
     )(value)
+
+
+def add_parts(parts, nx, nocc):
+    ways, rows, wide = parts.shape
+    r = rows // nx // nocc
+
+    def body(parts_ref, row_ref, three_ref):
+        total = parts_ref[0].astype(F32)
+        for k in range(1, ways):
+            total = total + parts_ref[k].astype(F32)
+        total = total.astype(BF)
+        three_ref[...] = total
+        for i in range(nocc):
+            row_ref[:, i * wide : (i + 1) * wide] = total[i * r : (i + 1) * r]
+
+    return pl.pallas_call(
+        body,
+        out_shape=(
+            pltpu.HBM((nx * r, nocc * wide), BF),
+            jax.ShapeDtypeStruct((rows, wide), BF),
+        ),
+        grid=(nx,),
+        in_specs=[pl.BlockSpec((ways, nocc * r, wide), lambda k: (0, k, 0))],
+        out_specs=(
+            pl.BlockSpec((r, nocc * wide), lambda k: (k, 0)),
+            pl.BlockSpec((nocc * r, wide), lambda k: (k, 0)),
+        ),
+        compiler_params=pltpu.CompilerParams(vmem_limit_bytes=12 * 1024 * 1024),
+        name="add_parts",
+    )(parts)
 
 
 def gram_half(row, col, which, nocc, ny, kind):
@@ -223,11 +253,10 @@
         coef = jnp.stack([low, high], axis=1).reshape(wide, ao_part)
         part = jnp.einsum("xyirm,am->yxira", masked, coef, preferred_element_type=F32)
         part = exchange(part.astype(BF).reshape(ny, nx * nocc * r, wide), "y")
-        three = jnp.sum(part.astype(F32), axis=0).astype(BF).reshape(nx, nocc, r, wide)
+        row, three = add_parts(part, nx, nocc)
 
     with jax.named_scope("panels"):
-        row = jnp.concatenate([three[:, i] for i in range(nocc)], axis=-1)
-        row = lax.all_gather(row.reshape(nx * r, nocc * wide), "z", axis=0, tiled=True)
+        row = lax.all_gather(row, "z", axis=0, tiled=True)
         col = exchange(three.reshape(nx, nocc * r, wide), "x")
         col = jnp.roll(col, nx // 2, axis=0).reshape(nx, nocc, r, ways // 2, 2, narrow)
         col = jnp.concatenate(

time: 242 us -> 243 us (level)
  the two profiles are of different devices: /device:TPU:2 before, /device:TPU:1 now
where the time goes in v9:
time: 243 us; the launch traced here: 238 us
  waiting for transfers between devices  71.4 us (29%)
  starting transfers between devices  69.9 us (29%)
  blocking collectives  60.6 us (25%)
  between operations  14.4 us (6%)
  Pallas kernels  12.1 us (5%)
  local copies, waits for them, and re-layouts  4.74 us (2%)
  other arithmetic  4.28 us (2%)
    all_to_all x5, waiting for transfers between devices, exchange(): value = lax.all_to_all(value, axis, split_axis=0, concat_axis=0, tiled=True)  44.1 us
    all_to_all x5, starting transfers between devices, exchange(): value = lax.all_to_all(value, axis, split_axis=0, concat_axis=0, tiled=True)  39.7 us
    all_gather x1, waiting for transfers between devices, local(): row = lax.all_gather(row, 'z', axis=0, tiled=True)  26 us
    ppermute x3, starting transfers between devices, swap_cores(): return lax.ppermute(value, 'c', [(0, 1), (1, 0)])  25.3 us
    all_to_all x2, blocking collectives, exchange(): value = lax.all_to_all(value, axis, split_axis=0, concat_axis=0, tiled=True)  24.4 us
    all_gather x1, blocking collectives, local(): masked = lax.all_gather(masked.reshape(-1, ao_part), 'x', axis=0)  13.2 us
    all_gather x1, blocking collectives, local(): col = lax.all_gather(col.reshape(nz * r, nocc * narrow), 'x', axis=0)  12.5 us
    all_gather x1, blocking collectives, local(): lax.all_gather(mixed.reshape(nocc * share, nocc * narrow), 'y', axis=0)  10.4 us
  transfers between devices with their start and end apart: 10, of which 7 were waited for; matrix products, arithmetic and copies ran while one was open for 2% of the time, Pallas kernels for 1%

profile of v9, /device:TPU:1, one launch (start us, length us, event | category | flops | bytes accessed | tf_op | source)
XLA Modules:
  0.0 238.1 jit_solution(1401266951427235067)
XLA Ops:
  7.9 0.9 spread.1
  8.8 15.8 %all-to-all-start = ((bf16[16,16,640]{2,1,0:T(8,128)(2,1)}), bf16[16,16,640]{2,1,0:T(8,128)(2,1)S(1)}, u32[]{:S(2)}, u32[]{:S(2)}) async-start(bf16[16,16,640]{2,1,0:T(8,128)(2,1)} %spread.1), calls=%async_computation | async-start | bytes 655360 | tf_op jit(solution)/shard_map/transform/all_to_all | solution.py:20
  25.5 13.2 %all_gather.12 = bf16[4,192,640]{2,1,0:T(8,128)(2,1)S(1)} all-gather(bf16[1,192,640]{2,1,0:T(8,128)(2,1)S(1)} %bitcast.67), channel_id=1, replica_groups=mesh['x'=4,'z'=16,'c'=2,'y'=4] {'x'}, dimensions={0}, use_global_device_ids=true | all-gather | bytes 1228800 | tf_op jit(solution)/shard_map/transform/all_gather | solution.py:249
  38.8 1.0 all-to-all-done
  39.8 8.4 %collective-permute-start = (bf16[16,16,640]{2,1,0:T(8,128)(2,1)S(1)}, bf16[16,16,640]{2,1,0:T(8,128)(2,1)S(1)}, u32[]{:S(2)}, u32[]{:S(2)}) collective-permute-start(bf16[16,16,640]{2,1,0:T(8,128)(2,1)S(1)} %all-to-all-done), channel_id=1, source_target_pairs={{0,4},{4,0},{1,5},{5,1},{2,6},{6,2},{3,7},{7,3},{8,12},{12,8},{9,1... | collective-permute-start | bytes 983048 | tf_op jit(solution)/shard_map/transform/ppermute | solution.py:14
  48.2 1.2 collective-permute-done
  50.5 15.4 %all_to_all.57.parts_ref = bf16[4,192,512]{2,1,0:T(8,128)(2,1)S(1)} all-to-all(bf16[4,192,512]{2,1,0:T(8,128)(2,1)S(1)} %bitcast.65), channel_id=1, replica_groups=mesh['x'=4,'z'=16,'c'=2,'y'=4] {'y'}, dimensions={0} | all-to-all | bytes 1572864 | tf_op jit(solution)/shard_map/transform/all_to_all | solution.py:20
  65.9 1.4 add_parts.1
  67.4 9.0 %all_to_all.58 = bf16[4,48,512]{2,1,0:T(8,128)(2,1)S(1)} all-to-all(bf16[4,48,512]{2,1,0:T(8,128)(2,1)S(1)} %bitcast.62), channel_id=1, replica_groups=mesh['x'=4,'z'=16,'c'=2,'y'=4] {'x'}, dimensions={0} | all-to-all | bytes 393216 | tf_op jit(solution)/shard_map/panels/all_to_all | solution.py:20
  77.5 6.7 %all-to-all-start.3 = ((bf16[16,16,384]{2,1,0:T(8,128)(2,1)}), bf16[16,16,384]{2,1,0:T(8,128)(2,1)S(1)}, u32[]{:S(2)}, u32[]{:S(2)}) async-start(bf16[16,16,384]{2,1,0:T(8,128)(2,1)} %pad_maximum_fusion.1), calls=%async_computation.3 | async-start | bytes 393216 | tf_op jit(solution)/shard_map/panels/all_to_all | solution.py:20
  84.2 14.7 %all-to-all-done.3 = bf16[16,16,384]{2,1,0:T(8,128)(2,1)S(1)} async-done(((bf16[16,16,384]{2,1,0:T(8,128)(2,1)}), bf16[16,16,384]{2,1,0:T(8,128)(2,1)S(1)}, u32[]{:S(2)}, u32[]{:S(2)}) %all-to-all-start.3) | async-done | bytes 196640 | tf_op jit(solution)/shard_map/panels/all_to_all | solution.py:20
  98.9 12.5 %all_gather.14 = bf16[4,256,384]{2,1,0:T(8,128)(2,1)} all-gather(bf16[1,256,384]{2,1,0:T(8,128)(2,1)S(1)} %bitcast.70), channel_id=1, replica_groups=mesh['x'=4,'z'=16,'c'=2,'y'=4] {'x'}, dimensions={0}, use_global_device_ids=true | all-gather | bytes 983040 | tf_op jit(solution)/shard_map/panels/all_gather | solution.py:266
  111.4 26.0 %all-gather.2.cloned.1.call-done.row_ref.refs_0_.refs_1_.refs_2_ = bf16[1024,1536]{1,0:T(8,128)(2,1)} async-done(((bf16[64,1536]{1,0:T(8,128)(2,1)}), bf16[1024,1536]{1,0:T(8,128)(2,1)}) %all-gather.2.cloned.1.call-update) | async-done | bytes 3145744 | tf_op jit(solution)/shard_map/panels/all_gather | solution.py:259
  137.5 1.9 copy-done.1
  139.3 1.1 copy-done.3
  140.5 1.7 gram_half.3
  142.2 10.8 %collective-permute-start.1 = (bf16[4,3,64,384]{3,2,1,0:T(8,128)(2,1)S(1)}, bf16[4,3,64,384]{3,2,1,0:T(8,128)(2,1)S(1)}, u32[]{:S(2)}, u32[]{:S(2)}) collective-permute-start(bf16[4,3,64,384]{3,2,1,0:T(8,128)(2,1)S(1)} %gram_half.3), channel_id=1, source_target_pairs={{0,4},{4,0},{1,5},{5,1},{2,6},{6,2},{3,7},{7,3},{8,12},{12,8},{9,1... | collective-permute-start | bytes 1769480 | tf_op jit(solution)/shard_map/gram/ppermute | solution.py:14
  153.0 1.8 gram_half.2
  154.8 1.0 add_convert_fusion
  155.7 4.3 %all-to-all-start.4 = ((bf16[4,192,384]{2,1,0:T(8,128)(2,1)}), bf16[4,192,384]{2,1,0:T(8,128)(2,1)}, u32[]{:S(2)}, u32[]{:S(2)}) async-start(bf16[4,192,384]{2,1,0:T(8,128)(2,1)} %bitcast.66), calls=%async_computation.4 | async-start | bytes 1179648 | tf_op jit(solution)/shard_map/gram/all_to_all | solution.py:20
  160.5 9.7 %all-to-all-done.4.parts_ref = bf16[4,192,384]{2,1,0:T(8,128)(2,1)} async-done(((bf16[4,192,384]{2,1,0:T(8,128)(2,1)}), bf16[4,192,384]{2,1,0:T(8,128)(2,1)}, u32[]{:S(2)}, u32[]{:S(2)}) %all-to-all-start.4) | async-done | bytes 589856 | tf_op jit(solution)/shard_map/gram/all_to_all | solution.py:20
  170.2 1.2 amplitudes_of.1
  171.4 10.4 %all_gather.15 = bf16[4,192,384]{2,1,0:T(8,128)(2,1)S(1)} all-gather(bf16[1,192,384]{2,1,0:T(8,128)(2,1)S(1)} %bitcast.63), channel_id=1, replica_groups=mesh['x'=4,'z'=16,'c'=2,'y'=4] {'y'}, dimensions={0}, use_global_device_ids=true | all-gather | bytes 737280 | tf_op jit(solution)/shard_map/amplitudes/all_gather | solution.py:284
  181.8 6.1 %collective-permute-start.2 = (bf16[4,3,64,384]{3,2,1,0:T(8,128)(2,1)S(1)}, bf16[4,3,64,384]{3,2,1,0:T(8,128)(2,1)S(1)}, u32[]{:S(2)}, u32[]{:S(2)}) collective-permute-start(bf16[4,3,64,384]{3,2,1,0:T(8,128)(2,1)S(1)} %bitcast.60), channel_id=1, source_target_pairs={{0,4},{4,0},{1,5},{5,1},{2,6},{6,2},{3,7},{7,3},{8,12},{12,8},{9,1... | collective-permute-start | bytes 1769480 | tf_op jit(solution)/shard_map/amplitudes/ppermute | solution.py:14
  188.0 1.7 contract.2.refs_4_
  189.7 2.7 %contract.3 = bf16[4,16,16,384]{3,2,1,0:T(8,128)(2,1)} custom-call(s32[1]{0:T(128)} %bitcast.which_ref.side_ref, bf16[1024,1536]{1,0:T(8,128)(2,1)S(1)} %copy-done.2, bf16[1024,1536]{1,0:T(8,128)(2,1)S(1)} %copy-done.2, bf16[1024,1536]{1,0:T(8,128)(2,1)S(1)} %copy-done.2, bf16[4,3,64,384]{3,2,1,0:T(8,128)(2,1)S(1)} %collective-permute-done.2.refs_3_, ...), custom_call_target="tpu_custom_call" | custom-call | flops 603979776 | bytes 3735552 | tf_op jit(solution)/shard_map/gamma/contract/pallas_call | solution.py:153
  192.4 4.1 %all-to-all-start.5 = ((bf16[4,256,384]{2,1,0:T(8,128)(2,1)}), bf16[4,256,384]{2,1,0:T(8,128)(2,1)S(1)}, u32[]{:S(2)}, u32[]{:S(2)}) async-start(bf16[4,256,384]{2,1,0:T(8,128)(2,1)} %bitcast.64), calls=%async_computation.5 | async-start | bytes 1572864 | tf_op jit(solution)/shard_map/gamma/all_to_all | solution.py:20
  196.6 4.8 %collective-permute-start.3 = (bf16[3,3,64,128]{3,2,1,0:T(8,128)(2,1)S(1)}, bf16[3,3,64,128]{3,2,1,0:T(8,128)(2,1)S(1)}, u32[]{:S(2)}, u32[]{:S(2)}) collective-permute-start(bf16[3,3,64,128]{3,2,1,0:T(8,128)(2,1)S(1)} %get-tuple-element.15), channel_id=1, source_target_pairs={{0,32},{4,96},{8,40},{12,104},{16,48},{20,112},{24,56},{28,120},{3... | collective-permute-start | bytes 442376 | tf_op jit(solution)/shard_map/amplitudes/ppermute | solution.py:283
  201.4 7.1 %all-to-all-done.5 = bf16[4,256,384]{2,1,0:T(8,128)(2,1)S(1)} async-done(((bf16[4,256,384]{2,1,0:T(8,128)(2,1)}), bf16[4,256,384]{2,1,0:T(8,128)(2,1)S(1)}, u32[]{:S(2)}, u32[]{:S(2)}) %all-to-all-start.5) | async-done | bytes 786464 | tf_op jit(solution)/shard_map/gamma/all_to_all | solution.py:20
  208.5 0.8 reduce_sum.22
  209.3 8.9 %all-to-all-start.6 = ((bf16[16,16,384]{2,1,0:T(8,128)(2,1)}), bf16[16,16,384]{2,1,0:T(8,128)(2,1)S(1)}, u32[]{:S(2)}, u32[]{:S(2)}) async-start(bf16[16,16,384]{2,1,0:T(8,128)(2,1)} %bitcast.34), calls=%async_computation.6 | async-start | bytes 393216 | tf_op jit(solution)/shard_map/gamma/all_to_all | solution.py:20
  218.9 11.6 %all-to-all-done.6.value_ref = bf16[16,16,384]{2,1,0:T(8,128)(2,1)S(1)} async-done(((bf16[16,16,384]{2,1,0:T(8,128)(2,1)}), bf16[16,16,384]{2,1,0:T(8,128)(2,1)S(1)}, u32[]{:S(2)}, u32[]{:S(2)}) %all-to-all-start.6) | async-done | bytes 196640 | tf_op jit(solution)/shard_map/gamma/all_to_all | solution.py:20
  (46 shorter events, 5.8 us)
Async XLA Ops:
  7.2 152.9 %copy-start = (f32[2048]{0:T(1024)S(1)}, f32[2048]{0:T(1024)}, u32[]{:S(2)}) copy-start(f32[2048]{0:T(1024)} %param.10) | copy-start | bytes 24580
  7.2 0.7 copy-start.4
  7.9 17.6 %copy-start.5 = (bf16[64,3,640]{2,0,1:T(8,128)(2,1)S(1)}, bf16[64,3,640]{2,0,1:T(8,128)(2,1)}, u32[]{:S(2)}) copy-start(bf16[64,3,640]{2,0,1:T(8,128)(2,1)} %param.6) | copy-start | bytes 737284
  8.8 31.0 %all-to-all-start = ((bf16[16,16,640]{2,1,0:T(8,128)(2,1)}), bf16[16,16,640]{2,1,0:T(8,128)(2,1)S(1)}, u32[]{:S(2)}, u32[]{:S(2)}) async-start(bf16[16,16,640]{2,1,0:T(8,128)(2,1)} %spread.1), calls=%async_computation | async-start | bytes 655360 | tf_op jit(solution)/shard_map/transform/all_to_all | solution.py:20
  24.6 112.9 %all-gather.2.cloned.1.call-start = ((), (), s32[]{:S(2)}) async-start(), calls=%async_computation.7 | async-start | bytes 3342336 | tf_op jit(solution)/shard_map/panels/all_gather | solution.py:259
  39.8 9.6 %collective-permute-start = (bf16[16,16,640]{2,1,0:T(8,128)(2,1)S(1)}, bf16[16,16,640]{2,1,0:T(8,128)(2,1)S(1)}, u32[]{:S(2)}, u32[]{:S(2)}) collective-permute-start(bf16[16,16,640]{2,1,0:T(8,128)(2,1)S(1)} %all-to-all-done), channel_id=1, source_target_pairs={{0,4},{4,0},{1,5},{5,1},{2,6},{6,2},{3,7},{7,3},{8,12},{12,8},{9,1... | collective-permute-start | bytes 983048 | tf_op jit(solution)/shard_map/transform/ppermute | solution.py:14
  77.5 21.3 %all-to-all-start.3 = ((bf16[16,16,384]{2,1,0:T(8,128)(2,1)}), bf16[16,16,384]{2,1,0:T(8,128)(2,1)S(1)}, u32[]{:S(2)}, u32[]{:S(2)}) async-start(bf16[16,16,384]{2,1,0:T(8,128)(2,1)} %pad_maximum_fusion.1), calls=%async_computation.3 | async-start | bytes 393216 | tf_op jit(solution)/shard_map/panels/all_to_all | solution.py:20
  137.5 1.9 copy-start.1
  139.3 1.1 copy-start.3
  140.5 12.5 %copy-start.2 = (bf16[1024,1536]{1,0:T(8,128)(2,1)S(1)}, bf16[1024,1536]{1,0:T(8,128)(2,1)}, u32[]{:S(2)}) copy-start(bf16[1024,1536]{1,0:T(8,128)(2,1)} %all-gather.2.cloned.1.call-done.row_ref.refs_0_.refs_1_.refs_2_) | copy-start | bytes 9437188
  142.2 12.6 %collective-permute-start.1 = (bf16[4,3,64,384]{3,2,1,0:T(8,128)(2,1)S(1)}, bf16[4,3,64,384]{3,2,1,0:T(8,128)(2,1)S(1)}, u32[]{:S(2)}, u32[]{:S(2)}) collective-permute-start(bf16[4,3,64,384]{3,2,1,0:T(8,128)(2,1)S(1)} %gram_half.3), channel_id=1, source_target_pairs={{0,4},{4,0},{1,5},{5,1},{2,6},{6,2},{3,7},{7,3},{8,12},{12,8},{9,1... | collective-permute-start | bytes 1769480 | tf_op jit(solution)/shard_map/gram/ppermute | solution.py:14
  155.7 4.6 %copy-start.6 = (f32[512]{0:T(512)S(1)}, f32[512]{0:T(512)}, u32[]{:S(2)}) copy-start(f32[512]{0:T(512)} %param.9) | copy-start | bytes 6148
  155.7 4.6 %copy-start.7 = (s32[3]{0:T(128)S(1)}, s32[3]{0:T(128)}, u32[]{:S(2)}) copy-start(s32[3]{0:T(128)} %param.11) | copy-start | bytes 40
  155.7 14.5 %all-to-all-start.4 = ((bf16[4,192,384]{2,1,0:T(8,128)(2,1)}), bf16[4,192,384]{2,1,0:T(8,128)(2,1)}, u32[]{:S(2)}, u32[]{:S(2)}) async-start(bf16[4,192,384]{2,1,0:T(8,128)(2,1)} %bitcast.66), calls=%async_computation.4 | async-start | bytes 1179648 | tf_op jit(solution)/shard_map/gram/all_to_all | solution.py:20
  181.8 7.9 %collective-permute-start.2 = (bf16[4,3,64,384]{3,2,1,0:T(8,128)(2,1)S(1)}, bf16[4,3,64,384]{3,2,1,0:T(8,128)(2,1)S(1)}, u32[]{:S(2)}, u32[]{:S(2)}) collective-permute-start(bf16[4,3,64,384]{3,2,1,0:T(8,128)(2,1)S(1)} %bitcast.60), channel_id=1, source_target_pairs={{0,4},{4,0},{1,5},{5,1},{2,6},{6,2},{3,7},{7,3},{8,12},{12,8},{9,1... | collective-permute-start | bytes 1769480 | tf_op jit(solution)/shard_map/amplitudes/ppermute | solution.py:14
  192.4 16.0 %all-to-all-start.5 = ((bf16[4,256,384]{2,1,0:T(8,128)(2,1)}), bf16[4,256,384]{2,1,0:T(8,128)(2,1)S(1)}, u32[]{:S(2)}, u32[]{:S(2)}) async-start(bf16[4,256,384]{2,1,0:T(8,128)(2,1)} %bitcast.64), calls=%async_computation.5 | async-start | bytes 1572864 | tf_op jit(solution)/shard_map/gamma/all_to_all | solution.py:20
  196.6 12.7 %collective-permute-start.3 = (bf16[3,3,64,128]{3,2,1,0:T(8,128)(2,1)S(1)}, bf16[3,3,64,128]{3,2,1,0:T(8,128)(2,1)S(1)}, u32[]{:S(2)}, u32[]{:S(2)}) collective-permute-start(bf16[3,3,64,128]{3,2,1,0:T(8,128)(2,1)S(1)} %get-tuple-element.15), channel_id=1, source_target_pairs={{0,32},{4,96},{8,40},{12,104},{16,48},{20,112},{24,56},{28,120},{3... | collective-permute-start | bytes 442376 | tf_op jit(solution)/shard_map/amplitudes/ppermute | solution.py:283
  209.3 21.3 %all-to-all-start.6 = ((bf16[16,16,384]{2,1,0:T(8,128)(2,1)}), bf16[16,16,384]{2,1,0:T(8,128)(2,1)S(1)}, u32[]{:S(2)}, u32[]{:S(2)}) async-start(bf16[16,16,384]{2,1,0:T(8,128)(2,1)} %bitcast.34), calls=%async_computation.6 | async-start | bytes 393216 | tf_op jit(solution)/shard_map/gamma/all_to_all | solution.py:20
Sparse Core Ops, SparseCore 0:
  67.5 69.9 all-gather.1

commit v10 on v8

--- a/solution.py
+++ b/solution.py
@@ -36,7 +36,7 @@
     return pl.pallas_call(
         body,
         out_shape=pltpu.HBM((copies,) + value.shape, value.dtype),
-        in_specs=[pl.BlockSpec(memory_space=pltpu.VMEM)],
+        in_specs=[pl.BlockSpec(memory_space=pltpu.HBM)],
         out_specs=pl.BlockSpec(memory_space=pltpu.HBM),
         scratch_shapes=[pltpu.SemaphoreType.DMA((copies,))],
         compiler_params=pltpu.CompilerParams(vmem_limit_bytes=12 * 1024 * 1024),
@@ -212,7 +212,7 @@
     slot_energy = jnp.sum(onehot * occ_energy[None, :], axis=1)
 
     with jax.named_scope("transform"):
-        coef = exchange(spread(coef_virt, nz), "z")
+        coef = exchange(spread(pltpu.with_memory_space_constraint(coef_virt, pltpu.HBM), nz), "z")
         expanded = jnp.repeat(jnp.repeat(screen, 32, axis=0), 128, axis=1).astype(BF)
         masked = half_ints * expanded[:, None, :]
         masked = masked.reshape(ny, r, nocc, ao_part).transpose(0, 2, 1, 3)
@@ -235,7 +235,7 @@
         )
         col = exchange(col, "z")
         col = lax.all_gather(col.reshape(nz * r, nocc * narrow), "x", axis=0)
-        col = col.reshape(nx, nz, r, nocc * narrow)
+        col = pltpu.with_memory_space_constraint(col.reshape(nx, nz, r, nocc * narrow), pltpu.HBM)
 
     with jax.named_scope("gram"):
         other = swap_cores(gram_half(row, col, 1 - c, nocc, ny, BF))

time: 242 us -> 253 us (1.045)
  the two profiles are of different devices: /device:TPU:2 before, /device:TPU:1 now
where the time goes in v10:
time: 253 us; the launch traced here: 248 us
  waiting for transfers between devices  71.7 us (28%)
  starting transfers between devices  69.6 us (28%)
  blocking collectives  60.6 us (24%)
  Pallas kernels  23.3 us (9%)
  between operations  14.4 us (6%)
  other arithmetic  5.11 us (2%)
  local copies, waits for them, and re-layouts  2.9 us (1%)
    all_to_all x5, waiting for transfers between devices, exchange(): value = lax.all_to_all(value, axis, split_axis=0, concat_axis=0, tiled=True)  44.2 us
    all_to_all x5, starting transfers between devices, exchange(): value = lax.all_to_all(value, axis, split_axis=0, concat_axis=0, tiled=True)  40.3 us
    all_gather x1, waiting for transfers between devices, local(): lax.all_gather(row.reshape(nx * r, nocc * wide), 'z', axis=0, tiled=True)  26.2 us
    ppermute x3, starting transfers between devices, swap_cores(): return lax.ppermute(value, 'c', [(0, 1), (1, 0)])  24.4 us
    all_to_all x2, blocking collectives, exchange(): value = lax.all_to_all(value, axis, split_axis=0, concat_axis=0, tiled=True)  24.4 us
    all_gather x1, blocking collectives, local(): masked = lax.all_gather(masked.reshape(-1, ao_part), 'x', axis=0)  13.2 us
    all_gather x1, blocking collectives, local(): col = lax.all_gather(col.reshape(nz * r, nocc * narrow), 'x', axis=0)  12.5 us
    pallas_call x1, Pallas kernels, spread(): pl.pallas_call(body, out_shape=pltpu.HBM((copies,) + value.shape, value.d...  11.2 us
  transfers between devices with their start and end apart: 10, of which 7 were waited for; matrix products, arithmetic and copies ran while one was open for 2% of the time, Pallas kernels for 2%

profile of v10, /device:TPU:1, one launch (start us, length us, event | category | flops | bytes accessed | tf_op | source)
XLA Modules:
  0.0 248.4 jit_solution(8005645108936760355)
XLA Ops:
  7.2 11.2 %spread.1 = bf16[16,16,640]{2,1,0:T(8,128)(2,1)} custom-call(bf16[16,640]{1,0:T(8,128)(2,1)} %value_ref.1), custom_call_target="tpu_custom_call" | custom-call | tf_op jit(solution)/shard_map/transform/spread/pallas_call | solution.py:36
  18.4 15.8 %all-to-all-start = ((bf16[16,16,640]{2,1,0:T(8,128)(2,1)}), bf16[16,16,640]{2,1,0:T(8,128)(2,1)S(1)}, u32[]{:S(2)}, u32[]{:S(2)}) async-start(bf16[16,16,640]{2,1,0:T(8,128)(2,1)} %spread.1), calls=%async_computation | async-start | bytes 655360 | tf_op jit(solution)/shard_map/transform/all_to_all | solution.py:20
  35.1 13.2 %all_gather.12 = bf16[4,192,640]{2,1,0:T(8,128)(2,1)S(1)} all-gather(bf16[1,192,640]{2,1,0:T(8,128)(2,1)S(1)} %bitcast.72), channel_id=1, replica_groups=mesh['x'=4,'z'=16,'c'=2,'y'=4] {'x'}, dimensions={0}, use_global_device_ids=true | all-gather | bytes 1228800 | tf_op jit(solution)/shard_map/transform/all_gather | solution.py:219
  48.4 1.0 all-to-all-done
  49.4 8.4 %collective-permute-start = (bf16[16,16,640]{2,1,0:T(8,128)(2,1)S(1)}, bf16[16,16,640]{2,1,0:T(8,128)(2,1)S(1)}, u32[]{:S(2)}, u32[]{:S(2)}) collective-permute-start(bf16[16,16,640]{2,1,0:T(8,128)(2,1)S(1)} %all-to-all-done), channel_id=1, source_target_pairs={{0,4},{4,0},{1,5},{5,1},{2,6},{6,2},{3,7},{7,3},{8,12},{12,8},{9,1... | collective-permute-start | bytes 983048 | tf_op jit(solution)/shard_map/transform/ppermute | solution.py:14
  57.8 1.2 collective-permute-done
  59.2 0.8 fusion
  60.1 15.4 %all_to_all.57 = bf16[4,192,512]{2,1,0:T(8,128)(2,1)S(1)} all-to-all(bf16[4,192,512]{2,1,0:T(8,128)(2,1)S(1)} %bitcast.68), channel_id=1, replica_groups=mesh['x'=4,'z'=16,'c'=2,'y'=4] {'y'}, dimensions={0} | all-to-all | bytes 1572864 | tf_op jit(solution)/shard_map/transform/all_to_all | solution.py:20
  76.4 9.0 %all_to_all.58 = bf16[4,48,512]{2,1,0:T(8,128)(2,1)S(1)} all-to-all(bf16[4,48,512]{2,1,0:T(8,128)(2,1)S(1)} %bitcast.71), channel_id=1, replica_groups=mesh['x'=4,'z'=16,'c'=2,'y'=4] {'x'}, dimensions={0} | all-to-all | bytes 393216 | tf_op jit(solution)/shard_map/panels/all_to_all | solution.py:20
  86.6 6.7 %all-to-all-start.3 = ((bf16[16,16,384]{2,1,0:T(8,128)(2,1)}), bf16[16,16,384]{2,1,0:T(8,128)(2,1)S(1)}, u32[]{:S(2)}, u32[]{:S(2)}) async-start(bf16[16,16,384]{2,1,0:T(8,128)(2,1)} %pad_maximum_fusion.2), calls=%async_computation.3 | async-start | bytes 393216 | tf_op jit(solution)/shard_map/panels/all_to_all | solution.py:20
  93.3 14.6 %all-to-all-done.3 = bf16[16,16,384]{2,1,0:T(8,128)(2,1)S(1)} async-done(((bf16[16,16,384]{2,1,0:T(8,128)(2,1)}), bf16[16,16,384]{2,1,0:T(8,128)(2,1)S(1)}, u32[]{:S(2)}, u32[]{:S(2)}) %all-to-all-start.3) | async-done | bytes 196640 | tf_op jit(solution)/shard_map/panels/all_to_all | solution.py:20
  107.9 12.5 %all_gather.14 = bf16[4,256,384]{2,1,0:T(8,128)(2,1)} all-gather(bf16[1,256,384]{2,1,0:T(8,128)(2,1)S(1)} %bitcast.75), channel_id=1, replica_groups=mesh['x'=4,'z'=16,'c'=2,'y'=4] {'x'}, dimensions={0}, use_global_device_ids=true | all-gather | bytes 983040 | tf_op jit(solution)/shard_map/panels/all_gather | solution.py:237
  120.4 26.2 %all-gather.2.cloned.1.call-done.row_ref.refs_0_.refs_1_.refs_2_ = bf16[1024,1536]{1,0:T(8,128)(2,1)} async-done(((bf16[64,1536]{1,0:T(8,128)(2,1)}), bf16[1024,1536]{1,0:T(8,128)(2,1)}) %all-gather.2.cloned.1.call-update) | async-done | bytes 3145744 | tf_op jit(solution)/shard_map/panels/all_gather | solution.py:230
  146.6 1.9 copy-done.1
  148.5 2.9 %gram_half.3 = bf16[4,3,64,384]{3,2,1,0:T(8,128)(2,1)S(1)} custom-call(s32[1]{0:T(128)} %bitcast.which_ref.side_ref, bf16[1024,1536]{1,0:T(8,128)(2,1)S(1)} %copy-done.1, bf16[4,16,16,384]{3,2,1,0:T(8,128)(2,1)} %bitcast.65), custom_call_target="tpu_custom_call" | custom-call | flops 603979776 | bytes 3538944 | tf_op jit(solution)/shard_map/gram/gram_half/pallas_call | solution.py:65
  151.4 10.6 %collective-permute-start.1 = (bf16[4,3,64,384]{3,2,1,0:T(8,128)(2,1)S(1)}, bf16[4,3,64,384]{3,2,1,0:T(8,128)(2,1)S(1)}, u32[]{:S(2)}, u32[]{:S(2)}) collective-permute-start(bf16[4,3,64,384]{3,2,1,0:T(8,128)(2,1)S(1)} %gram_half.3), channel_id=1, source_target_pairs={{0,4},{4,0},{1,5},{5,1},{2,6},{6,2},{3,7},{7,3},{8,12},{12,8},{9,1... | collective-permute-start | bytes 1769480 | tf_op jit(solution)/shard_map/gram/ppermute | solution.py:14
  162.1 2.8 %gram_half.2 = f32[4,3,64,384]{3,2,1,0:T(8,128)S(1)} custom-call(s32[1]{0:T(128)} %bitcast.19.which_ref.side_ref, bf16[1024,1536]{1,0:T(8,128)(2,1)S(1)} %copy-done.2, bf16[4,16,16,384]{3,2,1,0:T(8,128)(2,1)} %bitcast.66), custom_call_target="tpu_custom_call" | custom-call | flops 603979776 | bytes 3538944 | tf_op jit(solution)/shard_map/gram/gram_half/pallas_call | solution.py:65
  164.9 1.0 add_convert_fusion
  165.9 4.3 %all-to-all-start.4 = ((bf16[4,192,384]{2,1,0:T(8,128)(2,1)}), bf16[4,192,384]{2,1,0:T(8,128)(2,1)}, u32[]{:S(2)}, u32[]{:S(2)}) async-start(bf16[4,192,384]{2,1,0:T(8,128)(2,1)} %bitcast.69), calls=%async_computation.4 | async-start | bytes 1179648 | tf_op jit(solution)/shard_map/gram/all_to_all | solution.py:20
  170.7 9.9 %all-to-all-done.4.parts_ref = bf16[4,192,384]{2,1,0:T(8,128)(2,1)} async-done(((bf16[4,192,384]{2,1,0:T(8,128)(2,1)}), bf16[4,192,384]{2,1,0:T(8,128)(2,1)}, u32[]{:S(2)}, u32[]{:S(2)}) %all-to-all-start.4) | async-done | bytes 589856 | tf_op jit(solution)/shard_map/gram/all_to_all | solution.py:20
  180.6 1.2 amplitudes_of.1
  181.8 10.5 %all_gather.15 = bf16[4,192,384]{2,1,0:T(8,128)(2,1)S(1)} all-gather(bf16[1,192,384]{2,1,0:T(8,128)(2,1)S(1)} %bitcast.64), channel_id=1, replica_groups=mesh['x'=4,'z'=16,'c'=2,'y'=4] {'y'}, dimensions={0}, use_global_device_ids=true | all-gather | bytes 737280 | tf_op jit(solution)/shard_map/amplitudes/all_gather | solution.py:255
  192.3 5.4 %collective-permute-start.2 = (bf16[4,3,64,384]{3,2,1,0:T(8,128)(2,1)S(1)}, bf16[4,3,64,384]{3,2,1,0:T(8,128)(2,1)S(1)}, u32[]{:S(2)}, u32[]{:S(2)}) collective-permute-start(bf16[4,3,64,384]{3,2,1,0:T(8,128)(2,1)S(1)} %bitcast.62), channel_id=1, source_target_pairs={{0,4},{4,0},{1,5},{5,1},{2,6},{6,2},{3,7},{7,3},{8,12},{12,8},{9,1... | collective-permute-start | bytes 1769480 | tf_op jit(solution)/shard_map/amplitudes/ppermute | solution.py:14
  197.7 1.7 contract.2.refs_4_
  199.4 2.7 %contract.3 = bf16[4,16,16,384]{3,2,1,0:T(8,128)(2,1)} custom-call(s32[1]{0:T(128)} %bitcast.which_ref.side_ref, bf16[1024,1536]{1,0:T(8,128)(2,1)S(1)} %copy-done.2, bf16[1024,1536]{1,0:T(8,128)(2,1)S(1)} %copy-done.2, bf16[1024,1536]{1,0:T(8,128)(2,1)S(1)} %copy-done.2, bf16[4,3,64,384]{3,2,1,0:T(8,128)(2,1)S(1)} %collective-permute-done.2.refs_3_, ...), custom_call_target="tpu_custom_call" | custom-call | flops 603979776 | bytes 3735552 | tf_op jit(solution)/shard_map/gamma/contract/pallas_call | solution.py:123
  202.1 4.8 %all-to-all-start.5 = ((bf16[4,256,384]{2,1,0:T(8,128)(2,1)}), bf16[4,256,384]{2,1,0:T(8,128)(2,1)S(1)}, u32[]{:S(2)}, u32[]{:S(2)}) async-start(bf16[4,256,384]{2,1,0:T(8,128)(2,1)} %bitcast.67), calls=%async_computation.5 | async-start | bytes 1572864 | tf_op jit(solution)/shard_map/gamma/all_to_all | solution.py:20
  206.9 4.8 %collective-permute-start.3 = (bf16[3,3,64,128]{3,2,1,0:T(8,128)(2,1)S(1)}, bf16[3,3,64,128]{3,2,1,0:T(8,128)(2,1)S(1)}, u32[]{:S(2)}, u32[]{:S(2)}) collective-permute-start(bf16[3,3,64,128]{3,2,1,0:T(8,128)(2,1)S(1)} %get-tuple-element.11), channel_id=1, source_target_pairs={{0,32},{4,96},{8,40},{12,104},{16,48},{20,112},{24,56},{28,120},{3... | collective-permute-start | bytes 442376 | tf_op jit(solution)/shard_map/amplitudes/ppermute | solution.py:254
  211.7 7.1 %all-to-all-done.5 = bf16[4,256,384]{2,1,0:T(8,128)(2,1)S(1)} async-done(((bf16[4,256,384]{2,1,0:T(8,128)(2,1)}), bf16[4,256,384]{2,1,0:T(8,128)(2,1)S(1)}, u32[]{:S(2)}, u32[]{:S(2)}) %all-to-all-start.5) | async-done | bytes 786464 | tf_op jit(solution)/shard_map/gamma/all_to_all | solution.py:20
  218.8 0.8 reduce_sum.35
  219.7 8.8 %all-to-all-start.6 = ((bf16[16,16,384]{2,1,0:T(8,128)(2,1)}), bf16[16,16,384]{2,1,0:T(8,128)(2,1)S(1)}, u32[]{:S(2)}, u32[]{:S(2)}) async-start(bf16[16,16,384]{2,1,0:T(8,128)(2,1)} %bitcast.38), calls=%async_computation.6 | async-start | bytes 393216 | tf_op jit(solution)/shard_map/gamma/all_to_all | solution.py:20
  228.5 0.7 convert_bitcast_fusion
  229.2 11.6 %all-to-all-done.6.value_ref = bf16[16,16,384]{2,1,0:T(8,128)(2,1)S(1)} async-done(((bf16[16,16,384]{2,1,0:T(8,128)(2,1)}), bf16[16,16,384]{2,1,0:T(8,128)(2,1)S(1)}, u32[]{:S(2)}, u32[]{:S(2)}) %all-to-all-start.6) | async-done | bytes 196640 | tf_op jit(solution)/shard_map/gamma/all_to_all | solution.py:20
  (44 shorter events, 4.4 us)
Async XLA Ops:
  7.2 163.1 %copy-start = (f32[2048]{0:T(1024)S(1)}, f32[2048]{0:T(1024)}, u32[]{:S(2)}) copy-start(f32[2048]{0:T(1024)} %param.10) | copy-start | bytes 24580
  7.2 27.9 %copy-start.3 = (bf16[64,3,640]{2,0,1:T(8,128)(2,1)S(1)}, bf16[64,3,640]{2,0,1:T(8,128)(2,1)}, u32[]{:S(2)}) copy-start(bf16[64,3,640]{2,0,1:T(8,128)(2,1)} %param.6) | copy-start | bytes 737284
  18.4 31.0 %all-to-all-start = ((bf16[16,16,640]{2,1,0:T(8,128)(2,1)}), bf16[16,16,640]{2,1,0:T(8,128)(2,1)S(1)}, u32[]{:S(2)}, u32[]{:S(2)}) async-start(bf16[16,16,640]{2,1,0:T(8,128)(2,1)} %spread.1), calls=%async_computation | async-start | bytes 655360 | tf_op jit(solution)/shard_map/transform/all_to_all | solution.py:20
  34.1 112.4 %all-gather.2.cloned.1.call-start = ((), (), s32[]{:S(2)}) async-start(), calls=%async_computation.7 | async-start | bytes 3342336 | tf_op jit(solution)/shard_map/panels/all_gather | solution.py:230
  49.4 9.6 %collective-permute-start = (bf16[16,16,640]{2,1,0:T(8,128)(2,1)S(1)}, bf16[16,16,640]{2,1,0:T(8,128)(2,1)S(1)}, u32[]{:S(2)}, u32[]{:S(2)}) collective-permute-start(bf16[16,16,640]{2,1,0:T(8,128)(2,1)S(1)} %all-to-all-done), channel_id=1, source_target_pairs={{0,4},{4,0},{1,5},{5,1},{2,6},{6,2},{3,7},{7,3},{8,12},{12,8},{9,1... | collective-permute-start | bytes 983048 | tf_op jit(solution)/shard_map/transform/ppermute | solution.py:14
  86.6 21.3 %all-to-all-start.3 = ((bf16[16,16,384]{2,1,0:T(8,128)(2,1)}), bf16[16,16,384]{2,1,0:T(8,128)(2,1)S(1)}, u32[]{:S(2)}, u32[]{:S(2)}) async-start(bf16[16,16,384]{2,1,0:T(8,128)(2,1)} %pad_maximum_fusion.2), calls=%async_computation.3 | async-start | bytes 393216 | tf_op jit(solution)/shard_map/panels/all_to_all | solution.py:20
  146.6 1.9 copy-start.1
  148.5 13.6 %copy-start.2 = (bf16[1024,1536]{1,0:T(8,128)(2,1)S(1)}, bf16[1024,1536]{1,0:T(8,128)(2,1)}, u32[]{:S(2)}) copy-start(bf16[1024,1536]{1,0:T(8,128)(2,1)} %all-gather.2.cloned.1.call-done.row_ref.refs_0_.refs_1_.refs_2_) | copy-start | bytes 9437188
  151.4 13.5 %collective-permute-start.1 = (bf16[4,3,64,384]{3,2,1,0:T(8,128)(2,1)S(1)}, bf16[4,3,64,384]{3,2,1,0:T(8,128)(2,1)S(1)}, u32[]{:S(2)}, u32[]{:S(2)}) collective-permute-start(bf16[4,3,64,384]{3,2,1,0:T(8,128)(2,1)S(1)} %gram_half.3), channel_id=1, source_target_pairs={{0,4},{4,0},{1,5},{5,1},{2,6},{6,2},{3,7},{7,3},{8,12},{12,8},{9,1... | collective-permute-start | bytes 1769480 | tf_op jit(solution)/shard_map/gram/ppermute | solution.py:14
  165.9 4.6 %copy-start.4 = (f32[512]{0:T(512)S(1)}, f32[512]{0:T(512)}, u32[]{:S(2)}) copy-start(f32[512]{0:T(512)} %param.9) | copy-start | bytes 6148
  165.9 4.6 %copy-start.5 = (s32[3]{0:T(128)S(1)}, s32[3]{0:T(128)}, u32[]{:S(2)}) copy-start(s32[3]{0:T(128)} %param.11) | copy-start | bytes 40
  165.9 14.7 %all-to-all-start.4 = ((bf16[4,192,384]{2,1,0:T(8,128)(2,1)}), bf16[4,192,384]{2,1,0:T(8,128)(2,1)}, u32[]{:S(2)}, u32[]{:S(2)}) async-start(bf16[4,192,384]{2,1,0:T(8,128)(2,1)} %bitcast.69), calls=%async_computation.4 | async-start | bytes 1179648 | tf_op jit(solution)/shard_map/gram/all_to_all | solution.py:20
  192.3 7.1 %collective-permute-start.2 = (bf16[4,3,64,384]{3,2,1,0:T(8,128)(2,1)S(1)}, bf16[4,3,64,384]{3,2,1,0:T(8,128)(2,1)S(1)}, u32[]{:S(2)}, u32[]{:S(2)}) collective-permute-start(bf16[4,3,64,384]{3,2,1,0:T(8,128)(2,1)S(1)} %bitcast.62), channel_id=1, source_target_pairs={{0,4},{4,0},{1,5},{5,1},{2,6},{6,2},{3,7},{7,3},{8,12},{12,8},{9,1... | collective-permute-start | bytes 1769480 | tf_op jit(solution)/shard_map/amplitudes/ppermute | solution.py:14
  202.1 16.7 %all-to-all-start.5 = ((bf16[4,256,384]{2,1,0:T(8,128)(2,1)}), bf16[4,256,384]{2,1,0:T(8,128)(2,1)S(1)}, u32[]{:S(2)}, u32[]{:S(2)}) async-start(bf16[4,256,384]{2,1,0:T(8,128)(2,1)} %bitcast.67), calls=%async_computation.5 | async-start | bytes 1572864 | tf_op jit(solution)/shard_map/gamma/all_to_all | solution.py:20
  206.9 12.7 %collective-permute-start.3 = (bf16[3,3,64,128]{3,2,1,0:T(8,128)(2,1)S(1)}, bf16[3,3,64,128]{3,2,1,0:T(8,128)(2,1)S(1)}, u32[]{:S(2)}, u32[]{:S(2)}) collective-permute-start(bf16[3,3,64,128]{3,2,1,0:T(8,128)(2,1)S(1)} %get-tuple-element.11), channel_id=1, source_target_pairs={{0,32},{4,96},{8,40},{12,104},{16,48},{20,112},{24,56},{28,120},{3... | collective-permute-start | bytes 442376 | tf_op jit(solution)/shard_map/amplitudes/ppermute | solution.py:254
  219.7 21.1 %all-to-all-start.6 = ((bf16[16,16,384]{2,1,0:T(8,128)(2,1)}), bf16[16,16,384]{2,1,0:T(8,128)(2,1)S(1)}, u32[]{:S(2)}, u32[]{:S(2)}) async-start(bf16[16,16,384]{2,1,0:T(8,128)(2,1)} %bitcast.38), calls=%async_computation.6 | async-start | bytes 393216 | tf_op jit(solution)/shard_map/gamma/all_to_all | solution.py:20
Sparse Core Ops, SparseCore 0:
  76.5 70.0 all-gather.1

commit v11 on v8

--- a/solution.py
+++ b/solution.py
@@ -236,6 +236,13 @@
         col = exchange(col, "z")
         col = lax.all_gather(col.reshape(nz * r, nocc * narrow), "x", axis=0)
         col = col.reshape(nx, nz, r, nocc * narrow)
+        row_energy = lax.dynamic_slice_in_dim(virt_energy, x * wide + c * half + y * share, share, 0)
+        col_energy = lax.dynamic_slice_in_dim(virt_energy, ((zl + nl // 2) % nl * 2 + zh) * narrow, narrow, 0)
+        row_energy = jnp.broadcast_to(row_energy[:, None], (share, narrow))
+        col_energy = col_energy[None, :]
+        col, slot_energy, row_energy, col_energy = lax.optimization_barrier(
+            (col, slot_energy, row_energy, col_energy)
+        )
 
     with jax.named_scope("gram"):
         other = swap_cores(gram_half(row, col, 1 - c, nocc, ny, BF))
@@ -243,9 +250,7 @@
         gram = exchange(gram.astype(BF).reshape(ny, nocc * share, nocc * narrow), "y")
 
     with jax.named_scope("amplitudes"):
-        row_energy = lax.dynamic_slice_in_dim(virt_energy, x * wide + c * half + y * share, share, 0)
-        col_energy = lax.dynamic_slice_in_dim(virt_energy, ((zl + nl // 2) % nl * 2 + zh) * narrow, narrow, 0)
-        amps, mixed = amplitudes_of(gram, slot_energy, row_energy[:, None], col_energy[None, :])
+        amps, mixed = amplitudes_of(gram, slot_energy, row_energy, col_energy)
         swap = []
         for h in range(2):
             for l in range(nl):

time: 242 us -> 239 us (0.988)
  the two profiles are of different devices: /device:TPU:2 before, /device:TPU:1 now
where the time goes in v11:
time: 239 us; the launch traced here: 234 us
  blocking collectives  73.4 us (31%)
  starting transfers between devices  66.2 us (28%)
  waiting for transfers between devices  60.2 us (25%)
  between operations  14.4 us (6%)
  Pallas kernels  10.1 us (4%)
  local copies, waits for them, and re-layouts  4.96 us (2%)
  other arithmetic  4.27 us (2%)
    all_to_all x3, blocking collectives, exchange(): value = lax.all_to_all(value, axis, split_axis=0, concat_axis=0, tiled=True)  37.6 us
    all_to_all x4, starting transfers between devices, exchange(): value = lax.all_to_all(value, axis, split_axis=0, concat_axis=0, tiled=True)  35.4 us
    all_to_all x4, waiting for transfers between devices, exchange(): value = lax.all_to_all(value, axis, split_axis=0, concat_axis=0, tiled=True)  32 us
    all_gather x1, waiting for transfers between devices, local(): lax.all_gather(row.reshape(nx * r, nocc * wide), 'z', axis=0, tiled=True)  27 us
    ppermute x3, starting transfers between devices, swap_cores(): return lax.ppermute(value, 'c', [(0, 1), (1, 0)])  25.1 us
    all_gather x1, blocking collectives, local(): masked = lax.all_gather(masked.reshape(-1, ao_part), 'x', axis=0)  13.2 us
    all_gather x1, blocking collectives, local(): col = lax.all_gather(col.reshape(nz * r, nocc * narrow), 'x', axis=0)  11.6 us
    all_gather x1, blocking collectives, local(): lax.all_gather(mixed.reshape(nocc * share, nocc * narrow), 'y', axis=0)  11 us
  transfers between devices with their start and end apart: 9, of which 6 were waited for; matrix products, arithmetic and copies ran while one was open for 2% of the time, Pallas kernels for 1%

profile of v11, /device:TPU:1, one launch (start us, length us, event | category | flops | bytes accessed | tf_op | source)
XLA Modules:
  0.0 234.3 jit_solution(13375725159407203850)
XLA Ops:
  7.2 0.7 copy-done.2
  7.9 0.9 spread.1
  8.8 15.8 %all-to-all-start = ((bf16[16,16,640]{2,1,0:T(8,128)(2,1)}), bf16[16,16,640]{2,1,0:T(8,128)(2,1)S(1)}, u32[]{:S(2)}, u32[]{:S(2)}) async-start(bf16[16,16,640]{2,1,0:T(8,128)(2,1)} %spread.1), calls=%async_computation | async-start | bytes 655360 | tf_op jit(solution)/shard_map/transform/all_to_all | solution.py:20
  25.5 13.2 %all_gather.12 = bf16[4,192,640]{2,1,0:T(8,128)(2,1)S(1)} all-gather(bf16[1,192,640]{2,1,0:T(8,128)(2,1)S(1)} %bitcast.70), channel_id=1, replica_groups=mesh['x'=4,'z'=16,'c'=2,'y'=4] {'x'}, dimensions={0}, use_global_device_ids=true | all-gather | bytes 1228800 | tf_op jit(solution)/shard_map/transform/all_gather | solution.py:219
  38.7 1.0 all-to-all-done
  39.8 8.4 %collective-permute-start = (bf16[16,16,640]{2,1,0:T(8,128)(2,1)S(1)}, bf16[16,16,640]{2,1,0:T(8,128)(2,1)S(1)}, u32[]{:S(2)}, u32[]{:S(2)}) collective-permute-start(bf16[16,16,640]{2,1,0:T(8,128)(2,1)S(1)} %all-to-all-done), channel_id=1, source_target_pairs={{0,4},{4,0},{1,5},{5,1},{2,6},{6,2},{3,7},{7,3},{8,12},{12,8},{9,1... | collective-permute-start | bytes 983048 | tf_op jit(solution)/shard_map/transform/ppermute | solution.py:14
  48.2 1.2 collective-permute-done
  49.6 0.8 fusion
  50.5 15.4 %all_to_all.57 = bf16[4,192,512]{2,1,0:T(8,128)(2,1)S(1)} all-to-all(bf16[4,192,512]{2,1,0:T(8,128)(2,1)S(1)} %bitcast.66), channel_id=1, replica_groups=mesh['x'=4,'z'=16,'c'=2,'y'=4] {'y'}, dimensions={0} | all-to-all | bytes 1572864 | tf_op jit(solution)/shard_map/transform/all_to_all | solution.py:20
  66.8 9.0 %all_to_all.58 = bf16[4,48,512]{2,1,0:T(8,128)(2,1)S(1)} all-to-all(bf16[4,48,512]{2,1,0:T(8,128)(2,1)S(1)} %bitcast.69), channel_id=1, replica_groups=mesh['x'=4,'z'=16,'c'=2,'y'=4] {'x'}, dimensions={0} | all-to-all | bytes 393216 | tf_op jit(solution)/shard_map/panels/all_to_all | solution.py:20
  77.0 6.7 %all-to-all-start.3 = ((bf16[16,16,384]{2,1,0:T(8,128)(2,1)}), bf16[16,16,384]{2,1,0:T(8,128)(2,1)S(1)}, u32[]{:S(2)}, u32[]{:S(2)}) async-start(bf16[16,16,384]{2,1,0:T(8,128)(2,1)} %pad_maximum_fusion.2), calls=%async_computation.3 | async-start | bytes 393216 | tf_op jit(solution)/shard_map/panels/all_to_all | solution.py:20
  83.7 0.8 dynamic_slice.6
  84.5 0.8 dynamic-slice_bitcast_fusion.col_ref
  85.4 12.9 %all-to-all-done.3 = bf16[16,16,384]{2,1,0:T(8,128)(2,1)S(1)} async-done(((bf16[16,16,384]{2,1,0:T(8,128)(2,1)}), bf16[16,16,384]{2,1,0:T(8,128)(2,1)S(1)}, u32[]{:S(2)}, u32[]{:S(2)}) %all-to-all-start.3) | async-done | bytes 196640 | tf_op jit(solution)/shard_map/panels/all_to_all | solution.py:20
  98.3 11.6 %all_gather.14 = bf16[4,256,384]{2,1,0:T(8,128)(2,1)S(1)} all-gather(bf16[1,256,384]{2,1,0:T(8,128)(2,1)S(1)} %bitcast.73), channel_id=1, replica_groups=mesh['x'=4,'z'=16,'c'=2,'y'=4] {'x'}, dimensions={0}, use_global_device_ids=true | all-gather | bytes 983040 | tf_op jit(solution)/shard_map/panels/all_gather | solution.py:237
  110.0 27.0 %all-gather.2.cloned.1.call-done.row_ref.refs_0_.refs_1_.refs_2_ = bf16[1024,1536]{1,0:T(8,128)(2,1)} async-done(((bf16[64,1536]{1,0:T(8,128)(2,1)}), bf16[1024,1536]{1,0:T(8,128)(2,1)}) %all-gather.2.cloned.1.call-update) | async-done | bytes 3145744 | tf_op jit(solution)/shard_map/panels/all_gather | solution.py:230
  137.0 1.9 copy-done
  138.9 1.7 gram_half.3
  140.6 10.6 %collective-permute-start.1 = (bf16[4,3,64,384]{3,2,1,0:T(8,128)(2,1)S(1)}, bf16[4,3,64,384]{3,2,1,0:T(8,128)(2,1)S(1)}, u32[]{:S(2)}, u32[]{:S(2)}) collective-permute-start(bf16[4,3,64,384]{3,2,1,0:T(8,128)(2,1)S(1)} %gram_half.3), channel_id=1, source_target_pairs={{0,4},{4,0},{1,5},{5,1},{2,6},{6,2},{3,7},{7,3},{8,12},{12,8},{9,1... | collective-permute-start | bytes 1769480 | tf_op jit(solution)/shard_map/gram/ppermute | solution.py:14
  151.2 1.8 gram_half.2
  153.1 13.2 %all_to_all.59.parts_ref = bf16[4,192,384]{2,1,0:T(8,128)(2,1)S(1)} all-to-all(bf16[4,192,384]{2,1,0:T(8,128)(2,1)S(1)} %bitcast.67), channel_id=1, replica_groups=mesh['x'=4,'z'=16,'c'=2,'y'=4] {'y'}, dimensions={0} | all-to-all | bytes 1179648 | tf_op jit(solution)/shard_map/gram/all_to_all | solution.py:20
  167.0 11.0 %all_gather.15 = bf16[4,192,384]{2,1,0:T(8,128)(2,1)S(1)} all-gather(bf16[1,192,384]{2,1,0:T(8,128)(2,1)S(1)} %bitcast.64), channel_id=1, replica_groups=mesh['x'=4,'z'=16,'c'=2,'y'=4] {'y'}, dimensions={0}, use_global_device_ids=true | all-gather | bytes 737280 | tf_op jit(solution)/shard_map/amplitudes/all_gather | solution.py:260
  178.0 6.1 %collective-permute-start.2 = (bf16[4,3,64,384]{3,2,1,0:T(8,128)(2,1)S(1)}, bf16[4,3,64,384]{3,2,1,0:T(8,128)(2,1)S(1)}, u32[]{:S(2)}, u32[]{:S(2)}) collective-permute-start(bf16[4,3,64,384]{3,2,1,0:T(8,128)(2,1)S(1)} %bitcast.62), channel_id=1, source_target_pairs={{0,4},{4,0},{1,5},{5,1},{2,6},{6,2},{3,7},{7,3},{8,12},{12,8},{9,1... | collective-permute-start | bytes 1769480 | tf_op jit(solution)/shard_map/amplitudes/ppermute | solution.py:14
  184.1 1.7 contract.2.refs_4_
  185.9 2.7 %contract.3 = bf16[4,16,16,384]{3,2,1,0:T(8,128)(2,1)} custom-call(s32[1]{0:T(128)} %bitcast.which_ref.side_ref, bf16[1024,1536]{1,0:T(8,128)(2,1)S(1)} %copy-done.1, bf16[1024,1536]{1,0:T(8,128)(2,1)S(1)} %copy-done.1, bf16[1024,1536]{1,0:T(8,128)(2,1)S(1)} %copy-done.1, bf16[4,3,64,384]{3,2,1,0:T(8,128)(2,1)S(1)} %collective-permute-done.2.refs_3_, ...), custom_call_target="tpu_custom_call" | custom-call | flops 603979776 | bytes 3735552 | tf_op jit(solution)/shard_map/gamma/contract/pallas_call | solution.py:123
  188.5 3.9 %all-to-all-start.5 = ((bf16[4,256,384]{2,1,0:T(8,128)(2,1)}), bf16[4,256,384]{2,1,0:T(8,128)(2,1)S(1)}, u32[]{:S(2)}, u32[]{:S(2)}) async-start(bf16[4,256,384]{2,1,0:T(8,128)(2,1)} %bitcast.65), calls=%async_computation.5 | async-start | bytes 1572864 | tf_op jit(solution)/shard_map/gamma/all_to_all | solution.py:20
  192.4 5.6 %collective-permute-start.3 = (bf16[3,3,64,128]{3,2,1,0:T(8,128)(2,1)S(1)}, bf16[3,3,64,128]{3,2,1,0:T(8,128)(2,1)S(1)}, u32[]{:S(2)}, u32[]{:S(2)}) collective-permute-start(bf16[3,3,64,128]{3,2,1,0:T(8,128)(2,1)S(1)} %get-tuple-element.19), channel_id=1, source_target_pairs={{0,32},{4,96},{8,40},{12,104},{16,48},{20,112},{24,56},{28,120},{3... | collective-permute-start | bytes 442376 | tf_op jit(solution)/shard_map/amplitudes/ppermute | solution.py:259
  198.0 6.3 %all-to-all-done.5 = bf16[4,256,384]{2,1,0:T(8,128)(2,1)S(1)} async-done(((bf16[4,256,384]{2,1,0:T(8,128)(2,1)}), bf16[4,256,384]{2,1,0:T(8,128)(2,1)S(1)}, u32[]{:S(2)}, u32[]{:S(2)}) %all-to-all-start.5) | async-done | bytes 786464 | tf_op jit(solution)/shard_map/gamma/all_to_all | solution.py:20
  204.3 0.8 reduce_sum.35
  205.1 9.0 %all-to-all-start.6 = ((bf16[16,16,384]{2,1,0:T(8,128)(2,1)}), bf16[16,16,384]{2,1,0:T(8,128)(2,1)S(1)}, u32[]{:S(2)}, u32[]{:S(2)}) async-start(bf16[16,16,384]{2,1,0:T(8,128)(2,1)} %bitcast.37), calls=%async_computation.6 | async-start | bytes 393216 | tf_op jit(solution)/shard_map/gamma/all_to_all | solution.py:20
  214.2 0.7 convert_bitcast_fusion
  214.9 11.8 %all-to-all-done.6.value_ref = bf16[16,16,384]{2,1,0:T(8,128)(2,1)S(1)} async-done(((bf16[16,16,384]{2,1,0:T(8,128)(2,1)}), bf16[16,16,384]{2,1,0:T(8,128)(2,1)S(1)}, u32[]{:S(2)}, u32[]{:S(2)}) %all-to-all-start.6) | async-done | bytes 196640 | tf_op jit(solution)/shard_map/gamma/all_to_all | solution.py:20
  (43 shorter events, 5.0 us)
Async XLA Ops:
  7.2 0.7 copy-start.2
  7.9 17.5 %copy-start.3 = (bf16[64,3,640]{2,0,1:T(8,128)(2,1)S(1)}, bf16[64,3,640]{2,0,1:T(8,128)(2,1)}, u32[]{:S(2)}) copy-start(bf16[64,3,640]{2,0,1:T(8,128)(2,1)} %param.6) | copy-start | bytes 737284
  8.8 31.0 %all-to-all-start = ((bf16[16,16,640]{2,1,0:T(8,128)(2,1)}), bf16[16,16,640]{2,1,0:T(8,128)(2,1)S(1)}, u32[]{:S(2)}, u32[]{:S(2)}) async-start(bf16[16,16,640]{2,1,0:T(8,128)(2,1)} %spread.1), calls=%async_computation | async-start | bytes 655360 | tf_op jit(solution)/shard_map/transform/all_to_all | solution.py:20
  24.5 112.4 %all-gather.2.cloned.1.call-start = ((), (), s32[]{:S(2)}) async-start(), calls=%async_computation.7 | async-start | bytes 3342336 | tf_op jit(solution)/shard_map/panels/all_gather | solution.py:230
  39.8 9.6 %collective-permute-start = (bf16[16,16,640]{2,1,0:T(8,128)(2,1)S(1)}, bf16[16,16,640]{2,1,0:T(8,128)(2,1)S(1)}, u32[]{:S(2)}, u32[]{:S(2)}) collective-permute-start(bf16[16,16,640]{2,1,0:T(8,128)(2,1)S(1)} %all-to-all-done), channel_id=1, source_target_pairs={{0,4},{4,0},{1,5},{5,1},{2,6},{6,2},{3,7},{7,3},{8,12},{12,8},{9,1... | collective-permute-start | bytes 983048 | tf_op jit(solution)/shard_map/transform/ppermute | solution.py:14
  75.8 9.4 %copy-start.4 = (f32[512]{0:T(512)S(1)}, f32[512]{0:T(512)}, u32[]{:S(2)}) copy-start(f32[512]{0:T(512)} %param.9) | copy-start | bytes 6148
  75.8 9.4 %copy-start.5 = (s32[3]{0:T(128)S(1)}, s32[3]{0:T(128)}, u32[]{:S(2)}) copy-start(s32[3]{0:T(128)} %param.11) | copy-start | bytes 40
  77.0 21.3 %all-to-all-start.3 = ((bf16[16,16,384]{2,1,0:T(8,128)(2,1)}), bf16[16,16,384]{2,1,0:T(8,128)(2,1)S(1)}, u32[]{:S(2)}, u32[]{:S(2)}) async-start(bf16[16,16,384]{2,1,0:T(8,128)(2,1)} %pad_maximum_fusion.2), calls=%async_computation.3 | async-start | bytes 393216 | tf_op jit(solution)/shard_map/panels/all_to_all | solution.py:20
  137.0 1.9 copy-start
  138.9 12.3 %copy-start.1 = (bf16[1024,1536]{1,0:T(8,128)(2,1)S(1)}, bf16[1024,1536]{1,0:T(8,128)(2,1)}, u32[]{:S(2)}) copy-start(bf16[1024,1536]{1,0:T(8,128)(2,1)} %all-gather.2.cloned.1.call-done.row_ref.refs_0_.refs_1_.refs_2_) | copy-start | bytes 9437188
  140.6 12.4 %collective-permute-start.1 = (bf16[4,3,64,384]{3,2,1,0:T(8,128)(2,1)S(1)}, bf16[4,3,64,384]{3,2,1,0:T(8,128)(2,1)S(1)}, u32[]{:S(2)}, u32[]{:S(2)}) collective-permute-start(bf16[4,3,64,384]{3,2,1,0:T(8,128)(2,1)S(1)} %gram_half.3), channel_id=1, source_target_pairs={{0,4},{4,0},{1,5},{5,1},{2,6},{6,2},{3,7},{7,3},{8,12},{12,8},{9,1... | collective-permute-start | bytes 1769480 | tf_op jit(solution)/shard_map/gram/ppermute | solution.py:14
  178.0 7.9 %collective-permute-start.2 = (bf16[4,3,64,384]{3,2,1,0:T(8,128)(2,1)S(1)}, bf16[4,3,64,384]{3,2,1,0:T(8,128)(2,1)S(1)}, u32[]{:S(2)}, u32[]{:S(2)}) collective-permute-start(bf16[4,3,64,384]{3,2,1,0:T(8,128)(2,1)S(1)} %bitcast.62), channel_id=1, source_target_pairs={{0,4},{4,0},{1,5},{5,1},{2,6},{6,2},{3,7},{7,3},{8,12},{12,8},{9,1... | collective-permute-start | bytes 1769480 | tf_op jit(solution)/shard_map/amplitudes/ppermute | solution.py:14
  188.5 15.8 %all-to-all-start.5 = ((bf16[4,256,384]{2,1,0:T(8,128)(2,1)}), bf16[4,256,384]{2,1,0:T(8,128)(2,1)S(1)}, u32[]{:S(2)}, u32[]{:S(2)}) async-start(bf16[4,256,384]{2,1,0:T(8,128)(2,1)} %bitcast.65), calls=%async_computation.5 | async-start | bytes 1572864 | tf_op jit(solution)/shard_map/gamma/all_to_all | solution.py:20
  192.4 12.7 %collective-permute-start.3 = (bf16[3,3,64,128]{3,2,1,0:T(8,128)(2,1)S(1)}, bf16[3,3,64,128]{3,2,1,0:T(8,128)(2,1)S(1)}, u32[]{:S(2)}, u32[]{:S(2)}) collective-permute-start(bf16[3,3,64,128]{3,2,1,0:T(8,128)(2,1)S(1)} %get-tuple-element.19), channel_id=1, source_target_pairs={{0,32},{4,96},{8,40},{12,104},{16,48},{20,112},{24,56},{28,120},{3... | collective-permute-start | bytes 442376 | tf_op jit(solution)/shard_map/amplitudes/ppermute | solution.py:259
  205.1 21.6 %all-to-all-start.6 = ((bf16[16,16,384]{2,1,0:T(8,128)(2,1)}), bf16[16,16,384]{2,1,0:T(8,128)(2,1)S(1)}, u32[]{:S(2)}, u32[]{:S(2)}) async-start(bf16[16,16,384]{2,1,0:T(8,128)(2,1)} %bitcast.37), calls=%async_computation.6 | async-start | bytes 393216 | tf_op jit(solution)/shard_map/gamma/all_to_all | solution.py:20
Sparse Core Ops, SparseCore 0:
  66.9 70.0 all-gather.1

commit v12 on v11

--- a/solution.py
+++ b/solution.py
@@ -118,7 +118,7 @@
         out_shape, out_specs, extra = jax.ShapeDtypeStruct((k_rows, width), F32), flat, ()
     else:
         in_specs.append(flat)
-        out_shape = pltpu.HBM((nx, nz, r, width), BF)
+        out_shape = jax.ShapeDtypeStruct((nx, nz, r, width), BF)
         out_specs, extra = pl.BlockSpec((nx, zs, r, width), lambda s, w: (0, s, 0, 0)), (base,)
     return pl.pallas_call(
         body,
@@ -265,7 +265,6 @@
         value = contract(row, theirs, 1 - c, nx, nz, contract(row, mixed, c, nx, nz))
         value = exchange(value.reshape(nx, nz * r, nocc * narrow), "x")
         value = jnp.sum(value.astype(F32), axis=0).astype(BF)
-        value, own = lax.optimization_barrier((value, own))
         value = exchange(value.reshape(nz, r, nocc * narrow), "z")
         gamma = place(value, nocc)
     return own.astype(F32).transpose(0, 2, 1, 3)[None], gamma.transpose(1, 0, 2)

time: 239 us -> 241 us (level); the launches traced: 234 us -> 240 us
  blocking collectives: 73.4 us -> 89.7 us
  waiting for transfers between devices: 60.2 us -> 53.7 us
  starting transfers between devices: 66.2 us -> 62.9 us
    all_to_all x4 -> x3, waiting for transfers between devices: 32 us -> 13.9 us  [exchange(): value = lax.all_to_all(value, axis, split_axis=0, concat_axis=0, tiled=True)]
    all_to_all x3 -> x4, blocking collectives: 37.6 us -> 53.8 us  [exchange(): value = lax.all_to_all(value, axis, split_axis=0, concat_axis=0, tiled=True)]
    ppermute x1, waiting for transfers between devices: 0.01 us -> 11.5 us  [local(): own = lax.ppermute(amps, ('z', 'c'), swap)]
    all_to_all x4 -> x3, starting transfers between devices: 35.4 us -> 28.8 us  [exchange(): value = lax.all_to_all(value, axis, split_axis=0, concat_axis=0, tiled=True)]
    ppermute x1, starting transfers between devices: 5.58 us -> 8.98 us  [local(): own = lax.ppermute(amps, ('z', 'c'), swap)]
  transfers between devices with their start and end apart: 9 -> 8, of which waited for: 6 -> 5; matrix products, arithmetic and copies ran while one was open for 2% -> 2% of each run, Pallas kernels for 1% -> 1%
where the time goes in v12:
time: 241 us; the launch traced here: 240 us
  blocking collectives  89.7 us (37%)
  starting transfers between devices  62.9 us (26%)
  waiting for transfers between devices  53.7 us (22%)
  between operations  14.4 us (6%)
  Pallas kernels  9.21 us (4%)
  local copies, waits for them, and re-layouts  4.96 us (2%)
  other arithmetic  4.27 us (2%)
    all_to_all x4, blocking collectives, exchange(): value = lax.all_to_all(value, axis, split_axis=0, concat_axis=0, tiled=True)  53.8 us
    all_to_all x3, starting transfers between devices, exchange(): value = lax.all_to_all(value, axis, split_axis=0, concat_axis=0, tiled=True)  28.8 us
    all_gather x1, waiting for transfers between devices, local(): lax.all_gather(row.reshape(nx * r, nocc * wide), 'z', axis=0, tiled=True)  27.1 us
    ppermute x3, starting transfers between devices, swap_cores(): return lax.ppermute(value, 'c', [(0, 1), (1, 0)])  25.1 us
    all_to_all x3, waiting for transfers between devices, exchange(): value = lax.all_to_all(value, axis, split_axis=0, concat_axis=0, tiled=True)  13.9 us
    all_gather x1, blocking collectives, local(): masked = lax.all_gather(masked.reshape(-1, ao_part), 'x', axis=0)  13.2 us
    all_gather x1, blocking collectives, local(): col = lax.all_gather(col.reshape(nz * r, nocc * narrow), 'x', axis=0)  11.6 us
    ppermute x1, waiting for transfers between devices, local(): own = lax.ppermute(amps, ('z', 'c'), swap)  11.5 us
  transfers between devices with their start and end apart: 8, of which 5 were waited for; matrix products, arithmetic and copies ran while one was open for 2% of the time, Pallas kernels for 1%

profile of v12, /device:TPU:1, one launch (start us, length us, event | category | flops | bytes accessed | tf_op | source)
XLA Modules:
  0.0 239.9 jit_solution(3264384469976170750)
XLA Ops:
  7.2 0.7 copy-done.2
  7.9 0.9 spread.1
  8.8 15.8 %all-to-all-start = ((bf16[16,16,640]{2,1,0:T(8,128)(2,1)}), bf16[16,16,640]{2,1,0:T(8,128)(2,1)S(1)}, u32[]{:S(2)}, u32[]{:S(2)}) async-start(bf16[16,16,640]{2,1,0:T(8,128)(2,1)} %spread.1), calls=%async_computation | async-start | bytes 655360 | tf_op jit(solution)/shard_map/transform/all_to_all | solution.py:20
  25.5 13.2 %all_gather.12 = bf16[4,192,640]{2,1,0:T(8,128)(2,1)S(1)} all-gather(bf16[1,192,640]{2,1,0:T(8,128)(2,1)S(1)} %bitcast.70), channel_id=1, replica_groups=mesh['x'=4,'z'=16,'c'=2,'y'=4] {'x'}, dimensions={0}, use_global_device_ids=true | all-gather | bytes 1228800 | tf_op jit(solution)/shard_map/transform/all_gather | solution.py:219
  38.7 1.0 all-to-all-done
  39.8 8.4 %collective-permute-start = (bf16[16,16,640]{2,1,0:T(8,128)(2,1)S(1)}, bf16[16,16,640]{2,1,0:T(8,128)(2,1)S(1)}, u32[]{:S(2)}, u32[]{:S(2)}) collective-permute-start(bf16[16,16,640]{2,1,0:T(8,128)(2,1)S(1)} %all-to-all-done), channel_id=1, source_target_pairs={{0,4},{4,0},{1,5},{5,1},{2,6},{6,2},{3,7},{7,3},{8,12},{12,8},{9,1... | collective-permute-start | bytes 983048 | tf_op jit(solution)/shard_map/transform/ppermute | solution.py:14
  48.2 1.2 collective-permute-done
  49.6 0.8 fusion
  50.5 15.4 %all_to_all.57 = bf16[4,192,512]{2,1,0:T(8,128)(2,1)S(1)} all-to-all(bf16[4,192,512]{2,1,0:T(8,128)(2,1)S(1)} %bitcast.66), channel_id=1, replica_groups=mesh['x'=4,'z'=16,'c'=2,'y'=4] {'y'}, dimensions={0} | all-to-all | bytes 1572864 | tf_op jit(solution)/shard_map/transform/all_to_all | solution.py:20
  66.8 9.0 %all_to_all.58 = bf16[4,48,512]{2,1,0:T(8,128)(2,1)S(1)} all-to-all(bf16[4,48,512]{2,1,0:T(8,128)(2,1)S(1)} %bitcast.69), channel_id=1, replica_groups=mesh['x'=4,'z'=16,'c'=2,'y'=4] {'x'}, dimensions={0} | all-to-all | bytes 393216 | tf_op jit(solution)/shard_map/panels/all_to_all | solution.py:20
  77.0 6.7 %all-to-all-start.3 = ((bf16[16,16,384]{2,1,0:T(8,128)(2,1)}), bf16[16,16,384]{2,1,0:T(8,128)(2,1)S(1)}, u32[]{:S(2)}, u32[]{:S(2)}) async-start(bf16[16,16,384]{2,1,0:T(8,128)(2,1)} %pad_maximum_fusion.1), calls=%async_computation.3 | async-start | bytes 393216 | tf_op jit(solution)/shard_map/panels/all_to_all | solution.py:20
  83.7 0.8 dynamic_slice.6
  84.5 0.8 dynamic-slice_bitcast_fusion.col_ref
  85.4 12.9 %all-to-all-done.3 = bf16[16,16,384]{2,1,0:T(8,128)(2,1)S(1)} async-done(((bf16[16,16,384]{2,1,0:T(8,128)(2,1)}), bf16[16,16,384]{2,1,0:T(8,128)(2,1)S(1)}, u32[]{:S(2)}, u32[]{:S(2)}) %all-to-all-start.3) | async-done | bytes 196640 | tf_op jit(solution)/shard_map/panels/all_to_all | solution.py:20
  98.3 11.6 %all_gather.13 = bf16[4,256,384]{2,1,0:T(8,128)(2,1)S(1)} all-gather(bf16[1,256,384]{2,1,0:T(8,128)(2,1)S(1)} %bitcast.73), channel_id=1, replica_groups=mesh['x'=4,'z'=16,'c'=2,'y'=4] {'x'}, dimensions={0}, use_global_device_ids=true | all-gather | bytes 983040 | tf_op jit(solution)/shard_map/panels/all_gather | solution.py:237
  109.9 27.1 %all-gather.2.cloned.1.call-done.row_ref.refs_0_.refs_1_.refs_2_ = bf16[1024,1536]{1,0:T(8,128)(2,1)} async-done(((bf16[64,1536]{1,0:T(8,128)(2,1)}), bf16[1024,1536]{1,0:T(8,128)(2,1)}) %all-gather.2.cloned.1.call-update) | async-done | bytes 3145744 | tf_op jit(solution)/shard_map/panels/all_gather | solution.py:230
  137.0 1.9 copy-done
  138.9 1.7 gram_half.3
  140.6 10.6 %collective-permute-start.1 = (bf16[4,3,64,384]{3,2,1,0:T(8,128)(2,1)S(1)}, bf16[4,3,64,384]{3,2,1,0:T(8,128)(2,1)S(1)}, u32[]{:S(2)}, u32[]{:S(2)}) collective-permute-start(bf16[4,3,64,384]{3,2,1,0:T(8,128)(2,1)S(1)} %gram_half.3), channel_id=1, source_target_pairs={{0,4},{4,0},{1,5},{5,1},{2,6},{6,2},{3,7},{7,3},{8,12},{12,8},{9,1... | collective-permute-start | bytes 1769480 | tf_op jit(solution)/shard_map/gram/ppermute | solution.py:14
  151.2 1.8 gram_half.2
  153.1 13.1 %all_to_all.59.parts_ref = bf16[4,192,384]{2,1,0:T(8,128)(2,1)S(1)} all-to-all(bf16[4,192,384]{2,1,0:T(8,128)(2,1)S(1)} %bitcast.67), channel_id=1, replica_groups=mesh['x'=4,'z'=16,'c'=2,'y'=4] {'y'}, dimensions={0} | all-to-all | bytes 1179648 | tf_op jit(solution)/shard_map/gram/all_to_all | solution.py:20
  166.9 11.0 %all_gather.15 = bf16[4,192,384]{2,1,0:T(8,128)(2,1)S(1)} all-gather(bf16[1,192,384]{2,1,0:T(8,128)(2,1)S(1)} %bitcast.65), channel_id=1, replica_groups=mesh['x'=4,'z'=16,'c'=2,'y'=4] {'y'}, dimensions={0}, use_global_device_ids=true | all-gather | bytes 737280 | tf_op jit(solution)/shard_map/amplitudes/all_gather | solution.py:260
  178.0 6.1 %collective-permute-start.3 = (bf16[4,3,64,384]{3,2,1,0:T(8,128)(2,1)S(1)}, bf16[4,3,64,384]{3,2,1,0:T(8,128)(2,1)S(1)}, u32[]{:S(2)}, u32[]{:S(2)}) collective-permute-start(bf16[4,3,64,384]{3,2,1,0:T(8,128)(2,1)S(1)} %bitcast.63), channel_id=1, source_target_pairs={{0,4},{4,0},{1,5},{5,1},{2,6},{6,2},{3,7},{7,3},{8,12},{12,8},{9,1... | collective-permute-start | bytes 1769480 | tf_op jit(solution)/shard_map/amplitudes/ppermute | solution.py:14
  184.1 1.7 contract.2.refs_4_
  185.9 1.8 contract.3
  187.6 16.3 %all_to_all.60 = bf16[4,256,384]{2,1,0:T(8,128)(2,1)S(1)} all-to-all(bf16[4,256,384]{2,1,0:T(8,128)(2,1)S(1)} %bitcast.62), channel_id=1, replica_groups=mesh['x'=4,'z'=16,'c'=2,'y'=4] {'x'}, dimensions={0} | all-to-all | bytes 1572864 | tf_op jit(solution)/shard_map/gamma/all_to_all | solution.py:20
  203.9 0.8 reduce_sum.35
  204.7 6.3 %all-to-all-start.6 = ((bf16[16,16,384]{2,1,0:T(8,128)(2,1)}), bf16[16,16,384]{2,1,0:T(8,128)(2,1)S(1)}, u32[]{:S(2)}, u32[]{:S(2)}) async-start(bf16[16,16,384]{2,1,0:T(8,128)(2,1)} %bitcast.37), calls=%async_computation.6 | async-start | bytes 393216 | tf_op jit(solution)/shard_map/gamma/all_to_all | solution.py:20
  211.1 9.0 %collective-permute-start.2 = (bf16[3,3,64,128]{3,2,1,0:T(8,128)(2,1)S(1)}, bf16[3,3,64,128]{3,2,1,0:T(8,128)(2,1)S(1)}, u32[]{:S(2)}, u32[]{:S(2)}) collective-permute-start(bf16[3,3,64,128]{3,2,1,0:T(8,128)(2,1)S(1)} %get-tuple-element.16), channel_id=1, source_target_pairs={{0,32},{4,96},{8,40},{12,104},{16,48},{20,112},{24,56},{28,120},{3... | collective-permute-start | bytes 442376 | tf_op jit(solution)/shard_map/amplitudes/ppermute | solution.py:259
  220.1 11.5 %collective-permute-done.2 = bf16[3,3,64,128]{3,2,1,0:T(8,128)(2,1)S(1)} collective-permute-done((bf16[3,3,64,128]{3,2,1,0:T(8,128)(2,1)S(1)}, bf16[3,3,64,128]{3,2,1,0:T(8,128)(2,1)S(1)}, u32[]{:S(2)}, u32[]{:S(2)}) %collective-permute-start.2) | collective-permute-done | bytes 147488 | tf_op jit(solution)/shard_map/amplitudes/ppermute | solution.py:259
  231.6 0.7 convert_bitcast_fusion
  232.4 0.7 place.1
  (42 shorter events, 4.3 us)
Async XLA Ops:
  7.2 0.7 copy-start.2
  7.9 17.5 %copy-start.3 = (bf16[64,3,640]{2,0,1:T(8,128)(2,1)S(1)}, bf16[64,3,640]{2,0,1:T(8,128)(2,1)}, u32[]{:S(2)}) copy-start(bf16[64,3,640]{2,0,1:T(8,128)(2,1)} %param.6) | copy-start | bytes 737284
  8.8 31.0 %all-to-all-start = ((bf16[16,16,640]{2,1,0:T(8,128)(2,1)}), bf16[16,16,640]{2,1,0:T(8,128)(2,1)S(1)}, u32[]{:S(2)}, u32[]{:S(2)}) async-start(bf16[16,16,640]{2,1,0:T(8,128)(2,1)} %spread.1), calls=%async_computation | async-start | bytes 655360 | tf_op jit(solution)/shard_map/transform/all_to_all | solution.py:20
  24.5 112.5 %all-gather.2.cloned.1.call-start = ((), (), s32[]{:S(2)}) async-start(), calls=%async_computation.7 | async-start | bytes 3342336 | tf_op jit(solution)/shard_map/panels/all_gather | solution.py:230
  39.8 9.6 %collective-permute-start = (bf16[16,16,640]{2,1,0:T(8,128)(2,1)S(1)}, bf16[16,16,640]{2,1,0:T(8,128)(2,1)S(1)}, u32[]{:S(2)}, u32[]{:S(2)}) collective-permute-start(bf16[16,16,640]{2,1,0:T(8,128)(2,1)S(1)} %all-to-all-done), channel_id=1, source_target_pairs={{0,4},{4,0},{1,5},{5,1},{2,6},{6,2},{3,7},{7,3},{8,12},{12,8},{9,1... | collective-permute-start | bytes 983048 | tf_op jit(solution)/shard_map/transform/ppermute | solution.py:14
  75.8 9.4 %copy-start.4 = (f32[512]{0:T(512)S(1)}, f32[512]{0:T(512)}, u32[]{:S(2)}) copy-start(f32[512]{0:T(512)} %param.9) | copy-start | bytes 6148
  75.8 9.4 %copy-start.5 = (s32[3]{0:T(128)S(1)}, s32[3]{0:T(128)}, u32[]{:S(2)}) copy-start(s32[3]{0:T(128)} %param.11) | copy-start | bytes 40
  77.0 21.3 %all-to-all-start.3 = ((bf16[16,16,384]{2,1,0:T(8,128)(2,1)}), bf16[16,16,384]{2,1,0:T(8,128)(2,1)S(1)}, u32[]{:S(2)}, u32[]{:S(2)}) async-start(bf16[16,16,384]{2,1,0:T(8,128)(2,1)} %pad_maximum_fusion.1), calls=%async_computation.3 | async-start | bytes 393216 | tf_op jit(solution)/shard_map/panels/all_to_all | solution.py:20
  137.0 1.9 copy-start
  138.9 12.3 %copy-start.1 = (bf16[1024,1536]{1,0:T(8,128)(2,1)S(1)}, bf16[1024,1536]{1,0:T(8,128)(2,1)}, u32[]{:S(2)}) copy-start(bf16[1024,1536]{1,0:T(8,128)(2,1)} %all-gather.2.cloned.1.call-done.row_ref.refs_0_.refs_1_.refs_2_) | copy-start | bytes 9437188
  140.6 12.4 %collective-permute-start.1 = (bf16[4,3,64,384]{3,2,1,0:T(8,128)(2,1)S(1)}, bf16[4,3,64,384]{3,2,1,0:T(8,128)(2,1)S(1)}, u32[]{:S(2)}, u32[]{:S(2)}) collective-permute-start(bf16[4,3,64,384]{3,2,1,0:T(8,128)(2,1)S(1)} %gram_half.3), channel_id=1, source_target_pairs={{0,4},{4,0},{1,5},{5,1},{2,6},{6,2},{3,7},{7,3},{8,12},{12,8},{9,1... | collective-permute-start | bytes 1769480 | tf_op jit(solution)/shard_map/gram/ppermute | solution.py:14
  178.0 7.9 %collective-permute-start.3 = (bf16[4,3,64,384]{3,2,1,0:T(8,128)(2,1)S(1)}, bf16[4,3,64,384]{3,2,1,0:T(8,128)(2,1)S(1)}, u32[]{:S(2)}, u32[]{:S(2)}) collective-permute-start(bf16[4,3,64,384]{3,2,1,0:T(8,128)(2,1)S(1)} %bitcast.63), channel_id=1, source_target_pairs={{0,4},{4,0},{1,5},{5,1},{2,6},{6,2},{3,7},{7,3},{8,12},{12,8},{9,1... | collective-permute-start | bytes 1769480 | tf_op jit(solution)/shard_map/amplitudes/ppermute | solution.py:14
  204.7 27.6 %all-to-all-start.6 = ((bf16[16,16,384]{2,1,0:T(8,128)(2,1)}), bf16[16,16,384]{2,1,0:T(8,128)(2,1)S(1)}, u32[]{:S(2)}, u32[]{:S(2)}) async-start(bf16[16,16,384]{2,1,0:T(8,128)(2,1)} %bitcast.37), calls=%async_computation.6 | async-start | bytes 393216 | tf_op jit(solution)/shard_map/gamma/all_to_all | solution.py:20
  211.1 20.5 %collective-permute-start.2 = (bf16[3,3,64,128]{3,2,1,0:T(8,128)(2,1)S(1)}, bf16[3,3,64,128]{3,2,1,0:T(8,128)(2,1)S(1)}, u32[]{:S(2)}, u32[]{:S(2)}) collective-permute-start(bf16[3,3,64,128]{3,2,1,0:T(8,128)(2,1)S(1)} %get-tuple-element.16), channel_id=1, source_target_pairs={{0,32},{4,96},{8,40},{12,104},{16,48},{20,112},{24,56},{28,120},{3... | collective-permute-start | bytes 442376 | tf_op jit(solution)/shard_map/amplitudes/ppermute | solution.py:259
Sparse Core Ops, SparseCore 0:
  66.9 70.0 all-gather.1
